TPU v7x, 32 devices: a whole 2x2x4 slice. The times are simulated.
32 devices in a mesh: seq: 16 (over z, y, x), head: 2 (over core).
Axes of the slice: x: 2, y: 2, z: 4, core: 2. Of those that a mesh axis runs over, the one named last changes fastest.
Arguments:
- tokens: bfloat16 [2048, 1024], P('seq'), may hold values from -17 to 17
- w_query: bfloat16 [1024, 1024], P(None, 'head'), may hold values from -0.1875 to 0.1875
- w_key: bfloat16 [1024, 1024], P(None, 'head'), may hold values from -0.1875 to 0.1875
- w_value: bfloat16 [1024, 1024], P(None, 'head'), may hold values from -0.1875 to 0.1875
- w_out: bfloat16 [1024, 1024], P('head'), may hold values from -1.796875 to 1.796875
- cluster_ids: int32 [4, 2048], P('head', 'seq'), may hold values from 0 to 15, as said below
- positions: int32 [2048], P('seq'), may hold values from 0 to 2047, each once
Outputs:
- mixed: bfloat16 [2048, 1024], P(('seq', 'head'))
Inputs may be any that keep to these rules, and one draw needn't show every extreme that they name: `cluster_ids`: in each head group every cluster holds at most 320 tokens, and at most 20 of the 128 tokens of one index of seq; both bounds are reached.
All inputs are finite; a program needn't handle non-finite values.
Results may differ from a plain program's by a relative error of at most 0.0029.
The roundings to bfloat16 on the way count: a program that leaves them out, or rounds other values in their place, can miss the bound.
Values may be sent and summed in bfloat16 or wider, within the bound.
No kernel may reach another device: no remote copies, remote signals or barrier semaphores. Data moves between devices by JAX's collectives and lax.ppermute only.
A program may use at most 64 MiB of HBM per device.

v0:
```python
import jax
import jax.numpy as jnp
from jax import lax
from jax.sharding import PartitionSpec as P

HD = 64
GROUP_HEADS = 4


def attend_rows(query, keys, values, query_pos, key_pos):
    scores = jnp.einsum("qhd,khd->hqk", query, keys, preferred_element_type=jnp.float32) * HD ** (
        -0.5
    )
    allowed = (key_pos[None, None, :] >= 0) & (key_pos[None, None, :] <= query_pos[None, :, None])
    masked = jnp.where(allowed, scores, jnp.float32(-1e30))
    top = jnp.max(masked, axis=-1, keepdims=True)
    expo = jnp.exp(masked - top)
    weights = (expo / jnp.sum(expo, axis=-1, keepdims=True)).astype(jnp.bfloat16)
    return jnp.einsum("hqk,khd->qhd", weights, values, preferred_element_type=jnp.float32).astype(
        jnp.bfloat16
    )


def attend_group(data, pos):
    rows = data.shape[0]
    width = data.shape[1] // 3
    query = data[:, :width].reshape(rows, GROUP_HEADS, HD)
    keys = data[:, width : 2 * width].reshape(rows, GROUP_HEADS, HD)
    values = data[:, 2 * width :].reshape(rows, GROUP_HEADS, HD)
    half = rows // 2
    first = attend_rows(query[:half], keys, values, pos[:half], pos)
    second = attend_rows(query[half:], keys, values, pos[half:], pos)
    result = jnp.concatenate([first, second], axis=0)
    return result.reshape(rows, width)


def owner_side(pieces):
    data, pos = pieces
    outputs = [attend_group(data[:, item], pos[:, item]) for item in range(data.shape[1])]
    result = jnp.stack(outputs, axis=1)
    return lax.all_to_all(result, "seq", split_axis=0, concat_axis=0, tiled=True)


def per_device(tokens, w_query, w_key, w_value, w_out, cluster_ids, positions):
    tok = tokens.shape[0]
    groups_here = cluster_ids.shape[0]
    owners = lax.axis_size("seq")
    half = tok // 2
    fewer = owners // 4
    capacity = (half + owners - 1) // owners + (half + fewer - 1) // fewer
    slots = owners * capacity
    width = w_query.shape[1] // groups_here
    tok_ids = jnp.arange(tok, dtype=jnp.int32)
    earlier = tok_ids[None, :] < tok_ids[:, None]
    same = cluster_ids[:, :, None] == cluster_ids[:, None, :]
    rank = jnp.sum((same & earlier[None]).astype(jnp.int32), axis=2)
    dest = cluster_ids * capacity + rank
    slot_ids = jnp.arange(slots, dtype=jnp.int32)
    matches = slot_ids[None, :, None] == dest[:, None, :]
    onehot = matches.astype(jnp.bfloat16)
    filled = jnp.any(matches, axis=2)
    pos_sum = jnp.sum(jnp.where(matches, positions[None, None, :], 0), axis=2)
    pos_slots = jnp.where(filled, pos_sum, -1).T

    def project_group(index):
        lo = index * width
        parts = [
            jnp.dot(tokens, weight[:, lo : lo + width], preferred_element_type=jnp.float32).astype(
                jnp.bfloat16
            )
            for weight in (w_query, w_key, w_value)
        ]
        return jnp.concatenate(parts, axis=1)

    data = jnp.stack([project_group(index) for index in range(groups_here)], axis=1)
    send = jnp.einsum("gst,tgc->sgc", onehot, data, preferred_element_type=jnp.float32).astype(
        jnp.bfloat16
    )
    back = owner_side(
        (
            lax.all_to_all(send, "seq", split_axis=0, concat_axis=0, tiled=True),
            lax.all_to_all(pos_slots, "seq", split_axis=0, concat_axis=0, tiled=True),
        )
    )
    attended = jnp.einsum("gst,sgc->tgc", onehot, back, preferred_element_type=jnp.float32).astype(
        jnp.bfloat16
    )
    attended = attended.reshape(tok, groups_here * width)
    mixed = lax.psum_scatter(
        jnp.dot(attended, w_out, preferred_element_type=jnp.float32),
        "head",
        scatter_dimension=0,
        tiled=True,
    )
    return mixed.astype(jnp.bfloat16)


def solution(mesh):
    in_specs = (
        P("seq", None),
        P(None, "head"),
        P(None, "head"),
        P(None, "head"),
        P("head", None),
        P("head", "seq"),
        P("seq"),
    )
    out_specs = P(("seq", "head"), None)
    return jax.shard_map(
        per_device, mesh=mesh, in_specs=in_specs, out_specs=out_specs, check_vma=False
    )
```

profile of v0, /device:TPU:0, one launch (start us, length us, event | category | flops | bytes accessed | tf_op | source)
XLA Modules:
  0.0 112.5 jit_solution(17475957911828295855)
XLA Ops:
  6.5 0.0 copy-start
  6.6 1.0 convert_reduce_fusion
  7.6 0.7 multiply_add_fusion
  8.3 0.2 fusion.31
  8.5 0.8 select_reduce_fusion
  9.3 0.1 all_to_all.15
  9.4 0.6 copy.48
  10.0 8.3 %all-to-all-start.1 = ((s32[16,20,2]{1,2,0:T(2,128)}), s32[16,20,2]{1,2,0:T(2,128)S(1)}, u32[]{:S(2)}, u32[]{:S(2)}) async-start(s32[16,20,2]{1,2,0:T(2,128)} %copy.48), calls=%async_computation.1 | async-start | bytes 32768 | tf_op jit(solution)/shard_map/all_to_all | solution.py:82
  18.4 1.4 %convolution_convert_fusion.9 = bf16[128,256]{1,0:T(8,128)(2,1)S(1)} fusion(bf16[128,1024]{1,0:T(8,128)(2,1)} %param.7, bf16[1024,512]{1,0:T(8,128)(2,1)} %param.10), kind=kOutput, calls=%fused_computation.34 | convolution fusion | flops 67141632 | bytes 851968 | tf_op jit(solution)/shard_map/dot_general | solution.py:68
  19.7 0.0 copy-done.4
  19.7 0.0 copy-start.5
  19.7 1.3 %convolution_convert_fusion.6 = bf16[128,256]{1,0:T(8,128)(2,1)S(1)} fusion(bf16[128,1024]{1,0:T(8,128)(2,1)} %param.7, bf16[1024,512]{1,0:T(8,128)(2,1)S(1)} %copy-done.4), kind=kOutput, calls=%fused_computation.31 | convolution fusion | flops 67141632 | bytes 851968 | tf_op jit(solution)/shard_map/dot_general | solution.py:68
  21.0 0.0 copy-done.7
  21.0 0.0 copy-start.6
  21.0 1.4 %convolution_convert_fusion.10 = bf16[128,256]{1,0:T(8,128)(2,1)S(1)} fusion(bf16[128,1024]{1,0:T(8,128)(2,1)S(1)} %copy-done.7, bf16[1024,512]{1,0:T(8,128)(2,1)} %param.9), kind=kOutput, calls=%fused_computation.35 | convolution fusion | flops 67141632 | bytes 851968 | tf_op jit(solution)/shard_map/dot_general | solution.py:68
  22.4 0.0 copy-done.5
  22.4 0.2 convolution_convert_fusion.7
  22.7 0.0 copy-done.6
  22.7 0.2 convolution_convert_fusion.11
  22.9 0.2 convolution_convert_fusion.8
  23.2 0.4 fusion.8
  23.6 2.0 %copy.46 = bf16[320,2,768]{2,1,0:T(2,128)(2,1)} copy(bf16[320,2,768]{2,0,1:T(8,128)(2,1)S(1)} %fusion.8) | data formatting | bytes 1966080 | tf_op jit(solution)/shard_map/convert_element_type | solution.py:76
  25.6 0.1 all-to-all-done.1
  25.7 6.8 %all-to-all-start = ((bf16[320,2,768]{2,1,0:T(2,128)(2,1)}), bf16[320,2,768]{2,1,0:T(2,128)(2,1)S(1)}, u32[]{:S(2)}, u32[]{:S(2)}) async-start(bf16[320,2,768]{2,1,0:T(2,128)(2,1)} %copy.46), calls=%async_computation | async-start | bytes 1966080 | tf_op jit(solution)/shard_map/all_to_all | solution.py:81
  32.5 0.2 reduce-scatter.2.cloned.1.call-start
  32.7 0.1 all_to_all.17
  32.9 0.1 fusion.52
  33.0 0.2 compare_and_fusion.1
  33.2 22.0 %all-to-all-done = bf16[320,2,768]{2,1,0:T(2,128)(2,1)S(1)} async-done(((bf16[320,2,768]{2,1,0:T(2,128)(2,1)}), bf16[320,2,768]{2,1,0:T(2,128)(2,1)S(1)}, u32[]{:S(2)}, u32[]{:S(2)}) %all-to-all-start) | async-done | bytes 983072 | tf_op jit(solution)/shard_map/all_to_all | solution.py:81
  55.2 2.2 %fusion.47 = (bf16[320,1,768]{2,1,0:T(2,128)(2,1)S(1)}, bf16[320,1,768]{2,1,0:T(2,128)(2,1)}) fusion(bf16[320,2,768]{2,1,0:T(2,128)(2,1)S(1)} %all-to-all-done), kind=kLoop, calls=%fused_computation.86 | loop fusion | bytes 1966080 | tf_op jit(solution)/shard_map/slice | solution.py:39
  57.3 2.4 %copy.55 = bf16[320,1,768]{0,2,1:T(8,128)(2,1)S(1)} copy(bf16[320,1,768]{2,1,0:T(2,128)(2,1)} %get-tuple-element.8) | data formatting | bytes 983040
  59.7 0.7 fusion.51
  60.4 0.1 fusion.50
  60.5 0.6 fusion.53
  61.2 1.3 %fusion.16 = f32[4,160,320]{2,1,0:T(8,128)} fusion(bf16[160,4,64]{0,2,1:T(8,128)(2,1)S(1)} %bitcast.90, bf16[320,4,64]{0,2,1:T(8,128)(2,1)S(1)} %bitcast.80, pred[160,320]{1,0:T(8,128)(4,1)S(1)} %get-tuple-element.24), kind=kOutput, calls=%fused_computation.21 | convolution fusion | flops 26624000 | bytes 1116160 | tf_op jit(solution)/shard_map/qhd,khd->hqk/dot_general | solution.py:11
  62.5 0.6 fusion.54
  63.1 1.3 %fusion.15 = f32[4,160,320]{2,1,0:T(8,128)} fusion(bf16[160,4,64]{0,2,1:T(8,128)(2,1)S(1)} %bitcast.88, bf16[320,4,64]{0,2,1:T(8,128)(2,1)S(1)} %bitcast.82, pred[160,320]{1,0:T(8,128)(4,1)S(1)} %get-tuple-element.23), kind=kOutput, calls=%fused_computation.20 | convolution fusion | flops 26624000 | bytes 1116160 | tf_op jit(solution)/shard_map/qhd,khd->hqk/dot_general | solution.py:11
  64.4 1.0 copy.54
  65.4 0.7 fusion.49
  66.1 0.1 fusion.48
  66.2 0.6 fusion.55
  66.9 0.3 fusion.14
  67.2 0.6 fusion.56
  67.8 0.3 fusion.13
  68.2 0.0 copy-start.1
  68.2 2.9 %fusion.20 = bf16[160,4,64]{0,2,1:T(8,128)(2,1)S(1)} fusion(bf16[320,4,64]{0,2,1:T(8,128)(2,1)} %bitcast.93, f32[4,160]{1,0:T(4,128)S(1)} %fusion.53, f32[4,160,320]{2,1,0:T(8,128)} %fusion.16), kind=kOutput, calls=%fused_computation.30 | convolution fusion | flops 26870720 | bytes 1067520 | tf_op jit(solution)/shard_map/hqk,khd->qhd/dot_general | solution.py:19
  71.1 0.0 copy-done.1
  71.1 3.5 %fusion.19 = bf16[160,4,64]{0,2,1:T(8,128)(2,1)} fusion(bf16[320,4,64]{0,2,1:T(8,128)(2,1)S(1)} %bitcast.94, f32[4,160]{1,0:T(4,128)S(1)} %fusion.54, f32[4,160,320]{2,1,0:T(8,128)} %fusion.15), kind=kOutput, calls=%fused_computation.29 | convolution fusion | flops 26870720 | bytes 1067520 | tf_op jit(solution)/shard_map/hqk,khd->qhd/dot_general | solution.py:19
  74.6 1.0 pad_maximum_fusion.2
  75.6 0.2 copy.52
  75.8 0.0 copy-start.2
  75.8 3.0 %fusion.18 = bf16[160,4,64]{0,2,1:T(8,128)(2,1)} fusion(bf16[320,4,64]{0,2,1:T(8,128)(2,1)} %bitcast.95, f32[4,160]{1,0:T(4,128)S(1)} %fusion.55, f32[4,160,320]{2,1,0:T(8,128)S(1)} %fusion.14), kind=kOutput, calls=%fused_computation.28 | convolution fusion | flops 26870720 | bytes 1067520 | tf_op jit(solution)/shard_map/hqk,khd->qhd/dot_general | solution.py:19
  78.8 0.0 copy-done.2
  78.8 1.3 %fusion.17 = bf16[160,4,64]{0,2,1:T(8,128)(2,1)S(1)} fusion(bf16[320,4,64]{0,2,1:T(8,128)(2,1)S(1)} %bitcast.96, f32[4,160]{1,0:T(4,128)S(1)} %fusion.56, f32[4,160,320]{2,1,0:T(8,128)S(1)} %fusion.13), kind=kOutput, calls=%fused_computation.27 | convolution fusion | flops 26870720 | bytes 1067520 | tf_op jit(solution)/shard_map/hqk,khd->qhd/dot_general | solution.py:19
  80.1 0.0 copy-done.3
  80.1 0.1 pad_maximum_fusion.1
  80.2 0.2 copy.51
  80.5 0.7 pad_maximum_fusion
  81.2 15.4 %all_to_all.22 = bf16[320,2,256]{2,1,0:T(2,128)(2,1)S(1)} all-to-all(bf16[320,2,256]{2,1,0:T(2,128)(2,1)S(1)} %pad_maximum_fusion), channel_id=1, replica_groups=mesh['seq'=16,'head'=2] {'seq'}, dimensions={0} | all-to-all | bytes 655360 | tf_op jit(solution)/shard_map/all_to_all | solution.py:41
  96.6 0.3 convolution_convert_fusion.1
  96.9 1.1 fusion.57
  98.1 0.0 reduce-scatter.2.cloned.1.call-update
  98.1 6.0 %reduce-scatter.2.cloned.1.call-done = f32[64,1024]{1,0:T(8,128)} async-done(((f32[128,1024]{1,0:T(8,128)}), f32[64,1024]{1,0:T(8,128)}) %reduce-scatter.2.cloned.1.call-update) | async-done | bytes 262160 | tf_op jit(solution)/shard_map/reduce_scatter | solution.py:89
  104.1 1.6 %convert_element_type.96 = bf16[64,1024]{1,0:T(8,128)(2,1)} convert(f32[64,1024]{1,0:T(8,128)} %reduce-scatter.2.cloned.1.call-done) | non-fusion elementwise | flops 65536 | bytes 393216 | tf_op jit(solution)/shard_map/convert_element_type | solution.py:95
  (11 shorter events, 0.1 us)
Async XLA Ops:
  6.5 90.4 %copy-start = (bf16[512,1024]{1,0:T(8,128)(2,1)S(1)}, bf16[512,1024]{1,0:T(8,128)(2,1)}, u32[]{:S(2)}) copy-start(bf16[512,1024]{1,0:T(8,128)(2,1)} %param.11) | copy-start | bytes 3145732
  6.5 13.2 %copy-start.4 = (bf16[1024,512]{1,0:T(8,128)(2,1)S(1)}, bf16[1024,512]{1,0:T(8,128)(2,1)}, u32[]{:S(2)}) copy-start(bf16[1024,512]{1,0:T(8,128)(2,1)} %param.10) | copy-start | bytes 3145732
  6.5 14.5 %copy-start.7 = (bf16[128,1024]{1,0:T(8,128)(2,1)S(1)}, bf16[128,1024]{1,0:T(8,128)(2,1)}, u32[]{:S(2)}) copy-start(bf16[128,1024]{1,0:T(8,128)(2,1)} %param.7) | copy-start | bytes 786436
  10.0 15.7 %all-to-all-start.1 = ((s32[16,20,2]{1,2,0:T(2,128)}), s32[16,20,2]{1,2,0:T(2,128)S(1)}, u32[]{:S(2)}, u32[]{:S(2)}) async-start(s32[16,20,2]{1,2,0:T(2,128)} %copy.48), calls=%async_computation.1 | async-start | bytes 32768 | tf_op jit(solution)/shard_map/all_to_all | solution.py:82
  19.7 2.7 %copy-start.5 = (bf16[1024,512]{1,0:T(8,128)(2,1)S(1)}, bf16[1024,512]{1,0:T(8,128)(2,1)}, u32[]{:S(2)}) copy-start(bf16[1024,512]{1,0:T(8,128)(2,1)} %param.9) | copy-start | bytes 3145732
  21.0 1.6 %copy-start.6 = (bf16[1024,512]{1,0:T(8,128)(2,1)S(1)}, bf16[1024,512]{1,0:T(8,128)(2,1)}, u32[]{:S(2)}) copy-start(bf16[1024,512]{1,0:T(8,128)(2,1)} %param.8) | copy-start | bytes 3145732
  25.7 29.5 %all-to-all-start = ((bf16[320,2,768]{2,1,0:T(2,128)(2,1)}), bf16[320,2,768]{2,1,0:T(2,128)(2,1)S(1)}, u32[]{:S(2)}, u32[]{:S(2)}) async-start(bf16[320,2,768]{2,1,0:T(2,128)(2,1)} %copy.46), calls=%async_computation | async-start | bytes 1966080 | tf_op jit(solution)/shard_map/all_to_all | solution.py:81
  32.5 71.6 %reduce-scatter.2.cloned.1.call-start = ((), (), s32[]{:S(2)}) async-start(), calls=%async_computation.4 | async-start | bytes 786432 | tf_op jit(solution)/shard_map/reduce_scatter | solution.py:89
  68.2 2.9 %copy-start.1 = (bf16[320,256]{0,1:T(8,128)(2,1)S(1)}, bf16[320,256]{0,1:T(8,128)(2,1)}, u32[]{:S(2)}) copy-start(bf16[320,256]{0,1:T(8,128)(2,1)} %get-tuple-element.16) | copy-start | bytes 491524
  75.8 3.0 %copy-start.2 = (bf16[320,256]{0,1:T(8,128)(2,1)S(1)}, bf16[320,256]{0,1:T(8,128)(2,1)}, u32[]{:S(2)}) copy-start(bf16[320,256]{0,1:T(8,128)(2,1)} %get-tuple-element.12) | copy-start | bytes 491524
  78.8 1.3 %copy-start.3 = (bf16[160,4,64]{0,2,1:T(8,128)(2,1)S(1)}, bf16[160,4,64]{0,2,1:T(8,128)(2,1)}, u32[]{:S(2)}) copy-start(bf16[160,4,64]{0,2,1:T(8,128)(2,1)} %fusion.18) | copy-start | bytes 245764
Sparse Core Ops, SparseCore 0:
  98.2 5.8 reduce-scatter.1
where the time goes:
time: 113 us
  waiting for transfers between devices  28.1 us (25%)
  matrix products  23 us (20%)
  blocking collectives  15.4 us (14%)
  starting transfers between devices  15.3 us (14%)
  between operations  13.7 us (12%)
  local copies, waits for them, and re-layouts  10.5 us (9%)
  other arithmetic  6.52 us (6%)
    all_to_all x1, waiting for transfers between devices, per_device(): lax.all_to_all(send, 'seq', split_axis=0, concat_axis=0, tiled=True)  22 us
    all_to_all x1, blocking collectives, owner_side(): lax.all_to_all(result, 'seq', split_axis=0, concat_axis=0, tiled=True)  15.4 us
    dot_general x4, matrix products, attend_rows(): jnp.einsum('hqk,khd->qhd', weights, values, preferred_element_type=jnp.fl...  10.6 us
    all_to_all x1, starting transfers between devices, per_device(): lax.all_to_all(pos_slots, 'seq', split_axis=0, concat_axis=0, tiled=True)  8.31 us
    all_to_all x1, starting transfers between devices, per_device(): lax.all_to_all(send, 'seq', split_axis=0, concat_axis=0, tiled=True)  6.81 us
    reduce_scatter x1, waiting for transfers between devices, per_device(): lax.psum_scatter(jnp.dot(attended, w_out, preferred_element_type=jnp.floa...  5.98 us
    dot_general x6, matrix products, project_group(): jnp.dot(tokens, weight[:, lo:lo + width], preferred_element_type=jnp.floa...  4.71 us
    unnamed x18, local copies, waits for them, and re-layouts  3.37 us
  transfers between devices with their start and end apart: 3, of which 3 were waited for; matrix products, arithmetic and copies ran while one was open for 7% of the time, Pallas kernels for 0%

commit v1 on v0

--- a/solution.py
+++ b/solution.py
@@ -1,10 +1,233 @@
+import functools
+
 import jax
 import jax.numpy as jnp
 from jax import lax
+from jax.experimental import pallas as pl
+from jax.experimental.pallas import tpu as pltpu
 from jax.sharding import PartitionSpec as P
 
 HD = 64
 GROUP_HEADS = 4
+
+SPLIT = 4
+PLANE = 4
+META = 16
+BASE = 128
+VMEM_LIMIT = 48 << 20
+LOG2E = 1.4426950408889634
+
+
+def project_kernel(tok_ref, pos_ref, cid_ref, wq_ref, wk_ref, wv_ref, *rest):
+    kv0_ref, q0_ref, m1_ref, m2_ref, m3_ref, wbuf, qkv, sems = rest
+    tok, cols = tok_ref.shape[0], wq_ref.shape[1]
+    pair = cols // SPLIT
+    half = cols // 2
+    copies = []
+    for part, w_ref in enumerate((wq_ref, wk_ref, wv_ref)):
+        for side in range(2):
+            lanes = pl.ds(side * half, half)
+            copy = pltpu.make_async_copy(
+                w_ref.at[:, lanes], wbuf.at[part, :, lanes], sems.at[part, side]
+            )
+            copy.start()
+            copies.append((part, side, copy))
+    rows = tok_ref[...]
+    for part, side, copy in copies:
+        copy.wait()
+        result = jnp.dot(
+            rows, wbuf[part, :, side * half : (side + 1) * half], preferred_element_type=jnp.float32
+        )
+        start = part * cols + side * half
+        qkv[:, start : start + half] = result.astype(jnp.bfloat16)
+    high_digit = jnp.broadcast_to(pos_ref[...] // BASE, (META, tok))
+    low_digit = jnp.broadcast_to(pos_ref[...] % BASE, (META, tok))
+    first = lax.broadcasted_iota(jnp.int32, (META, tok), 0) == 0
+    chip = lax.axis_index("seq") // PLANE
+    for step, refs in enumerate(((kv0_ref, q0_ref), (m1_ref,), (m2_ref,), (m3_ref,))):
+        who = jnp.bitwise_xor(chip, step)
+        kv_ref = refs[0]
+        lo = pl.multiple_of(who * pair, pair)
+        query = qkv[:, pl.ds(lo, pair)]
+        kv_ref[:tok, :pair] = qkv[:, pl.ds(pl.multiple_of(cols + lo, pair), pair)]
+        kv_ref[:tok, pair:] = qkv[:, pl.ds(pl.multiple_of(2 * cols + lo, pair), pair)]
+        ids = jnp.where(who >= SPLIT // 2, cid_ref[1:2, :], cid_ref[0:1, :])
+        left = jnp.where(first, jnp.broadcast_to(ids, (META, tok)), low_digit)
+        kv_ref[tok : tok + META, :pair] = left.astype(jnp.float32).astype(jnp.bfloat16)
+        kv_ref[tok : tok + META, pair:] = high_digit.astype(jnp.float32).astype(jnp.bfloat16)
+        q_ref, base = (refs[1], 0) if step == 0 else (kv_ref, tok + META)
+        q_ref[base : base + tok // 2, :pair] = query[: tok // 2]
+        q_ref[base : base + tok // 2, pair:] = query[tok // 2 :]
+
+
+def project(tokens, positions, cluster_ids, w_query, w_key, w_value):
+    tok, depth = tokens.shape
+    cols = w_query.shape[1]
+    wide = 2 * cols // SPLIT
+    vmem = pl.BlockSpec(memory_space=pltpu.VMEM)
+    hbm = pl.BlockSpec(memory_space=pl.ANY)
+    full = tok + META + tok // 2
+
+    def shape(rows):
+        return jax.ShapeDtypeStruct((rows, wide), jnp.bfloat16)
+
+    return pl.pallas_call(
+        project_kernel,
+        out_shape=(shape(tok + META), shape(tok // 2), shape(full), shape(full), shape(full)),
+        in_specs=[vmem, vmem, vmem, hbm, hbm, hbm],
+        out_specs=(vmem,) * 5,
+        scratch_shapes=[
+            pltpu.VMEM((3, depth, cols), jnp.bfloat16),
+            pltpu.VMEM((tok, 3 * cols), jnp.bfloat16),
+            pltpu.SemaphoreType.DMA((3, 2)),
+        ],
+        compiler_params=pltpu.CompilerParams(vmem_limit_bytes=VMEM_LIMIT),
+        cost_estimate=pl.CostEstimate(
+            flops=6 * tok * depth * cols, bytes_accessed=6 * depth * cols, transcendentals=0
+        ),
+        name="project",
+    )(tokens, positions.reshape(1, tok), cluster_ids, w_query, w_key, w_value)
+
+
+def attend_kernel(total, tok, *refs):
+    q_refs = refs[:SPLIT]
+    kv_refs = refs[SPLIT : SPLIT + 2 * PLANE]
+    out_refs = refs[SPLIT + 2 * PLANE : SPLIT + 2 * PLANE + SPLIT]
+    keys, values, codes, column = refs[SPLIT + 2 * PLANE + SPLIT :]
+    pair = keys.shape[1]
+    block = tok + META
+    stride = 2 * total
+
+    def ids_of(ref, base):
+        cid = ref[base + tok : base + tok + 1, :pair].astype(jnp.float32)
+        low = ref[base + tok + 1 : base + tok + 2, :pair].astype(jnp.float32)
+        high = ref[base + tok : base + tok + 1, pair:].astype(jnp.float32)
+        pos = high * float(BASE) + low
+        return cid * float(stride) + pos, pos
+
+    at = 0
+    for ref in kv_refs:
+        for item in range(ref.shape[0] // block):
+            base = item * block
+            keys[at : at + tok, :] = ref[base : base + tok, :pair]
+            values[at : at + tok, :] = ref[base : base + tok, pair:]
+            codes[0:1, at : at + tok] = ids_of(ref, base)[0]
+            at += tok
+    lane = lax.broadcasted_iota(jnp.int32, (tok, pair), 1) < HD
+    key_codes = codes[0:1, :]
+    scale = HD**-0.5 * LOG2E
+    for item in range(SPLIT):
+        ref, base = (kv_refs[0], 0) if item == 0 else (kv_refs[1], (item - 1) * block)
+        code, pos = ids_of(ref, base)
+        column[0:1, :] = code
+        column[1:2, :] = pos
+        turned = jnp.transpose(column[...])
+        gap = turned[:, 0:1] - key_codes
+        allowed = (gap >= 0.0) & (gap <= turned[:, 1:2])
+        bias = jnp.where(allowed, 0.0, -1e30)
+        q_ref = q_refs[item]
+        start = q_ref.shape[0] - tok // 2
+        query = jnp.concatenate([q_ref[start:, :pair], q_ref[start:, pair:]], axis=0)
+        results = []
+        for head in range(2):
+            own = jnp.where(lane if head == 0 else jnp.logical_not(lane), query, jnp.zeros_like(query))
+            scores = lax.dot_general(
+                own, keys[...], (((1,), (1,)), ((), ())), preferred_element_type=jnp.float32
+            )
+            scores = scores * scale + bias
+            top = jnp.max(scores, axis=1, keepdims=True)
+            expo = jnp.exp2(scores - top)
+            weights = expo * (1.0 / jnp.sum(expo, axis=1, keepdims=True))
+            results.append(
+                jnp.dot(weights.astype(jnp.bfloat16), values[...], preferred_element_type=jnp.float32)
+            )
+        out_refs[item][...] = jnp.where(lane, results[0], results[1]).astype(jnp.bfloat16)
+
+
+def attend(total, tok, queries, sources):
+    pair = sources[0].shape[1] // 2
+    vmem = pl.BlockSpec(memory_space=pltpu.VMEM)
+    count = SPLIT * PLANE * tok
+    return pl.pallas_call(
+        functools.partial(attend_kernel, total, tok),
+        out_shape=(jax.ShapeDtypeStruct((tok, pair), jnp.bfloat16),) * SPLIT,
+        in_specs=[vmem] * (len(queries) + len(sources)),
+        out_specs=(vmem,) * SPLIT,
+        scratch_shapes=[
+            pltpu.VMEM((count, pair), jnp.bfloat16),
+            pltpu.VMEM((count, pair), jnp.bfloat16),
+            pltpu.VMEM((8, count), jnp.float32),
+            pltpu.VMEM((8, tok), jnp.float32),
+        ],
+        compiler_params=pltpu.CompilerParams(vmem_limit_bytes=VMEM_LIMIT),
+        cost_estimate=pl.CostEstimate(
+            flops=8 * SPLIT * tok * count * pair,
+            bytes_accessed=4 * count * pair,
+            transcendentals=2 * SPLIT * tok * count,
+        ),
+        name="attend",
+    )(*queries, *sources)
+
+
+def mix_kernel(*refs):
+    own_refs, other_refs = refs[:SPLIT], refs[SPLIT : 2 * SPLIT]
+    w_own, w_other, out_ref, left, right = refs[2 * SPLIT :]
+    rows, pair = out_ref.shape[0], own_refs[0].shape[1]
+    chip = lax.axis_index("seq") // PLANE
+    mine = pl.ds(pl.multiple_of(lax.axis_index("head") * rows, rows), rows)
+    for step in range(SPLIT):
+        lanes = pl.ds(pl.multiple_of(jnp.bitwise_xor(chip, step) * pair, pair), pair)
+        left[:, lanes] = own_refs[step][mine, :]
+        right[:, lanes] = other_refs[step][mine, :]
+    total = jnp.dot(left[...], w_own[...], preferred_element_type=jnp.float32)
+    total += jnp.dot(right[...], w_other[...], preferred_element_type=jnp.float32)
+    out_ref[...] = total.astype(jnp.bfloat16)
+
+
+def mix(own, other, w_own, w_other):
+    rows = own[0].shape[0] // 2
+    deep, width = w_own.shape
+    vmem = pl.BlockSpec(memory_space=pltpu.VMEM)
+    return pl.pallas_call(
+        mix_kernel,
+        out_shape=jax.ShapeDtypeStruct((rows, width), jnp.bfloat16),
+        in_specs=[vmem] * (2 * SPLIT + 2),
+        out_specs=vmem,
+        scratch_shapes=[pltpu.VMEM((rows, deep), jnp.bfloat16)] * 2,
+        compiler_params=pltpu.CompilerParams(vmem_limit_bytes=VMEM_LIMIT),
+        cost_estimate=pl.CostEstimate(
+            flops=4 * rows * deep * width, bytes_accessed=4 * deep * width, transcendentals=0
+        ),
+        name="mix",
+    )(*own, *other, w_own, w_other)
+
+
+def per_device_split(tokens, w_query, w_key, w_value, w_out, cluster_ids, positions):
+    tok = tokens.shape[0]
+    owners = lax.axis_size("seq")
+    block = tok + META
+
+    def send(array, bits):
+        return lax.ppermute(array, "seq", [(i, i ^ bits) for i in range(owners)])
+
+    def swap(array):
+        return lax.ppermute(array, "head", [(0, 1), (1, 0)])
+
+    w_other = swap(w_out)
+    kv0, q0, m1, m2, m3 = project(tokens, positions, cluster_ids, w_query, w_key, w_value)
+    r2 = send(m2, 2 * PLANE)
+    r3 = send(m3, 3 * PLANE)
+    r1 = send(m1, PLANE)
+    rest = jnp.concatenate([r1[:block], r2[:block], r3[:block]], axis=0)
+    sources = [kv0, rest]
+    for bits in (1, 2, 3):
+        sources += [send(kv0, bits), send(rest, bits)]
+    a0, a1, a2, a3 = attend(owners * tok, tok, (q0, r1, r2, r3), sources)
+    b2 = send(a2, 2 * PLANE)
+    b3 = send(a3, 3 * PLANE)
+    b1 = send(a1, PLANE)
+    own = (a0, b1, b2, b3)
+    return mix(own, tuple(swap(item) for item in own), w_out, w_other)
 
 
 def attend_rows(query, keys, values, query_pos, key_pos):
@@ -41,7 +264,7 @@
     return lax.all_to_all(result, "seq", split_axis=0, concat_axis=0, tiled=True)
 
 
-def per_device(tokens, w_query, w_key, w_value, w_out, cluster_ids, positions):
+def per_device_owner(tokens, w_query, w_key, w_value, w_out, cluster_ids, positions):
     tok = tokens.shape[0]
     groups_here = cluster_ids.shape[0]
     owners = lax.axis_size("seq")
@@ -106,6 +329,7 @@
         P("seq"),
     )
     out_specs = P(("seq", "head"), None)
+    plan = per_device_split if mesh.shape["seq"] == SPLIT * PLANE else per_device_owner
     return jax.shard_map(
-        per_device, mesh=mesh, in_specs=in_specs, out_specs=out_specs, check_vma=False
-    )
+        plan, mesh=mesh, in_specs=in_specs, out_specs=out_specs, check_vma=False
+    )

time: 113 us -> 57.5 us (0.51)
  matrix products: 23 us -> 0 us
  blocking collectives: 15.4 us -> 0 us
  between operations: 13.7 us -> 0.09 us
  Pallas kernels: 0 us -> 9.22 us
  waiting for transfers between devices: 28.1 us -> 20 us
  other arithmetic: 6.52 us -> 0.02 us
  starting transfers between devices: 15.3 us -> 21.5 us
  local copies, waits for them, and re-layouts: 10.5 us -> 6.43 us
    all_to_all x2 -> x0, waiting for transfers between devices: 22.1 us -> none  [the longest x1 22 us: per_device(): lax.all_to_all(send, 'seq', split_axis=0, concat_axis=0, tiled=True)]
    ppermute x0 -> x17, starting transfers between devices: none -> 21.5 us  [the longest x12 20.5 us: send(): return lax.ppermute(array, 'seq', [(i, i ^ bits) for i in range(owners)])]
    dot_general x17 -> x0, matrix products: 20.5 us -> none  [the longest x4 10.6 us: attend_rows(): jnp.einsum('hqk,khd->qhd', weights, values, preferred_element_type=jnp.fl...]
    ppermute x0 -> x17, waiting for transfers between devices: none -> 20 us  [the longest x12 18.8 us: send(): return lax.ppermute(array, 'seq', [(i, i ^ bits) for i in range(owners)])]
    all_to_all x1 -> x0, blocking collectives: 15.4 us -> none  [owner_side(): lax.all_to_all(result, 'seq', split_axis=0, concat_axis=0, tiled=True)]
    all_to_all x2 -> x0, starting transfers between devices: 15.1 us -> none  [the longest x1 8.31 us: per_device(): lax.all_to_all(pos_slots, 'seq', split_axis=0, concat_axis=0, tiled=True)]
    pallas_call x0 -> x3, Pallas kernels: none -> 9.22 us  [the longest x1 6.02 us: attend(): pl.pallas_call(functools.partial(attend_kernel, total, tok), out_shape=(j...]
    reduce_scatter x1 -> x0, waiting for transfers between devices: 5.98 us -> none  [per_device(): lax.psum_scatter(jnp.dot(attended, w_out, preferred_element_type=jnp.floa...]
  transfers between devices with their start and end apart: 3 -> 17, of which waited for: 3 -> 6; matrix products, arithmetic and copies ran while one was open for 7% -> 0% of each run, Pallas kernels for 0% -> 14%
where the time goes in v1:
time: 57.5 us; the launch traced here: 57.2 us
  starting transfers between devices  21.5 us (37%)
  waiting for transfers between devices  20 us (35%)
  Pallas kernels  9.22 us (16%)
  local copies, waits for them, and re-layouts  6.43 us (11%)
    ppermute x12, starting transfers between devices, send(): return lax.ppermute(array, 'seq', [(i, i ^ bits) for i in range(owners)])  20.5 us
    ppermute x12, waiting for transfers between devices, send(): return lax.ppermute(array, 'seq', [(i, i ^ bits) for i in range(owners)])  18.8 us
    pallas_call x1, Pallas kernels, attend(): pl.pallas_call(functools.partial(attend_kernel, total, tok), out_shape=(j...  6.02 us
    unnamed x22, local copies, waits for them, and re-layouts  5.51 us
    pallas_call x1, Pallas kernels, project(): pl.pallas_call(project_kernel, out_shape=(shape(tok + META), shape(tok //...  2.06 us
    ppermute x5, waiting for transfers between devices, swap(): return lax.ppermute(array, 'head', [(0, 1), (1, 0)])  1.2 us
  transfers between devices with their start and end apart: 17, of which 6 were waited for; matrix products, arithmetic and copies ran while one was open for 0% of the time, Pallas kernels for 14%

profile of v1, /device:TPU:0, one launch (start us, length us, event | category | flops | bytes accessed | tf_op | source)
XLA Modules:
  0.0 57.2 jit_solution(18437211259739842047)
XLA Ops:
  0.0 0.0 copy-start.10
  0.0 0.0 copy-start.9
  0.0 0.5 collective-permute-start.16
  0.5 0.2 copy-done.10
  0.7 0.0 copy-done.9
  0.7 0.0 copy-start.1
  0.7 1.2 %copy-done.1 = bf16[1024,512]{1,0:T(8,128)(2,1)S(1)} copy-done((bf16[1024,512]{1,0:T(8,128)(2,1)S(1)}, bf16[1024,512]{1,0:T(8,128)(2,1)}, u32[]{:S(2)}) %copy-start.1) | copy-done | bytes 1048600
  1.9 0.0 copy-start.2
  1.9 1.2 %copy-done.2 = bf16[1024,512]{1,0:T(8,128)(2,1)S(1)} copy-done((bf16[1024,512]{1,0:T(8,128)(2,1)S(1)}, bf16[1024,512]{1,0:T(8,128)(2,1)}, u32[]{:S(2)}) %copy-start.2) | copy-done | bytes 1048600
  3.1 0.0 copy-start.3
  3.1 1.2 %copy-done.3 = bf16[1024,512]{1,0:T(8,128)(2,1)S(1)} copy-done((bf16[1024,512]{1,0:T(8,128)(2,1)S(1)}, bf16[1024,512]{1,0:T(8,128)(2,1)}, u32[]{:S(2)}) %copy-start.3) | copy-done | bytes 1048600
  4.4 0.0 copy-start.4
  4.4 0.9 %copy-done.4 = bf16[128,1024]{1,0:T(8,128)(2,1)S(1)} copy-done((bf16[128,1024]{1,0:T(8,128)(2,1)S(1)}, bf16[128,1024]{1,0:T(8,128)(2,1)}, u32[]{:S(2)}) %copy-start.4) | copy-done | bytes 262168
  5.3 2.1 %project.1 = (bf16[144,256]{1,0:T(8,128)(2,1)S(1)}, bf16[64,256]{1,0:T(8,128)(2,1)S(1)}, bf16[208,256]{1,0:T(8,128)(2,1)S(1)}, bf16[208,256]{1,0:T(8,128)(2,1)S(1)}, bf16[208,256]{1,0:T(8,128)(2,1)S(1)}) custom-call(bf16[128,1024]{1,0:T(8,128)(2,1)S(1)} %copy-done.4, s32[1,128]{1,0:T(1,128)S(1)} %bitcast.1, s32[2,128]{1,0:T(2,128)S(1)} %copy-done.9, ...), custom_call_target="tpu_custom_call" | custom-call | flops 402653184 | bytes 3145728 | tf_op jit(solution)/shard_map/project/pallas_call | solution.py:74
  7.4 3.1 %collective-permute-start = (bf16[208,256]{1,0:T(8,128)(2,1)S(1)}, bf16[208,256]{1,0:T(8,128)(2,1)S(1)}, u32[]{:S(2)}, u32[]{:S(2)}) collective-permute-start(bf16[208,256]{1,0:T(8,128)(2,1)S(1)} %get-tuple-element.15), channel_id=1, source_target_pairs={{0,8},{2,10},{4,12},{6,14},{8,0},{10,2},{12,4},{14,6},{16,24},{18,... | collective-permute-start | bytes 319496 | tf_op jit(solution)/shard_map/ppermute | solution.py:211
  10.5 2.6 %collective-permute-start.1 = (bf16[208,256]{1,0:T(8,128)(2,1)S(1)}, bf16[208,256]{1,0:T(8,128)(2,1)S(1)}, u32[]{:S(2)}, u32[]{:S(2)}) collective-permute-start(bf16[208,256]{1,0:T(8,128)(2,1)S(1)} %get-tuple-element.16), channel_id=1, source_target_pairs={{0,16},{2,18},{4,20},{6,22},{8,24},{10,26},{12,28},{14,30},{16,0},... | collective-permute-start | bytes 319496 | tf_op jit(solution)/shard_map/ppermute | solution.py:211
  13.1 0.0 collective-permute-start.2
  13.1 2.7 %collective-permute-start.7 = (bf16[144,256]{1,0:T(8,128)(2,1)S(1)}, bf16[144,256]{1,0:T(8,128)(2,1)S(1)}, u32[]{:S(2)}, u32[]{:S(2)}) collective-permute-start(bf16[144,256]{1,0:T(8,128)(2,1)S(1)} %get-tuple-element.18.refs_4_), channel_id=1, source_target_pairs={{0,6},{2,4},{4,2},{6,0},{8,14},{10,12},{12,10},{14,8},{16,22},{18,... | collective-permute-start | bytes 221192 | tf_op jit(solution)/shard_map/ppermute | solution.py:211
  15.7 0.0 collective-permute-done.refs_1_
  15.7 0.0 copy-start.5
  15.7 5.8 %collective-permute-done.1.refs_2_ = bf16[208,256]{1,0:T(8,128)(2,1)S(1)} collective-permute-done((bf16[208,256]{1,0:T(8,128)(2,1)S(1)}, bf16[208,256]{1,0:T(8,128)(2,1)S(1)}, u32[]{:S(2)}, u32[]{:S(2)}) %collective-permute-start.1) | collective-permute-done | bytes 106528 | tf_op jit(solution)/shard_map/ppermute | solution.py:211
  21.5 0.0 copy-start.7
  21.5 0.0 copy-done.5
  21.5 0.6 %copy-done.7 = bf16[208,256]{1,0:T(8,128)(2,1)} copy-done((bf16[208,256]{1,0:T(8,128)(2,1)}, bf16[208,256]{1,0:T(8,128)(2,1)S(1)}, u32[]{:S(2)}) %copy-start.7) | copy-done | bytes 106520
  22.1 0.0 collective-permute-done.2.refs_3_
  22.1 0.0 slice-start
  22.2 0.0 slice-start.1
  22.2 0.9 %slice-done = bf16[144,256]{1,0:T(8,128)(2,1)S(1)} async-done(((bf16[208,256]{1,0:T(8,128)(2,1)}), bf16[144,256]{1,0:T(8,128)(2,1)S(1)}, s32[]{:S(2)}) %slice-start) | async-done | bytes 73752 | tf_op jit(solution)/shard_map/slice | solution.py:221
  23.0 0.0 slice-done.1
  23.1 0.0 copy-start.6
  23.1 0.0 copy-start.8
  23.1 2.5 %collective-permute-start.8 = (bf16[432,256]{1,0:T(8,128)(2,1)S(1)}, bf16[432,256]{1,0:T(8,128)(2,1)S(1)}, u32[]{:S(2)}, u32[]{:S(2)}) collective-permute-start(bf16[432,256]{1,0:T(8,128)(2,1)S(1)} %pad_maximum_fusion.refs_5_), channel_id=1, source_target_pairs={{0,6},{2,4},{4,2},{6,0},{8,14},{10,12},{12,10},{14,8},{16,22},{18,... | collective-permute-start | bytes 663560 | tf_op jit(solution)/shard_map/ppermute | solution.py:211
  25.6 0.5 collective-permute-start.6
  26.1 0.5 collective-permute-start.4
  26.6 0.0 collective-permute-done.7.refs_10_
  26.7 1.5 %collective-permute-start.5 = (bf16[144,256]{1,0:T(8,128)(2,1)S(1)}, bf16[144,256]{1,0:T(8,128)(2,1)S(1)}, u32[]{:S(2)}, u32[]{:S(2)}) collective-permute-start(bf16[144,256]{1,0:T(8,128)(2,1)S(1)} %get-tuple-element.18.refs_4_), channel_id=1, source_target_pairs={{0,4},{2,6},{4,0},{6,2},{8,12},{10,14},{12,8},{14,10},{16,20},{18,... | collective-permute-start | bytes 221192 | tf_op jit(solution)/shard_map/ppermute | solution.py:211
  28.2 6.3 %collective-permute-done.5.refs_8_ = bf16[144,256]{1,0:T(8,128)(2,1)S(1)} collective-permute-done((bf16[144,256]{1,0:T(8,128)(2,1)S(1)}, bf16[144,256]{1,0:T(8,128)(2,1)S(1)}, u32[]{:S(2)}, u32[]{:S(2)}) %collective-permute-start.5) | collective-permute-done | bytes 73760 | tf_op jit(solution)/shard_map/ppermute | solution.py:211
  34.4 1.5 %collective-permute-start.3 = (bf16[144,256]{1,0:T(8,128)(2,1)S(1)}, bf16[144,256]{1,0:T(8,128)(2,1)S(1)}, u32[]{:S(2)}, u32[]{:S(2)}) collective-permute-start(bf16[144,256]{1,0:T(8,128)(2,1)S(1)} %get-tuple-element.18.refs_4_), channel_id=1, source_target_pairs={{0,2},{2,0},{4,6},{6,4},{8,10},{10,8},{12,14},{14,12},{16,18},{18,... | collective-permute-start | bytes 221192 | tf_op jit(solution)/shard_map/ppermute | solution.py:211
  35.9 2.9 %collective-permute-done.3.refs_6_ = bf16[144,256]{1,0:T(8,128)(2,1)S(1)} collective-permute-done((bf16[144,256]{1,0:T(8,128)(2,1)S(1)}, bf16[144,256]{1,0:T(8,128)(2,1)S(1)}, u32[]{:S(2)}, u32[]{:S(2)}) %collective-permute-start.3) | collective-permute-done | bytes 73760 | tf_op jit(solution)/shard_map/ppermute | solution.py:211
  38.8 0.0 collective-permute-done.8.refs_11_
  38.8 0.0 collective-permute-done.6.refs_9_
  38.8 0.0 collective-permute-done.4.refs_7_
  38.8 0.0 copy-done.6
  38.8 0.0 copy-done.8
  38.8 0.0 copy-start
  38.8 6.0 %attend.1 = (bf16[128,128]{1,0:T(8,128)(2,1)S(1)}, bf16[128,128]{1,0:T(8,128)(2,1)S(1)}, bf16[128,128]{1,0:T(8,128)(2,1)S(1)}, bf16[128,128]{1,0:T(8,128)(2,1)S(1)}) custom-call(bf16[64,256]{1,0:T(8,128)(2,1)S(1)} %get-tuple-element.14.refs_0_, bf16[208,256]{1,0:T(8,128)(2,1)S(1)} %copy-done.6, bf16[208,256]{1,0:T(8,128)(2,1)S(1)} %copy-done.8, ...), custom_call_target="tpu_custom_call" | custom-call | flops 1073741824 | bytes 1048576 | tf_op jit(solution)/shard_map/attend/pallas_call | solution.py:151
  44.9 3.0 %collective-permute-start.9 = (bf16[128,128]{1,0:T(8,128)(2,1)S(1)}, bf16[128,128]{1,0:T(8,128)(2,1)S(1)}, u32[]{:S(2)}, u32[]{:S(2)}) collective-permute-start(bf16[128,128]{1,0:T(8,128)(2,1)S(1)} %get-tuple-element.20), channel_id=1, source_target_pairs={{0,8},{2,10},{4,12},{6,14},{8,0},{10,2},{12,4},{14,6},{16,24},{18,... | collective-permute-start | bytes 98312 | tf_op jit(solution)/shard_map/ppermute | solution.py:211
  47.8 1.2 %collective-permute-start.10 = (bf16[128,128]{1,0:T(8,128)(2,1)S(1)}, bf16[128,128]{1,0:T(8,128)(2,1)S(1)}, u32[]{:S(2)}, u32[]{:S(2)}) collective-permute-start(bf16[128,128]{1,0:T(8,128)(2,1)S(1)} %get-tuple-element.21), channel_id=1, source_target_pairs={{0,16},{2,18},{4,20},{6,22},{8,24},{10,26},{12,28},{14,30},{16,0},... | collective-permute-start | bytes 98312 | tf_op jit(solution)/shard_map/ppermute | solution.py:211
  49.1 1.3 %collective-permute-start.11 = (bf16[128,128]{1,0:T(8,128)(2,1)S(1)}, bf16[128,128]{1,0:T(8,128)(2,1)S(1)}, u32[]{:S(2)}, u32[]{:S(2)}) collective-permute-start(bf16[128,128]{1,0:T(8,128)(2,1)S(1)} %get-tuple-element.22), channel_id=1, source_target_pairs={{0,24},{2,26},{4,28},{6,30},{8,16},{10,18},{12,20},{14,22},{16,8},... | collective-permute-start | bytes 98312 | tf_op jit(solution)/shard_map/ppermute | solution.py:211
  50.4 0.0 collective-permute-start.12
  50.4 0.0 collective-permute-done.9.refs_1_
  50.4 0.5 collective-permute-start.13
  50.9 2.1 %collective-permute-done.10.refs_2_ = bf16[128,128]{1,0:T(8,128)(2,1)S(1)} collective-permute-done((bf16[128,128]{1,0:T(8,128)(2,1)S(1)}, bf16[128,128]{1,0:T(8,128)(2,1)S(1)}, u32[]{:S(2)}, u32[]{:S(2)}) %collective-permute-start.10) | collective-permute-done | bytes 32800 | tf_op jit(solution)/shard_map/ppermute | solution.py:211
  53.0 0.0 collective-permute-start.14
  53.0 1.8 %collective-permute-done.11.refs_3_ = bf16[128,128]{1,0:T(8,128)(2,1)S(1)} collective-permute-done((bf16[128,128]{1,0:T(8,128)(2,1)S(1)}, bf16[128,128]{1,0:T(8,128)(2,1)S(1)}, u32[]{:S(2)}, u32[]{:S(2)}) %collective-permute-start.11) | collective-permute-done | bytes 32800 | tf_op jit(solution)/shard_map/ppermute | solution.py:211
  54.8 0.0 collective-permute-start.15
  54.8 0.0 collective-permute-done.12.refs_4_
  54.8 0.0 collective-permute-done.13.refs_5_
  54.8 0.0 collective-permute-done.14.refs_6_
  54.8 1.2 %collective-permute-done.15.refs_7_ = bf16[128,128]{1,0:T(8,128)(2,1)S(1)} collective-permute-done((bf16[128,128]{1,0:T(8,128)(2,1)S(1)}, bf16[128,128]{1,0:T(8,128)(2,1)S(1)}, u32[]{:S(2)}, u32[]{:S(2)}) %collective-permute-start.15) | collective-permute-done | bytes 32800 | tf_op jit(solution)/shard_map/ppermute | solution.py:214
  56.0 0.0 collective-permute-done.16.refs_9_
  56.0 0.0 copy-done
  56.0 1.1 %mix.1 = bf16[64,1024]{1,0:T(8,128)(2,1)} custom-call(bf16[128,128]{1,0:T(8,128)(2,1)S(1)} %get-tuple-element.19.refs_0_, bf16[128,128]{1,0:T(8,128)(2,1)S(1)} %collective-permute-done.9.refs_1_, bf16[128,128]{1,0:T(8,128)(2,1)S(1)} %collective-permute-done.10.refs_2_, bf16[128,128]{1,0:T(8,128)(2,1)S(1)} %collective-permute-done.11.refs_3_, ...), custom_call_target="tpu_custom_call" | custom-call | flops 134217728 | bytes 2097152 | tf_op jit(solution)/shard_map/mix/pallas_call | solution.py:191
  (2 shorter events, 0.0 us)
Async XLA Ops:
  0.0 0.7 %copy-start.10 = (s32[128]{0:T(128)S(1)}, s32[128]{0:T(128)}, u32[]{:S(2)}) copy-start(s32[128]{0:T(128)} %param.13) | copy-start | bytes 1540
  0.0 0.7 %copy-start.9 = (s32[2,128]{1,0:T(2,128)S(1)}, s32[2,128]{1,0:T(2,128)}, u32[]{:S(2)}) copy-start(s32[2,128]{1,0:T(2,128)} %cid_ref.1) | copy-start | bytes 3076
  0.0 56.0 %collective-permute-start.16 = (bf16[512,1024]{1,0:T(8,128)(2,1)}, bf16[512,1024]{1,0:T(8,128)(2,1)S(1)}, u32[]{:S(2)}, u32[]{:S(2)}) collective-permute-start(bf16[512,1024]{1,0:T(8,128)(2,1)} %refs_8_.1), channel_id=1, source_target_pairs={{0,1},{1,0},{2,3},{3,2},{4,5},{5,4},{6,7},{7,6},{8,9},{9,8},{10,11... | collective-permute-start | bytes 3145736 | tf_op jit(solution)/shard_map/ppermute | solution.py:214
  0.7 1.2 %copy-start.1 = (bf16[1024,512]{1,0:T(8,128)(2,1)S(1)}, bf16[1024,512]{1,0:T(8,128)(2,1)}, u32[]{:S(2)}) copy-start(bf16[1024,512]{1,0:T(8,128)(2,1)} %wq_ref.1) | copy-start | bytes 3145732
  1.9 1.2 %copy-start.2 = (bf16[1024,512]{1,0:T(8,128)(2,1)S(1)}, bf16[1024,512]{1,0:T(8,128)(2,1)}, u32[]{:S(2)}) copy-start(bf16[1024,512]{1,0:T(8,128)(2,1)} %wk_ref.1) | copy-start | bytes 3145732
  3.1 1.2 %copy-start.3 = (bf16[1024,512]{1,0:T(8,128)(2,1)S(1)}, bf16[1024,512]{1,0:T(8,128)(2,1)}, u32[]{:S(2)}) copy-start(bf16[1024,512]{1,0:T(8,128)(2,1)} %wv_ref.1) | copy-start | bytes 3145732
  4.4 0.9 %copy-start.4 = (bf16[128,1024]{1,0:T(8,128)(2,1)S(1)}, bf16[128,1024]{1,0:T(8,128)(2,1)}, u32[]{:S(2)}) copy-start(bf16[128,1024]{1,0:T(8,128)(2,1)} %tok_ref.1) | copy-start | bytes 786436
  7.4 8.3 %collective-permute-start = (bf16[208,256]{1,0:T(8,128)(2,1)S(1)}, bf16[208,256]{1,0:T(8,128)(2,1)S(1)}, u32[]{:S(2)}, u32[]{:S(2)}) collective-permute-start(bf16[208,256]{1,0:T(8,128)(2,1)S(1)} %get-tuple-element.15), channel_id=1, source_target_pairs={{0,8},{2,10},{4,12},{6,14},{8,0},{10,2},{12,4},{14,6},{16,24},{18,... | collective-permute-start | bytes 319496 | tf_op jit(solution)/shard_map/ppermute | solution.py:211
  10.5 11.0 %collective-permute-start.1 = (bf16[208,256]{1,0:T(8,128)(2,1)S(1)}, bf16[208,256]{1,0:T(8,128)(2,1)S(1)}, u32[]{:S(2)}, u32[]{:S(2)}) collective-permute-start(bf16[208,256]{1,0:T(8,128)(2,1)S(1)} %get-tuple-element.16), channel_id=1, source_target_pairs={{0,16},{2,18},{4,20},{6,22},{8,24},{10,26},{12,28},{14,30},{16,0},... | collective-permute-start | bytes 319496 | tf_op jit(solution)/shard_map/ppermute | solution.py:211
  13.1 9.1 %collective-permute-start.2 = (bf16[208,256]{1,0:T(8,128)(2,1)S(1)}, bf16[208,256]{1,0:T(8,128)(2,1)S(1)}, u32[]{:S(2)}, u32[]{:S(2)}) collective-permute-start(bf16[208,256]{1,0:T(8,128)(2,1)S(1)} %get-tuple-element.17), channel_id=1, source_target_pairs={{0,24},{2,26},{4,28},{6,30},{8,16},{10,18},{12,20},{14,22},{16,8},... | collective-permute-start | bytes 319496 | tf_op jit(solution)/shard_map/ppermute | solution.py:211
  13.1 13.6 %collective-permute-start.7 = (bf16[144,256]{1,0:T(8,128)(2,1)S(1)}, bf16[144,256]{1,0:T(8,128)(2,1)S(1)}, u32[]{:S(2)}, u32[]{:S(2)}) collective-permute-start(bf16[144,256]{1,0:T(8,128)(2,1)S(1)} %get-tuple-element.18.refs_4_), channel_id=1, source_target_pairs={{0,6},{2,4},{4,2},{6,0},{8,14},{10,12},{12,10},{14,8},{16,22},{18,... | collective-permute-start | bytes 221192 | tf_op jit(solution)/shard_map/ppermute | solution.py:211
  15.7 5.8 %copy-start.5 = (bf16[208,256]{1,0:T(8,128)(2,1)}, bf16[208,256]{1,0:T(8,128)(2,1)S(1)}, u32[]{:S(2)}) copy-start(bf16[208,256]{1,0:T(8,128)(2,1)S(1)} %collective-permute-done.refs_1_) | copy-start | bytes 319492
  21.5 0.6 %copy-start.7 = (bf16[208,256]{1,0:T(8,128)(2,1)}, bf16[208,256]{1,0:T(8,128)(2,1)S(1)}, u32[]{:S(2)}) copy-start(bf16[208,256]{1,0:T(8,128)(2,1)S(1)} %collective-permute-done.1.refs_2_) | copy-start | bytes 319492
  22.1 0.9 %slice-start = ((bf16[208,256]{1,0:T(8,128)(2,1)}), bf16[144,256]{1,0:T(8,128)(2,1)S(1)}, s32[]{:S(2)}) async-start(bf16[208,256]{1,0:T(8,128)(2,1)} %copy-done.5), calls=%async_computation | async-start | bytes 147456 | tf_op jit(solution)/shard_map/slice | solution.py:221
  22.2 0.9 %slice-start.1 = ((bf16[208,256]{1,0:T(8,128)(2,1)}), bf16[144,256]{1,0:T(8,128)(2,1)S(1)}, s32[]{:S(2)}) async-start(bf16[208,256]{1,0:T(8,128)(2,1)} %copy-done.7), calls=%async_computation.1 | async-start | bytes 147456 | tf_op jit(solution)/shard_map/slice | solution.py:221
  23.1 15.7 %copy-start.6 = (bf16[208,256]{1,0:T(8,128)(2,1)S(1)}, bf16[208,256]{1,0:T(8,128)(2,1)}, u32[]{:S(2)}) copy-start(bf16[208,256]{1,0:T(8,128)(2,1)} %copy-done.5) | copy-start | bytes 319492
  23.1 15.7 %copy-start.8 = (bf16[208,256]{1,0:T(8,128)(2,1)S(1)}, bf16[208,256]{1,0:T(8,128)(2,1)}, u32[]{:S(2)}) copy-start(bf16[208,256]{1,0:T(8,128)(2,1)} %copy-done.7) | copy-start | bytes 319492
  23.1 15.7 %collective-permute-start.8 = (bf16[432,256]{1,0:T(8,128)(2,1)S(1)}, bf16[432,256]{1,0:T(8,128)(2,1)S(1)}, u32[]{:S(2)}, u32[]{:S(2)}) collective-permute-start(bf16[432,256]{1,0:T(8,128)(2,1)S(1)} %pad_maximum_fusion.refs_5_), channel_id=1, source_target_pairs={{0,6},{2,4},{4,2},{6,0},{8,14},{10,12},{12,10},{14,8},{16,22},{18,... | collective-permute-start | bytes 663560 | tf_op jit(solution)/shard_map/ppermute | solution.py:211
  25.6 13.2 %collective-permute-start.6 = (bf16[432,256]{1,0:T(8,128)(2,1)S(1)}, bf16[432,256]{1,0:T(8,128)(2,1)S(1)}, u32[]{:S(2)}, u32[]{:S(2)}) collective-permute-start(bf16[432,256]{1,0:T(8,128)(2,1)S(1)} %pad_maximum_fusion.refs_5_), channel_id=1, source_target_pairs={{0,4},{2,6},{4,0},{6,2},{8,12},{10,14},{12,8},{14,10},{16,20},{18,... | collective-permute-start | bytes 663560 | tf_op jit(solution)/shard_map/ppermute | solution.py:211
  26.1 12.7 %collective-permute-start.4 = (bf16[432,256]{1,0:T(8,128)(2,1)S(1)}, bf16[432,256]{1,0:T(8,128)(2,1)S(1)}, u32[]{:S(2)}, u32[]{:S(2)}) collective-permute-start(bf16[432,256]{1,0:T(8,128)(2,1)S(1)} %pad_maximum_fusion.refs_5_), channel_id=1, source_target_pairs={{0,2},{2,0},{4,6},{6,4},{8,10},{10,8},{12,14},{14,12},{16,18},{18,... | collective-permute-start | bytes 663560 | tf_op jit(solution)/shard_map/ppermute | solution.py:211
  26.7 7.8 %collective-permute-start.5 = (bf16[144,256]{1,0:T(8,128)(2,1)S(1)}, bf16[144,256]{1,0:T(8,128)(2,1)S(1)}, u32[]{:S(2)}, u32[]{:S(2)}) collective-permute-start(bf16[144,256]{1,0:T(8,128)(2,1)S(1)} %get-tuple-element.18.refs_4_), channel_id=1, source_target_pairs={{0,4},{2,6},{4,0},{6,2},{8,12},{10,14},{12,8},{14,10},{16,20},{18,... | collective-permute-start | bytes 221192 | tf_op jit(solution)/shard_map/ppermute | solution.py:211
  34.4 4.4 %collective-permute-start.3 = (bf16[144,256]{1,0:T(8,128)(2,1)S(1)}, bf16[144,256]{1,0:T(8,128)(2,1)S(1)}, u32[]{:S(2)}, u32[]{:S(2)}) collective-permute-start(bf16[144,256]{1,0:T(8,128)(2,1)S(1)} %get-tuple-element.18.refs_4_), channel_id=1, source_target_pairs={{0,2},{2,0},{4,6},{6,4},{8,10},{10,8},{12,14},{14,12},{16,18},{18,... | collective-permute-start | bytes 221192 | tf_op jit(solution)/shard_map/ppermute | solution.py:211
  38.8 17.2 %copy-start = (bf16[512,1024]{1,0:T(8,128)(2,1)S(1)}, bf16[512,1024]{1,0:T(8,128)(2,1)}, u32[]{:S(2)}) copy-start(bf16[512,1024]{1,0:T(8,128)(2,1)} %refs_8_.1) | copy-start | bytes 3145732
  44.9 5.6 %collective-permute-start.9 = (bf16[128,128]{1,0:T(8,128)(2,1)S(1)}, bf16[128,128]{1,0:T(8,128)(2,1)S(1)}, u32[]{:S(2)}, u32[]{:S(2)}) collective-permute-start(bf16[128,128]{1,0:T(8,128)(2,1)S(1)} %get-tuple-element.20), channel_id=1, source_target_pairs={{0,8},{2,10},{4,12},{6,14},{8,0},{10,2},{12,4},{14,6},{16,24},{18,... | collective-permute-start | bytes 98312 | tf_op jit(solution)/shard_map/ppermute | solution.py:211
  47.8 5.2 %collective-permute-start.10 = (bf16[128,128]{1,0:T(8,128)(2,1)S(1)}, bf16[128,128]{1,0:T(8,128)(2,1)S(1)}, u32[]{:S(2)}, u32[]{:S(2)}) collective-permute-start(bf16[128,128]{1,0:T(8,128)(2,1)S(1)} %get-tuple-element.21), channel_id=1, source_target_pairs={{0,16},{2,18},{4,20},{6,22},{8,24},{10,26},{12,28},{14,30},{16,0},... | collective-permute-start | bytes 98312 | tf_op jit(solution)/shard_map/ppermute | solution.py:211
  49.1 5.7 %collective-permute-start.11 = (bf16[128,128]{1,0:T(8,128)(2,1)S(1)}, bf16[128,128]{1,0:T(8,128)(2,1)S(1)}, u32[]{:S(2)}, u32[]{:S(2)}) collective-permute-start(bf16[128,128]{1,0:T(8,128)(2,1)S(1)} %get-tuple-element.22), channel_id=1, source_target_pairs={{0,24},{2,26},{4,28},{6,30},{8,16},{10,18},{12,20},{14,22},{16,8},... | collective-permute-start | bytes 98312 | tf_op jit(solution)/shard_map/ppermute | solution.py:211
  50.4 4.4 %collective-permute-start.12 = (bf16[128,128]{1,0:T(8,128)(2,1)S(1)}, bf16[128,128]{1,0:T(8,128)(2,1)S(1)}, u32[]{:S(2)}, u32[]{:S(2)}) collective-permute-start(bf16[128,128]{1,0:T(8,128)(2,1)S(1)} %get-tuple-element.19.refs_0_), channel_id=1, source_target_pairs={{0,1},{1,0},{2,3},{3,2},{4,5},{5,4},{6,7},{7,6},{8,9},{9,8},{10,11... | collective-permute-start | bytes 98312 | tf_op jit(solution)/shard_map/ppermute | solution.py:214
  50.4 4.4 %collective-permute-start.13 = (bf16[128,128]{1,0:T(8,128)(2,1)S(1)}, bf16[128,128]{1,0:T(8,128)(2,1)S(1)}, u32[]{:S(2)}, u32[]{:S(2)}) collective-permute-start(bf16[128,128]{1,0:T(8,128)(2,1)S(1)} %collective-permute-done.9.refs_1_), channel_id=1, source_target_pairs={{0,1},{1,0},{2,3},{3,2},{4,5},{5,4},{6,7},{7,6},{8,9},{9,8},{10,11... | collective-permute-start | bytes 98312 | tf_op jit(solution)/shard_map/ppermute | solution.py:214
  53.0 1.8 %collective-permute-start.14 = (bf16[128,128]{1,0:T(8,128)(2,1)S(1)}, bf16[128,128]{1,0:T(8,128)(2,1)S(1)}, u32[]{:S(2)}, u32[]{:S(2)}) collective-permute-start(bf16[128,128]{1,0:T(8,128)(2,1)S(1)} %collective-permute-done.10.refs_2_), channel_id=1, source_target_pairs={{0,1},{1,0},{2,3},{3,2},{4,5},{5,4},{6,7},{7,6},{8,9},{9,8},{10,11... | collective-permute-start | bytes 98312 | tf_op jit(solution)/shard_map/ppermute | solution.py:214
  54.8 1.2 %collective-permute-start.15 = (bf16[128,128]{1,0:T(8,128)(2,1)S(1)}, bf16[128,128]{1,0:T(8,128)(2,1)S(1)}, u32[]{:S(2)}, u32[]{:S(2)}) collective-permute-start(bf16[128,128]{1,0:T(8,128)(2,1)S(1)} %collective-permute-done.11.refs_3_), channel_id=1, source_target_pairs={{0,1},{1,0},{2,3},{3,2},{4,5},{5,4},{6,7},{7,6},{8,9},{9,8},{10,11... | collective-permute-start | bytes 98312 | tf_op jit(solution)/shard_map/ppermute | solution.py:214

commit v2 on v1

--- a/solution.py
+++ b/solution.py
@@ -15,14 +15,17 @@
 META = 16
 BASE = 128
 VMEM_LIMIT = 48 << 20
+PACK_LIMIT = 4 << 20
 LOG2E = 1.4426950408889634
 
 
 def project_kernel(tok_ref, pos_ref, cid_ref, wq_ref, wk_ref, wv_ref, *rest):
-    kv0_ref, q0_ref, m1_ref, m2_ref, m3_ref, wbuf, qkv, sems = rest
+    kv0_ref, q0_ref, m1_ref, m2_ref, m3_ref, rows, wbuf, qkv, sems, rows_sem = rest
     tok, cols = tok_ref.shape[0], wq_ref.shape[1]
     pair = cols // SPLIT
     half = cols // 2
+    rows_copy = pltpu.make_async_copy(tok_ref, rows, rows_sem)
+    rows_copy.start()
     copies = []
     for part, w_ref in enumerate((wq_ref, wk_ref, wv_ref)):
         for side in range(2):
@@ -32,11 +35,13 @@
             )
             copy.start()
             copies.append((part, side, copy))
-    rows = tok_ref[...]
+    rows_copy.wait()
     for part, side, copy in copies:
         copy.wait()
         result = jnp.dot(
-            rows, wbuf[part, :, side * half : (side + 1) * half], preferred_element_type=jnp.float32
+            rows[...],
+            wbuf[part, :, side * half : (side + 1) * half],
+            preferred_element_type=jnp.float32,
         )
         start = part * cols + side * half
         qkv[:, start : start + half] = result.astype(jnp.bfloat16)
@@ -65,7 +70,7 @@
     cols = w_query.shape[1]
     wide = 2 * cols // SPLIT
     vmem = pl.BlockSpec(memory_space=pltpu.VMEM)
-    hbm = pl.BlockSpec(memory_space=pl.ANY)
+    hbm = pl.BlockSpec(memory_space=pltpu.HBM)
     full = tok + META + tok // 2
 
     def shape(rows):
@@ -74,19 +79,42 @@
     return pl.pallas_call(
         project_kernel,
         out_shape=(shape(tok + META), shape(tok // 2), shape(full), shape(full), shape(full)),
-        in_specs=[vmem, vmem, vmem, hbm, hbm, hbm],
+        in_specs=[hbm, vmem, vmem, hbm, hbm, hbm],
         out_specs=(vmem,) * 5,
         scratch_shapes=[
+            pltpu.VMEM((tok, depth), jnp.bfloat16),
             pltpu.VMEM((3, depth, cols), jnp.bfloat16),
             pltpu.VMEM((tok, 3 * cols), jnp.bfloat16),
             pltpu.SemaphoreType.DMA((3, 2)),
+            pltpu.SemaphoreType.DMA(()),
         ],
-        compiler_params=pltpu.CompilerParams(vmem_limit_bytes=VMEM_LIMIT),
         cost_estimate=pl.CostEstimate(
             flops=6 * tok * depth * cols, bytes_accessed=6 * depth * cols, transcendentals=0
         ),
         name="project",
     )(tokens, positions.reshape(1, tok), cluster_ids, w_query, w_key, w_value)
+
+
+def pack_kernel(first_ref, second_ref, out_ref):
+    half = out_ref.shape[0] // 2
+    out_ref[:half, :] = first_ref[:half, :]
+    out_ref[half:, :] = second_ref[:half, :]
+
+
+def pack(first, second, block, flops):
+    vmem = pl.BlockSpec(memory_space=pltpu.VMEM)
+    wide = first.shape[1]
+    return pl.pallas_call(
+        pack_kernel,
+        out_shape=jax.ShapeDtypeStruct((2 * block, wide), jnp.bfloat16),
+        in_specs=[vmem, vmem],
+        out_specs=vmem,
+        compiler_params=pltpu.CompilerParams(vmem_limit_bytes=PACK_LIMIT),
+        cost_estimate=pl.CostEstimate(
+            flops=flops, bytes_accessed=8 * block * wide, transcendentals=0
+        ),
+        name="pack",
+    )(first, second)
 
 
 def attend_kernel(total, tok, *refs):
@@ -117,7 +145,7 @@
     key_codes = codes[0:1, :]
     scale = HD**-0.5 * LOG2E
     for item in range(SPLIT):
-        ref, base = (kv_refs[0], 0) if item == 0 else (kv_refs[1], (item - 1) * block)
+        ref, base = kv_refs[item // 2], (item % 2) * block
         code, pos = ids_of(ref, base)
         column[0:1, :] = code
         column[1:2, :] = pos
@@ -215,13 +243,16 @@
 
     w_other = swap(w_out)
     kv0, q0, m1, m2, m3 = project(tokens, positions, cluster_ids, w_query, w_key, w_value)
+    r1 = send(m1, PLANE)
     r2 = send(m2, 2 * PLANE)
     r3 = send(m3, 3 * PLANE)
-    r1 = send(m1, PLANE)
-    rest = jnp.concatenate([r1[:block], r2[:block], r3[:block]], axis=0)
-    sources = [kv0, rest]
-    for bits in (1, 2, 3):
-        sources += [send(kv0, bits), send(rest, bits)]
+    kv0, w_other = lax.optimization_barrier((kv0, w_other))
+    near = pack(kv0, r1, block, 0)
+    nears = [send(near, bits) for bits in (1, 2, 3)]
+    far = pack(r2, r3, block, 10**10)
+    far, *nears = lax.optimization_barrier((far, *nears))
+    fars = [send(far, bits) for bits in (1, 2, 3)]
+    sources = [near, far, *nears, *fars]
     a0, a1, a2, a3 = attend(owners * tok, tok, (q0, r1, r2, r3), sources)
     b2 = send(a2, 2 * PLANE)
     b3 = send(a3, 3 * PLANE)

time: 57.5 us -> 52.2 us (0.908)
  local copies, waits for them, and re-layouts: 6.43 us -> 0.89 us
  Pallas kernels: 9.22 us -> 12.2 us
  starting transfers between devices: 21.5 us -> 18.6 us
    unnamed x22 -> x6, local copies, waits for them, and re-layouts: 5.51 us -> 0.89 us
    pallas_call x1, Pallas kernels: 2.06 us -> 5.03 us  [project(): pl.pallas_call(project_kernel, out_shape=(shape(tok + META), shape(tok //...]
    ppermute x12, starting transfers between devices: 20.5 us -> 17.6 us  [send(): return lax.ppermute(array, 'seq', [(i, i ^ bits) for i in range(owners)])]
    slice x5 -> x0, local copies, waits for them, and re-layouts: 0.92 us -> none  [per_device_split(): rest = jnp.concatenate([r1[:block], r2[:block], r3[:block]], axis=0)]
  transfers between devices with their start and end apart: 17 -> 17, of which waited for: 6 -> 10; matrix products, arithmetic and copies ran while one was open for 0% -> 0% of each run, Pallas kernels for 14% -> 10%
where the time goes in v2:
time: 52.2 us; the launch traced here: 52 us
  waiting for transfers between devices  20.3 us (39%)
  starting transfers between devices  18.6 us (36%)
  Pallas kernels  12.2 us (23%)
  local copies, waits for them, and re-layouts  0.89 us (2%)
    ppermute x12, waiting for transfers between devices, send(): return lax.ppermute(array, 'seq', [(i, i ^ bits) for i in range(owners)])  19.1 us
    ppermute x12, starting transfers between devices, send(): return lax.ppermute(array, 'seq', [(i, i ^ bits) for i in range(owners)])  17.6 us
    pallas_call x1, Pallas kernels, attend(): pl.pallas_call(functools.partial(attend_kernel, total, tok), out_shape=(j...  6.01 us
    pallas_call x1, Pallas kernels, project(): pl.pallas_call(project_kernel, out_shape=(shape(tok + META), shape(tok //...  5.03 us
    ppermute x5, waiting for transfers between devices, swap(): return lax.ppermute(array, 'head', [(0, 1), (1, 0)])  1.2 us
    pallas_call x1, Pallas kernels, mix(): pl.pallas_call(mix_kernel, out_shape=jax.ShapeDtypeStruct((rows, width),...  1.14 us
  transfers between devices with their start and end apart: 17, of which 10 were waited for; matrix products, arithmetic and copies ran while one was open for 0% of the time, Pallas kernels for 10%

profile of v2, /device:TPU:0, one launch (start us, length us, event | category | flops | bytes accessed | tf_op | source)
XLA Modules:
  0.0 52.0 jit_solution(4375105375867596340)
XLA Ops:
  0.0 0.5 collective-permute-start.3
  0.5 5.0 %project.1 = (bf16[144,256]{1,0:T(8,128)(2,1)}, bf16[64,256]{1,0:T(8,128)(2,1)}, bf16[208,256]{1,0:T(8,128)(2,1)}, bf16[208,256]{1,0:T(8,128)(2,1)}, bf16[208,256]{1,0:T(8,128)(2,1)}) custom-call(bf16[128,1024]{1,0:T(8,128)(2,1)} %tok_ref.1, s32[1,128]{1,0:T(1,128)} %bitcast.1, s32[2,128]{1,0:T(2,128)} %cid_ref.1, bf16[1024,512]{1,0:T(8,128)(2,1)} %wq_ref.1, ...), custom_call_target="tpu_custom_call" | custom-call | flops 402653184 | bytes 3145728 | tf_op jit(solution)/shard_map/project/pallas_call | solution.py:79
  5.5 2.6 %collective-permute-start = (bf16[208,256]{1,0:T(8,128)(2,1)}, bf16[208,256]{1,0:T(8,128)(2,1)S(1)}, u32[]{:S(2)}, u32[]{:S(2)}) collective-permute-start(bf16[208,256]{1,0:T(8,128)(2,1)} %get-tuple-element.21), channel_id=1, source_target_pairs={{0,8},{2,10},{4,12},{6,14},{8,0},{10,2},{12,4},{14,6},{16,24},{18,... | collective-permute-start | bytes 319496 | tf_op jit(solution)/shard_map/ppermute | solution.py:239
  8.1 2.6 %collective-permute-start.1 = (bf16[208,256]{1,0:T(8,128)(2,1)}, bf16[208,256]{1,0:T(8,128)(2,1)S(1)}, u32[]{:S(2)}, u32[]{:S(2)}) collective-permute-start(bf16[208,256]{1,0:T(8,128)(2,1)} %get-tuple-element.22), channel_id=1, source_target_pairs={{0,16},{2,18},{4,20},{6,22},{8,24},{10,26},{12,28},{14,30},{16,0},... | collective-permute-start | bytes 319496 | tf_op jit(solution)/shard_map/ppermute | solution.py:239
  10.7 0.0 collective-permute-start.2
  10.7 0.0 collective-permute-done.3.refs_9_
  10.7 1.3 %collective-permute-done.second_ref.refs_1_ = bf16[208,256]{1,0:T(8,128)(2,1)S(1)} collective-permute-done((bf16[208,256]{1,0:T(8,128)(2,1)}, bf16[208,256]{1,0:T(8,128)(2,1)S(1)}, u32[]{:S(2)}, u32[]{:S(2)}) %collective-permute-start) | collective-permute-done | bytes 106528 | tf_op jit(solution)/shard_map/ppermute | solution.py:239
  12.0 0.0 copy-start.1
  12.0 0.9 %copy-done.1 = bf16[144,256]{1,0:T(8,128)(2,1)S(1)} copy-done((bf16[144,256]{1,0:T(8,128)(2,1)S(1)}, bf16[144,256]{1,0:T(8,128)(2,1)}, u32[]{:S(2)}) %copy-start.1) | copy-done | bytes 73752
  12.9 0.0 copy-start.2
  12.9 2.7 %collective-permute-start.6 = (bf16[288,256]{1,0:T(8,128)(2,1)S(1)}, bf16[288,256]{1,0:T(8,128)(2,1)S(1)}, u32[]{:S(2)}, u32[]{:S(2)}) collective-permute-start(bf16[288,256]{1,0:T(8,128)(2,1)S(1)} %pack.2.refs_4_), channel_id=1, source_target_pairs={{0,6},{2,4},{4,2},{6,0},{8,14},{10,12},{12,10},{14,8},{16,22},{18,... | collective-permute-start | bytes 442376 | tf_op jit(solution)/shard_map/ppermute | solution.py:239
  15.6 0.5 collective-permute-start.5
  16.1 0.4 collective-permute-start.4
  16.4 3.2 %collective-permute-done.1.first_ref.refs_2_ = bf16[208,256]{1,0:T(8,128)(2,1)S(1)} collective-permute-done((bf16[208,256]{1,0:T(8,128)(2,1)}, bf16[208,256]{1,0:T(8,128)(2,1)S(1)}, u32[]{:S(2)}, u32[]{:S(2)}) %collective-permute-start.1) | collective-permute-done | bytes 106528 | tf_op jit(solution)/shard_map/ppermute | solution.py:239
  19.6 0.0 collective-permute-done.2.second_ref.refs_3_
  19.6 0.6 %collective-permute-done.6.refs_8_ = bf16[288,256]{1,0:T(8,128)(2,1)S(1)} collective-permute-done((bf16[288,256]{1,0:T(8,128)(2,1)S(1)}, bf16[288,256]{1,0:T(8,128)(2,1)S(1)}, u32[]{:S(2)}, u32[]{:S(2)}) %collective-permute-start.6) | collective-permute-done | bytes 147488 | tf_op jit(solution)/shard_map/ppermute | solution.py:239
  20.2 2.5 %collective-permute-done.5.refs_7_ = bf16[288,256]{1,0:T(8,128)(2,1)S(1)} collective-permute-done((bf16[288,256]{1,0:T(8,128)(2,1)S(1)}, bf16[288,256]{1,0:T(8,128)(2,1)S(1)}, u32[]{:S(2)}, u32[]{:S(2)}) %collective-permute-start.5) | collective-permute-done | bytes 147488 | tf_op jit(solution)/shard_map/ppermute | solution.py:239
  22.7 0.0 collective-permute-done.4.refs_6_
  22.7 1.7 %collective-permute-start.9 = (bf16[288,256]{1,0:T(8,128)(2,1)S(1)}, bf16[288,256]{1,0:T(8,128)(2,1)S(1)}, u32[]{:S(2)}, u32[]{:S(2)}) collective-permute-start(bf16[288,256]{1,0:T(8,128)(2,1)S(1)} %pack.3.refs_5_), channel_id=1, source_target_pairs={{0,6},{2,4},{4,2},{6,0},{8,14},{10,12},{12,10},{14,8},{16,22},{18,... | collective-permute-start | bytes 442376 | tf_op jit(solution)/shard_map/ppermute | solution.py:239
  24.4 1.3 %collective-permute-start.8 = (bf16[288,256]{1,0:T(8,128)(2,1)S(1)}, bf16[288,256]{1,0:T(8,128)(2,1)S(1)}, u32[]{:S(2)}, u32[]{:S(2)}) collective-permute-start(bf16[288,256]{1,0:T(8,128)(2,1)S(1)} %pack.3.refs_5_), channel_id=1, source_target_pairs={{0,4},{2,6},{4,0},{6,2},{8,12},{10,14},{12,8},{14,10},{16,20},{18,... | collective-permute-start | bytes 442376 | tf_op jit(solution)/shard_map/ppermute | solution.py:239
  25.7 0.5 collective-permute-start.7
  26.2 4.2 %collective-permute-done.9.refs_11_ = bf16[288,256]{1,0:T(8,128)(2,1)S(1)} collective-permute-done((bf16[288,256]{1,0:T(8,128)(2,1)S(1)}, bf16[288,256]{1,0:T(8,128)(2,1)S(1)}, u32[]{:S(2)}, u32[]{:S(2)}) %collective-permute-start.9) | collective-permute-done | bytes 147488 | tf_op jit(solution)/shard_map/ppermute | solution.py:239
  30.4 2.1 %collective-permute-done.8.refs_10_ = bf16[288,256]{1,0:T(8,128)(2,1)S(1)} collective-permute-done((bf16[288,256]{1,0:T(8,128)(2,1)S(1)}, bf16[288,256]{1,0:T(8,128)(2,1)S(1)}, u32[]{:S(2)}, u32[]{:S(2)}) %collective-permute-start.8) | collective-permute-done | bytes 147488 | tf_op jit(solution)/shard_map/ppermute | solution.py:239
  32.5 0.1 collective-permute-done.7.refs_9_
  32.6 0.0 copy-done.2
  32.6 0.0 copy-start
  32.6 6.0 %attend.1 = (bf16[128,128]{1,0:T(8,128)(2,1)S(1)}, bf16[128,128]{1,0:T(8,128)(2,1)S(1)}, bf16[128,128]{1,0:T(8,128)(2,1)S(1)}, bf16[128,128]{1,0:T(8,128)(2,1)S(1)}) custom-call(bf16[64,256]{1,0:T(8,128)(2,1)S(1)} %copy-done.2, bf16[208,256]{1,0:T(8,128)(2,1)S(1)} %collective-permute-done.second_ref.refs_1_, ...), custom_call_target="tpu_custom_call" | custom-call | flops 1073741824 | bytes 1048576 | tf_op jit(solution)/shard_map/attend/pallas_call | solution.py:179
  38.6 1.6 %collective-permute-start.10 = (bf16[128,128]{1,0:T(8,128)(2,1)S(1)}, bf16[128,128]{1,0:T(8,128)(2,1)S(1)}, u32[]{:S(2)}, u32[]{:S(2)}) collective-permute-start(bf16[128,128]{1,0:T(8,128)(2,1)S(1)} %get-tuple-element.31), channel_id=1, source_target_pairs={{0,8},{2,10},{4,12},{6,14},{8,0},{10,2},{12,4},{14,6},{16,24},{18,... | collective-permute-start | bytes 98312 | tf_op jit(solution)/shard_map/ppermute | solution.py:239
  40.3 3.7 %collective-permute-start.11 = (bf16[128,128]{1,0:T(8,128)(2,1)S(1)}, bf16[128,128]{1,0:T(8,128)(2,1)S(1)}, u32[]{:S(2)}, u32[]{:S(2)}) collective-permute-start(bf16[128,128]{1,0:T(8,128)(2,1)S(1)} %get-tuple-element.32), channel_id=1, source_target_pairs={{0,16},{2,18},{4,20},{6,22},{8,24},{10,26},{12,28},{14,30},{16,0},... | collective-permute-start | bytes 98312 | tf_op jit(solution)/shard_map/ppermute | solution.py:239
  43.9 0.0 collective-permute-start.12
  44.0 0.0 collective-permute-start.13
  44.0 0.0 collective-permute-done.10.refs_1_
  44.0 0.5 collective-permute-start.14
  44.5 1.9 %collective-permute-done.11.refs_2_ = bf16[128,128]{1,0:T(8,128)(2,1)S(1)} collective-permute-done((bf16[128,128]{1,0:T(8,128)(2,1)S(1)}, bf16[128,128]{1,0:T(8,128)(2,1)S(1)}, u32[]{:S(2)}, u32[]{:S(2)}) %collective-permute-start.11) | collective-permute-done | bytes 32800 | tf_op jit(solution)/shard_map/ppermute | solution.py:239
  46.3 0.0 collective-permute-start.15
  46.3 3.3 %collective-permute-done.12.refs_3_ = bf16[128,128]{1,0:T(8,128)(2,1)S(1)} collective-permute-done((bf16[128,128]{1,0:T(8,128)(2,1)S(1)}, bf16[128,128]{1,0:T(8,128)(2,1)S(1)}, u32[]{:S(2)}, u32[]{:S(2)}) %collective-permute-start.12) | collective-permute-done | bytes 32800 | tf_op jit(solution)/shard_map/ppermute | solution.py:239
  49.7 0.0 collective-permute-start.16
  49.7 0.0 collective-permute-done.13.refs_4_
  49.7 0.0 collective-permute-done.14.refs_5_
  49.7 0.0 collective-permute-done.15.refs_6_
  49.7 1.2 %collective-permute-done.16.refs_7_ = bf16[128,128]{1,0:T(8,128)(2,1)S(1)} collective-permute-done((bf16[128,128]{1,0:T(8,128)(2,1)S(1)}, bf16[128,128]{1,0:T(8,128)(2,1)S(1)}, u32[]{:S(2)}, u32[]{:S(2)}) %collective-permute-start.16) | collective-permute-done | bytes 32800 | tf_op jit(solution)/shard_map/ppermute | solution.py:242
  50.9 0.0 copy-done
  50.9 1.1 %mix.1 = bf16[64,1024]{1,0:T(8,128)(2,1)} custom-call(bf16[128,128]{1,0:T(8,128)(2,1)S(1)} %get-tuple-element.30.refs_0_, bf16[128,128]{1,0:T(8,128)(2,1)S(1)} %collective-permute-done.10.refs_1_, bf16[128,128]{1,0:T(8,128)(2,1)S(1)} %collective-permute-done.11.refs_2_, bf16[128,128]{1,0:T(8,128)(2,1)S(1)} %collective-permute-done.12.refs_3_, ...), custom_call_target="tpu_custom_call" | custom-call | flops 134217728 | bytes 2097152 | tf_op jit(solution)/shard_map/mix/pallas_call | solution.py:219
  (2 shorter events, 0.0 us)
Async XLA Ops:
  0.0 10.7 %collective-permute-start.3 = (bf16[512,1024]{1,0:T(8,128)(2,1)}, bf16[512,1024]{1,0:T(8,128)(2,1)S(1)}, u32[]{:S(2)}, u32[]{:S(2)}) collective-permute-start(bf16[512,1024]{1,0:T(8,128)(2,1)} %refs_8_.1), channel_id=1, source_target_pairs={{0,1},{1,0},{2,3},{3,2},{4,5},{5,4},{6,7},{7,6},{8,9},{9,8},{10,11... | collective-permute-start | bytes 3145736 | tf_op jit(solution)/shard_map/ppermute | solution.py:242
  5.5 6.5 %collective-permute-start = (bf16[208,256]{1,0:T(8,128)(2,1)}, bf16[208,256]{1,0:T(8,128)(2,1)S(1)}, u32[]{:S(2)}, u32[]{:S(2)}) collective-permute-start(bf16[208,256]{1,0:T(8,128)(2,1)} %get-tuple-element.21), channel_id=1, source_target_pairs={{0,8},{2,10},{4,12},{6,14},{8,0},{10,2},{12,4},{14,6},{16,24},{18,... | collective-permute-start | bytes 319496 | tf_op jit(solution)/shard_map/ppermute | solution.py:239
  8.1 11.5 %collective-permute-start.1 = (bf16[208,256]{1,0:T(8,128)(2,1)}, bf16[208,256]{1,0:T(8,128)(2,1)S(1)}, u32[]{:S(2)}, u32[]{:S(2)}) collective-permute-start(bf16[208,256]{1,0:T(8,128)(2,1)} %get-tuple-element.22), channel_id=1, source_target_pairs={{0,16},{2,18},{4,20},{6,22},{8,24},{10,26},{12,28},{14,30},{16,0},... | collective-permute-start | bytes 319496 | tf_op jit(solution)/shard_map/ppermute | solution.py:239
  10.7 8.9 %collective-permute-start.2 = (bf16[208,256]{1,0:T(8,128)(2,1)}, bf16[208,256]{1,0:T(8,128)(2,1)S(1)}, u32[]{:S(2)}, u32[]{:S(2)}) collective-permute-start(bf16[208,256]{1,0:T(8,128)(2,1)} %get-tuple-element.23), channel_id=1, source_target_pairs={{0,24},{2,26},{4,28},{6,30},{8,16},{10,18},{12,20},{14,22},{16,8},... | collective-permute-start | bytes 319496 | tf_op jit(solution)/shard_map/ppermute | solution.py:239
  12.0 0.9 %copy-start.1 = (bf16[144,256]{1,0:T(8,128)(2,1)S(1)}, bf16[144,256]{1,0:T(8,128)(2,1)}, u32[]{:S(2)}) copy-start(bf16[144,256]{1,0:T(8,128)(2,1)} %get-tuple-element.25.first_ref) | copy-start | bytes 221188
  12.9 19.7 %copy-start.2 = (bf16[64,256]{1,0:T(8,128)(2,1)S(1)}, bf16[64,256]{1,0:T(8,128)(2,1)}, u32[]{:S(2)}) copy-start(bf16[64,256]{1,0:T(8,128)(2,1)} %get-tuple-element.20.refs_0_) | copy-start | bytes 98308
  12.9 7.3 %collective-permute-start.6 = (bf16[288,256]{1,0:T(8,128)(2,1)S(1)}, bf16[288,256]{1,0:T(8,128)(2,1)S(1)}, u32[]{:S(2)}, u32[]{:S(2)}) collective-permute-start(bf16[288,256]{1,0:T(8,128)(2,1)S(1)} %pack.2.refs_4_), channel_id=1, source_target_pairs={{0,6},{2,4},{4,2},{6,0},{8,14},{10,12},{12,10},{14,8},{16,22},{18,... | collective-permute-start | bytes 442376 | tf_op jit(solution)/shard_map/ppermute | solution.py:239
  15.6 7.1 %collective-permute-start.5 = (bf16[288,256]{1,0:T(8,128)(2,1)S(1)}, bf16[288,256]{1,0:T(8,128)(2,1)S(1)}, u32[]{:S(2)}, u32[]{:S(2)}) collective-permute-start(bf16[288,256]{1,0:T(8,128)(2,1)S(1)} %pack.2.refs_4_), channel_id=1, source_target_pairs={{0,4},{2,6},{4,0},{6,2},{8,12},{10,14},{12,8},{14,10},{16,20},{18,... | collective-permute-start | bytes 442376 | tf_op jit(solution)/shard_map/ppermute | solution.py:239
  16.1 6.6 %collective-permute-start.4 = (bf16[288,256]{1,0:T(8,128)(2,1)S(1)}, bf16[288,256]{1,0:T(8,128)(2,1)S(1)}, u32[]{:S(2)}, u32[]{:S(2)}) collective-permute-start(bf16[288,256]{1,0:T(8,128)(2,1)S(1)} %pack.2.refs_4_), channel_id=1, source_target_pairs={{0,2},{2,0},{4,6},{6,4},{8,10},{10,8},{12,14},{14,12},{16,18},{18,... | collective-permute-start | bytes 442376 | tf_op jit(solution)/shard_map/ppermute | solution.py:239
  22.7 7.7 %collective-permute-start.9 = (bf16[288,256]{1,0:T(8,128)(2,1)S(1)}, bf16[288,256]{1,0:T(8,128)(2,1)S(1)}, u32[]{:S(2)}, u32[]{:S(2)}) collective-permute-start(bf16[288,256]{1,0:T(8,128)(2,1)S(1)} %pack.3.refs_5_), channel_id=1, source_target_pairs={{0,6},{2,4},{4,2},{6,0},{8,14},{10,12},{12,10},{14,8},{16,22},{18,... | collective-permute-start | bytes 442376 | tf_op jit(solution)/shard_map/ppermute | solution.py:239
  24.4 8.0 %collective-permute-start.8 = (bf16[288,256]{1,0:T(8,128)(2,1)S(1)}, bf16[288,256]{1,0:T(8,128)(2,1)S(1)}, u32[]{:S(2)}, u32[]{:S(2)}) collective-permute-start(bf16[288,256]{1,0:T(8,128)(2,1)S(1)} %pack.3.refs_5_), channel_id=1, source_target_pairs={{0,4},{2,6},{4,0},{6,2},{8,12},{10,14},{12,8},{14,10},{16,20},{18,... | collective-permute-start | bytes 442376 | tf_op jit(solution)/shard_map/ppermute | solution.py:239
  25.7 6.9 %collective-permute-start.7 = (bf16[288,256]{1,0:T(8,128)(2,1)S(1)}, bf16[288,256]{1,0:T(8,128)(2,1)S(1)}, u32[]{:S(2)}, u32[]{:S(2)}) collective-permute-start(bf16[288,256]{1,0:T(8,128)(2,1)S(1)} %pack.3.refs_5_), channel_id=1, source_target_pairs={{0,2},{2,0},{4,6},{6,4},{8,10},{10,8},{12,14},{14,12},{16,18},{18,... | collective-permute-start | bytes 442376 | tf_op jit(solution)/shard_map/ppermute | solution.py:239
  32.6 18.3 %copy-start = (bf16[512,1024]{1,0:T(8,128)(2,1)S(1)}, bf16[512,1024]{1,0:T(8,128)(2,1)}, u32[]{:S(2)}) copy-start(bf16[512,1024]{1,0:T(8,128)(2,1)} %refs_8_.1) | copy-start | bytes 3145732
  38.6 5.3 %collective-permute-start.10 = (bf16[128,128]{1,0:T(8,128)(2,1)S(1)}, bf16[128,128]{1,0:T(8,128)(2,1)S(1)}, u32[]{:S(2)}, u32[]{:S(2)}) collective-permute-start(bf16[128,128]{1,0:T(8,128)(2,1)S(1)} %get-tuple-element.31), channel_id=1, source_target_pairs={{0,8},{2,10},{4,12},{6,14},{8,0},{10,2},{12,4},{14,6},{16,24},{18,... | collective-permute-start | bytes 98312 | tf_op jit(solution)/shard_map/ppermute | solution.py:239
  40.3 6.1 %collective-permute-start.11 = (bf16[128,128]{1,0:T(8,128)(2,1)S(1)}, bf16[128,128]{1,0:T(8,128)(2,1)S(1)}, u32[]{:S(2)}, u32[]{:S(2)}) collective-permute-start(bf16[128,128]{1,0:T(8,128)(2,1)S(1)} %get-tuple-element.32), channel_id=1, source_target_pairs={{0,16},{2,18},{4,20},{6,22},{8,24},{10,26},{12,28},{14,30},{16,0},... | collective-permute-start | bytes 98312 | tf_op jit(solution)/shard_map/ppermute | solution.py:239
  43.9 5.7 %collective-permute-start.12 = (bf16[128,128]{1,0:T(8,128)(2,1)S(1)}, bf16[128,128]{1,0:T(8,128)(2,1)S(1)}, u32[]{:S(2)}, u32[]{:S(2)}) collective-permute-start(bf16[128,128]{1,0:T(8,128)(2,1)S(1)} %get-tuple-element.33), channel_id=1, source_target_pairs={{0,24},{2,26},{4,28},{6,30},{8,16},{10,18},{12,20},{14,22},{16,8},... | collective-permute-start | bytes 98312 | tf_op jit(solution)/shard_map/ppermute | solution.py:239
  44.0 5.7 %collective-permute-start.13 = (bf16[128,128]{1,0:T(8,128)(2,1)S(1)}, bf16[128,128]{1,0:T(8,128)(2,1)S(1)}, u32[]{:S(2)}, u32[]{:S(2)}) collective-permute-start(bf16[128,128]{1,0:T(8,128)(2,1)S(1)} %get-tuple-element.30.refs_0_), channel_id=1, source_target_pairs={{0,1},{1,0},{2,3},{3,2},{4,5},{5,4},{6,7},{7,6},{8,9},{9,8},{10,11... | collective-permute-start | bytes 98312 | tf_op jit(solution)/shard_map/ppermute | solution.py:242
  44.0 5.7 %collective-permute-start.14 = (bf16[128,128]{1,0:T(8,128)(2,1)S(1)}, bf16[128,128]{1,0:T(8,128)(2,1)S(1)}, u32[]{:S(2)}, u32[]{:S(2)}) collective-permute-start(bf16[128,128]{1,0:T(8,128)(2,1)S(1)} %collective-permute-done.10.refs_1_), channel_id=1, source_target_pairs={{0,1},{1,0},{2,3},{3,2},{4,5},{5,4},{6,7},{7,6},{8,9},{9,8},{10,11... | collective-permute-start | bytes 98312 | tf_op jit(solution)/shard_map/ppermute | solution.py:242
  46.3 3.4 %collective-permute-start.15 = (bf16[128,128]{1,0:T(8,128)(2,1)S(1)}, bf16[128,128]{1,0:T(8,128)(2,1)S(1)}, u32[]{:S(2)}, u32[]{:S(2)}) collective-permute-start(bf16[128,128]{1,0:T(8,128)(2,1)S(1)} %collective-permute-done.11.refs_2_), channel_id=1, source_target_pairs={{0,1},{1,0},{2,3},{3,2},{4,5},{5,4},{6,7},{7,6},{8,9},{9,8},{10,11... | collective-permute-start | bytes 98312 | tf_op jit(solution)/shard_map/ppermute | solution.py:242
  49.7 1.2 %collective-permute-start.16 = (bf16[128,128]{1,0:T(8,128)(2,1)S(1)}, bf16[128,128]{1,0:T(8,128)(2,1)S(1)}, u32[]{:S(2)}, u32[]{:S(2)}) collective-permute-start(bf16[128,128]{1,0:T(8,128)(2,1)S(1)} %collective-permute-done.12.refs_3_), channel_id=1, source_target_pairs={{0,1},{1,0},{2,3},{3,2},{4,5},{5,4},{6,7},{7,6},{8,9},{9,8},{10,11... | collective-permute-start | bytes 98312 | tf_op jit(solution)/shard_map/ppermute | solution.py:242

commit v3 on v2

--- a/solution.py
+++ b/solution.py
@@ -14,8 +14,10 @@
 PLANE = 4
 META = 16
 BASE = 128
-VMEM_LIMIT = 48 << 20
 PACK_LIMIT = 4 << 20
+ATTEND_LIMIT = 16 << 20
+EARLY_FLOPS = 8 * 10**9
+LATE_FLOPS = (3 * 10**9,) * SPLIT
 LOG2E = 1.4426950408889634
 
 
@@ -23,28 +25,18 @@
     kv0_ref, q0_ref, m1_ref, m2_ref, m3_ref, rows, wbuf, qkv, sems, rows_sem = rest
     tok, cols = tok_ref.shape[0], wq_ref.shape[1]
     pair = cols // SPLIT
-    half = cols // 2
     rows_copy = pltpu.make_async_copy(tok_ref, rows, rows_sem)
     rows_copy.start()
     copies = []
     for part, w_ref in enumerate((wq_ref, wk_ref, wv_ref)):
-        for side in range(2):
-            lanes = pl.ds(side * half, half)
-            copy = pltpu.make_async_copy(
-                w_ref.at[:, lanes], wbuf.at[part, :, lanes], sems.at[part, side]
-            )
-            copy.start()
-            copies.append((part, side, copy))
+        copy = pltpu.make_async_copy(w_ref, wbuf.at[part], sems.at[part])
+        copy.start()
+        copies.append(copy)
     rows_copy.wait()
-    for part, side, copy in copies:
+    for part, copy in enumerate(copies):
         copy.wait()
-        result = jnp.dot(
-            rows[...],
-            wbuf[part, :, side * half : (side + 1) * half],
-            preferred_element_type=jnp.float32,
-        )
-        start = part * cols + side * half
-        qkv[:, start : start + half] = result.astype(jnp.bfloat16)
+        result = jnp.dot(rows[...], wbuf[part], preferred_element_type=jnp.float32)
+        qkv[:, part * cols : (part + 1) * cols] = result.astype(jnp.bfloat16)
     high_digit = jnp.broadcast_to(pos_ref[...] // BASE, (META, tok))
     low_digit = jnp.broadcast_to(pos_ref[...] % BASE, (META, tok))
     first = lax.broadcasted_iota(jnp.int32, (META, tok), 0) == 0
@@ -85,7 +77,7 @@
             pltpu.VMEM((tok, depth), jnp.bfloat16),
             pltpu.VMEM((3, depth, cols), jnp.bfloat16),
             pltpu.VMEM((tok, 3 * cols), jnp.bfloat16),
-            pltpu.SemaphoreType.DMA((3, 2)),
+            pltpu.SemaphoreType.DMA((3,)),
             pltpu.SemaphoreType.DMA(()),
         ],
         cost_estimate=pl.CostEstimate(
@@ -117,84 +109,139 @@
     )(first, second)
 
 
-def attend_kernel(total, tok, *refs):
-    q_refs = refs[:SPLIT]
-    kv_refs = refs[SPLIT : SPLIT + 2 * PLANE]
-    out_refs = refs[SPLIT + 2 * PLANE : SPLIT + 2 * PLANE + SPLIT]
-    keys, values, codes, column = refs[SPLIT + 2 * PLANE + SPLIT :]
+def ids_of(ref, base, tok, total):
+    pair = ref.shape[1] // 2
+    cid = ref[base + tok : base + tok + 1, :pair].astype(jnp.float32)
+    low = ref[base + tok + 1 : base + tok + 2, :pair].astype(jnp.float32)
+    high = ref[base + tok : base + tok + 1, pair:].astype(jnp.float32)
+    pos = high * float(BASE) + low
+    return cid * float(2 * total) + pos, pos
+
+
+def unpack(refs, tok, total, keys, values, codes):
     pair = keys.shape[1]
     block = tok + META
-    stride = 2 * total
-
-    def ids_of(ref, base):
-        cid = ref[base + tok : base + tok + 1, :pair].astype(jnp.float32)
-        low = ref[base + tok + 1 : base + tok + 2, :pair].astype(jnp.float32)
-        high = ref[base + tok : base + tok + 1, pair:].astype(jnp.float32)
-        pos = high * float(BASE) + low
-        return cid * float(stride) + pos, pos
-
     at = 0
-    for ref in kv_refs:
-        for item in range(ref.shape[0] // block):
-            base = item * block
+    for ref in refs:
+        for base in range(0, ref.shape[0], block):
             keys[at : at + tok, :] = ref[base : base + tok, :pair]
             values[at : at + tok, :] = ref[base : base + tok, pair:]
-            codes[0:1, at : at + tok] = ids_of(ref, base)[0]
+            codes[0:1, at : at + tok] = ids_of(ref, base, tok, total)[0]
             at += tok
+
+
+def scores_of(q_ref, ids_ref, base, tok, total, keys, codes, column):
+    pair = keys.shape[1]
+    code, pos = ids_of(ids_ref, base, tok, total)
+    column[0:1, :] = code
+    column[1:2, :] = pos
+    turned = jnp.transpose(column[...])
+    gap = turned[:, 0:1] - codes[0:1, :]
+    allowed = (gap >= 0.0) & (gap <= turned[:, 1:2])
+    bias = jnp.where(allowed, 0.0, -1e30)
+    start = q_ref.shape[0] - tok // 2
+    query = jnp.concatenate([q_ref[start:, :pair], q_ref[start:, pair:]], axis=0)
     lane = lax.broadcasted_iota(jnp.int32, (tok, pair), 1) < HD
-    key_codes = codes[0:1, :]
-    scale = HD**-0.5 * LOG2E
+    none = jnp.zeros_like(query)
+    both = jnp.concatenate([jnp.where(lane, query, none), jnp.where(lane, none, query)], axis=0)
+    scores = lax.dot_general(
+        both, keys[...], (((1,), (1,)), ((), ())), preferred_element_type=jnp.float32
+    )
+    return scores * (HD**-0.5 * LOG2E) + jnp.concatenate([bias, bias], axis=0)
+
+
+def early_kernel(total, tok, count, *refs):
+    q_refs = refs[:SPLIT]
+    kv_refs = refs[SPLIT : SPLIT + count]
+    expo_ref, stats_ref, values, keys, codes, column = refs[SPLIT + count :]
+    unpack(kv_refs, tok, total, keys, values, codes)
+    block = tok + META
     for item in range(SPLIT):
-        ref, base = kv_refs[item // 2], (item % 2) * block
-        code, pos = ids_of(ref, base)
-        column[0:1, :] = code
-        column[1:2, :] = pos
-        turned = jnp.transpose(column[...])
-        gap = turned[:, 0:1] - key_codes
-        allowed = (gap >= 0.0) & (gap <= turned[:, 1:2])
-        bias = jnp.where(allowed, 0.0, -1e30)
-        q_ref = q_refs[item]
-        start = q_ref.shape[0] - tok // 2
-        query = jnp.concatenate([q_ref[start:, :pair], q_ref[start:, pair:]], axis=0)
-        results = []
-        for head in range(2):
-            own = jnp.where(lane if head == 0 else jnp.logical_not(lane), query, jnp.zeros_like(query))
-            scores = lax.dot_general(
-                own, keys[...], (((1,), (1,)), ((), ())), preferred_element_type=jnp.float32
-            )
-            scores = scores * scale + bias
-            top = jnp.max(scores, axis=1, keepdims=True)
-            expo = jnp.exp2(scores - top)
-            weights = expo * (1.0 / jnp.sum(expo, axis=1, keepdims=True))
-            results.append(
-                jnp.dot(weights.astype(jnp.bfloat16), values[...], preferred_element_type=jnp.float32)
-            )
-        out_refs[item][...] = jnp.where(lane, results[0], results[1]).astype(jnp.bfloat16)
-
-
-def attend(total, tok, queries, sources):
-    pair = sources[0].shape[1] // 2
+        scores = scores_of(
+            q_refs[item], kv_refs[item // 2], (item % 2) * block, tok, total, keys, codes, column
+        )
+        top = jnp.max(scores, axis=1, keepdims=True)
+        expo = jnp.exp2(scores - top)
+        rows = slice(item * 2 * tok, (item + 1) * 2 * tok)
+        expo_ref[rows, :] = expo
+        stats_ref[rows, 0:1] = top
+        stats_ref[rows, 1:2] = jnp.sum(expo, axis=1, keepdims=True)
+
+
+def early(total, tok, queries, sources):
+    wide = sources[0].shape[1]
+    pair = wide // 2
     vmem = pl.BlockSpec(memory_space=pltpu.VMEM)
-    count = SPLIT * PLANE * tok
+    count = sum(item.shape[0] for item in sources) // (tok + META) * tok
+    rows = 2 * SPLIT * tok
     return pl.pallas_call(
-        functools.partial(attend_kernel, total, tok),
-        out_shape=(jax.ShapeDtypeStruct((tok, pair), jnp.bfloat16),) * SPLIT,
+        functools.partial(early_kernel, total, tok, len(sources)),
+        out_shape=(
+            jax.ShapeDtypeStruct((rows, count), jnp.float32),
+            jax.ShapeDtypeStruct((rows, pair), jnp.float32),
+            jax.ShapeDtypeStruct((count, pair), jnp.bfloat16),
+        ),
         in_specs=[vmem] * (len(queries) + len(sources)),
-        out_specs=(vmem,) * SPLIT,
+        out_specs=(vmem,) * 3,
+        scratch_shapes=[
+            pltpu.VMEM((count, pair), jnp.bfloat16),
+            pltpu.VMEM((8, count), jnp.float32),
+            pltpu.VMEM((8, tok), jnp.float32),
+        ],
+        compiler_params=pltpu.CompilerParams(vmem_limit_bytes=ATTEND_LIMIT),
+        cost_estimate=pl.CostEstimate(
+            flops=EARLY_FLOPS, bytes_accessed=8 * count * pair, transcendentals=rows * count
+        ),
+        name="early",
+    )(*queries, *sources)
+
+
+def late_kernel(total, tok, item, count, *refs):
+    q_ref, ids_ref, expo_ref, stats_ref, old_values = refs[:5]
+    kv_refs = refs[5 : 5 + count]
+    out_ref, keys, values, codes, column = refs[5 + count :]
+    unpack(kv_refs, tok, total, keys, values, codes)
+    pair = keys.shape[1]
+    scores = scores_of(q_ref, ids_ref, (item % 2) * (tok + META), tok, total, keys, codes, column)
+    rows = slice(item * 2 * tok, (item + 1) * 2 * tok)
+    old_top = stats_ref[rows, 0:1]
+    top = jnp.maximum(jnp.max(scores, axis=1, keepdims=True), old_top)
+    expo = jnp.exp2(scores - top)
+    factor = jnp.exp2(old_top - top)
+    inverse = 1.0 / (jnp.sum(expo, axis=1, keepdims=True) + stats_ref[rows, 1:2] * factor)
+    result = jnp.dot(
+        (expo_ref[rows, :] * (factor * inverse)).astype(jnp.bfloat16),
+        old_values[...],
+        preferred_element_type=jnp.float32,
+    )
+    result += jnp.dot(
+        (expo * inverse).astype(jnp.bfloat16), values[...], preferred_element_type=jnp.float32
+    )
+    lane = lax.broadcasted_iota(jnp.int32, (tok, pair), 1) < HD
+    out_ref[...] = jnp.where(lane, result[:tok], result[tok:]).astype(jnp.bfloat16)
+
+
+def late(total, tok, item, query, ids, expo, stats, old_values, sources):
+    pair = old_values.shape[1]
+    vmem = pl.BlockSpec(memory_space=pltpu.VMEM)
+    count = sum(part.shape[0] for part in sources) // (tok + META) * tok
+    return pl.pallas_call(
+        functools.partial(late_kernel, total, tok, item, len(sources)),
+        out_shape=jax.ShapeDtypeStruct((tok, pair), jnp.bfloat16),
+        in_specs=[vmem] * (5 + len(sources)),
+        out_specs=vmem,
         scratch_shapes=[
             pltpu.VMEM((count, pair), jnp.bfloat16),
             pltpu.VMEM((count, pair), jnp.bfloat16),
             pltpu.VMEM((8, count), jnp.float32),
             pltpu.VMEM((8, tok), jnp.float32),
         ],
-        compiler_params=pltpu.CompilerParams(vmem_limit_bytes=VMEM_LIMIT),
+        compiler_params=pltpu.CompilerParams(vmem_limit_bytes=ATTEND_LIMIT),
         cost_estimate=pl.CostEstimate(
-            flops=8 * SPLIT * tok * count * pair,
-            bytes_accessed=4 * count * pair,
-            transcendentals=2 * SPLIT * tok * count,
-        ),
-        name="attend",
-    )(*queries, *sources)
+            flops=LATE_FLOPS[item], bytes_accessed=4 * count * pair, transcendentals=2 * tok * count
+        ),
+        name="late",
+    )(query, ids, expo, stats, old_values, *sources)
 
 
 def mix_kernel(*refs):
@@ -222,7 +269,7 @@
         in_specs=[vmem] * (2 * SPLIT + 2),
         out_specs=vmem,
         scratch_shapes=[pltpu.VMEM((rows, deep), jnp.bfloat16)] * 2,
-        compiler_params=pltpu.CompilerParams(vmem_limit_bytes=VMEM_LIMIT),
+        compiler_params=pltpu.CompilerParams(vmem_limit_bytes=PACK_LIMIT),
         cost_estimate=pl.CostEstimate(
             flops=4 * rows * deep * width, bytes_accessed=4 * deep * width, transcendentals=0
         ),
@@ -250,15 +297,20 @@
     near = pack(kv0, r1, block, 0)
     nears = [send(near, bits) for bits in (1, 2, 3)]
     far = pack(r2, r3, block, 10**10)
-    far, *nears = lax.optimization_barrier((far, *nears))
+    far, nears[2] = lax.optimization_barrier((far, nears[2]))
     fars = [send(far, bits) for bits in (1, 2, 3)]
-    sources = [near, far, *nears, *fars]
-    a0, a1, a2, a3 = attend(owners * tok, tok, (q0, r1, r2, r3), sources)
-    b2 = send(a2, 2 * PLANE)
-    b3 = send(a3, 3 * PLANE)
-    b1 = send(a1, PLANE)
-    own = (a0, b1, b2, b3)
-    return mix(own, tuple(swap(item) for item in own), w_out, w_other)
+    total = owners * tok
+    queries = (q0, r1, r2, r3)
+    expo, stats, values = early(total, tok, queries, [near, far, *nears])
+    own = [None] * SPLIT
+    for item in (3, 2, 1, 0):
+        ids = near if item < 2 else far
+        part = late(total, tok, item, queries[item], ids, expo, stats, values, fars)
+        part, stats = lax.optimization_barrier((part, stats))
+        own[item] = send(part, item * PLANE) if item else part
+        if item == 1:
+            own[3], stats = lax.optimization_barrier((own[3], stats))
+    return mix(own, [swap(item) for item in own], w_out, w_other)
 
 
 def attend_rows(query, keys, values, query_pos, key_pos):

time: 52.2 us -> 45.4 us (0.87)
  waiting for transfers between devices: 20.3 us -> 12.6 us
  Pallas kernels: 12.2 us -> 12.9 us
    ppermute x12, waiting for transfers between devices: 19.1 us -> 11.8 us  [send(): return lax.ppermute(array, 'seq', [(i, i ^ bits) for i in range(owners)])]
    pallas_call x1 -> x5, Pallas kernels: 6.01 us -> 7.71 us  [the longest x4 5.49 us: late(): pl.pallas_call(functools.partial(late_kernel, total, tok, item, len(sourc...]
    pallas_call x1, Pallas kernels: 5.03 us -> 4.06 us  [project(): pl.pallas_call(project_kernel, out_shape=(shape(tok + META), shape(tok //...]
  transfers between devices with their start and end apart: 17 -> 17, of which waited for: 10 -> 10; matrix products, arithmetic and copies ran while one was open for 0% -> 0% of each run, Pallas kernels for 10% -> 20%
where the time goes in v3:
time: 45.4 us; the launch traced here: 45.2 us
  starting transfers between devices  18.7 us (41%)
  Pallas kernels  12.9 us (28%)
  waiting for transfers between devices  12.6 us (28%)
  local copies, waits for them, and re-layouts  0.89 us (2%)
    ppermute x12, starting transfers between devices, send(): return lax.ppermute(array, 'seq', [(i, i ^ bits) for i in range(owners)])  17.6 us
    ppermute x12, waiting for transfers between devices, send(): return lax.ppermute(array, 'seq', [(i, i ^ bits) for i in range(owners)])  11.8 us
    pallas_call x4, Pallas kernels, late(): pl.pallas_call(functools.partial(late_kernel, total, tok, item, len(sourc...  5.49 us
    pallas_call x1, Pallas kernels, project(): pl.pallas_call(project_kernel, out_shape=(shape(tok + META), shape(tok //...  4.06 us
    pallas_call x1, Pallas kernels, early(): pl.pallas_call(functools.partial(early_kernel, total, tok, len(sources)),...  2.22 us
    pallas_call x1, Pallas kernels, mix(): pl.pallas_call(mix_kernel, out_shape=jax.ShapeDtypeStruct((rows, width),...  1.14 us
    ppermute x5, starting transfers between devices, swap(): return lax.ppermute(array, 'head', [(0, 1), (1, 0)])  1.04 us
  transfers between devices with their start and end apart: 17, of which 10 were waited for; matrix products, arithmetic and copies ran while one was open for 0% of the time, Pallas kernels for 20%

profile of v3, /device:TPU:0, one launch (start us, length us, event | category | flops | bytes accessed | tf_op | source)
XLA Modules:
  0.0 45.2 jit_solution(7301036123307883374)
XLA Ops:
  0.0 0.5 %collective-permute-start = (bf16[512,1024]{1,0:T(8,128)(2,1)}, bf16[512,1024]{1,0:T(8,128)(2,1)S(1)}, u32[]{:S(2)}, u32[]{:S(2)}) collective-permute-start(bf16[512,1024]{1,0:T(8,128)(2,1)} %refs_8_.1), channel_id=1, source_target_pairs={{0,1},{1,0},{2,3},{3,2},{4,5},{5,4},{6,7},{7,6},{8,9},{9,8},{10,11... | collective-permute-start | bytes 3145736 | tf_op jit(solution)/shard_map/ppermute | solution.py:289
  0.5 4.1 %project.1 = (bf16[144,256]{1,0:T(8,128)(2,1)}, bf16[64,256]{1,0:T(8,128)(2,1)}, bf16[208,256]{1,0:T(8,128)(2,1)}, bf16[208,256]{1,0:T(8,128)(2,1)}, bf16[208,256]{1,0:T(8,128)(2,1)}) custom-call(bf16[128,1024]{1,0:T(8,128)(2,1)} %tok_ref.1, s32[1,128]{1,0:T(1,128)} %bitcast.1, s32[2,128]{1,0:T(2,128)} %cid_ref.1, bf16[1024,512]{1,0:T(8,128)(2,1)} %wq_ref.1, ...), custom_call_target="tpu_custom_call" | custom-call | flops 402653184 | bytes 3145728 | tf_op jit(solution)/shard_map/project/pallas_call | solution.py:71
  4.5 2.6 %collective-permute-start.1 = (bf16[208,256]{1,0:T(8,128)(2,1)}, bf16[208,256]{1,0:T(8,128)(2,1)S(1)}, u32[]{:S(2)}, u32[]{:S(2)}) collective-permute-start(bf16[208,256]{1,0:T(8,128)(2,1)} %get-tuple-element.29), channel_id=1, source_target_pairs={{0,8},{2,10},{4,12},{6,14},{8,0},{10,2},{12,4},{14,6},{16,24},{18,... | collective-permute-start | bytes 319496 | tf_op jit(solution)/shard_map/ppermute | solution.py:286
  7.2 2.6 %collective-permute-start.2 = (bf16[208,256]{1,0:T(8,128)(2,1)}, bf16[208,256]{1,0:T(8,128)(2,1)S(1)}, u32[]{:S(2)}, u32[]{:S(2)}) collective-permute-start(bf16[208,256]{1,0:T(8,128)(2,1)} %get-tuple-element.30), channel_id=1, source_target_pairs={{0,16},{2,18},{4,20},{6,22},{8,24},{10,26},{12,28},{14,30},{16,0},... | collective-permute-start | bytes 319496 | tf_op jit(solution)/shard_map/ppermute | solution.py:286
  9.7 0.0 collective-permute-start.3
  9.7 0.0 collective-permute-done.refs_9_
  9.8 1.3 %collective-permute-done.1.second_ref.refs_1_.refs_0_ = bf16[208,256]{1,0:T(8,128)(2,1)S(1)} collective-permute-done((bf16[208,256]{1,0:T(8,128)(2,1)}, bf16[208,256]{1,0:T(8,128)(2,1)S(1)}, u32[]{:S(2)}, u32[]{:S(2)}) %collective-permute-start.1) | collective-permute-done | bytes 106528 | tf_op jit(solution)/shard_map/ppermute | solution.py:286
  11.0 0.0 copy-start.1
  11.0 0.9 %copy-done.1 = bf16[144,256]{1,0:T(8,128)(2,1)S(1)} copy-done((bf16[144,256]{1,0:T(8,128)(2,1)S(1)}, bf16[144,256]{1,0:T(8,128)(2,1)}, u32[]{:S(2)}) %copy-start.1) | copy-done | bytes 73752
  11.9 0.0 copy-start.2
  11.9 2.7 %collective-permute-start.4 = (bf16[288,256]{1,0:T(8,128)(2,1)S(1)}, bf16[288,256]{1,0:T(8,128)(2,1)S(1)}, u32[]{:S(2)}, u32[]{:S(2)}) collective-permute-start(bf16[288,256]{1,0:T(8,128)(2,1)S(1)} %pack.2.refs_4_.refs_1_), channel_id=1, source_target_pairs={{0,6},{2,4},{4,2},{6,0},{8,14},{10,12},{12,10},{14,8},{16,22},{18,... | collective-permute-start | bytes 442376 | tf_op jit(solution)/shard_map/ppermute | solution.py:286
  14.6 0.5 %collective-permute-start.5 = (bf16[288,256]{1,0:T(8,128)(2,1)S(1)}, bf16[288,256]{1,0:T(8,128)(2,1)S(1)}, u32[]{:S(2)}, u32[]{:S(2)}) collective-permute-start(bf16[288,256]{1,0:T(8,128)(2,1)S(1)} %pack.2.refs_4_.refs_1_), channel_id=1, source_target_pairs={{0,2},{2,0},{4,6},{6,4},{8,10},{10,8},{12,14},{14,12},{16,18},{18,... | collective-permute-start | bytes 442376 | tf_op jit(solution)/shard_map/ppermute | solution.py:286
  15.1 0.3 collective-permute-start.6
  15.5 3.2 %collective-permute-done.2.first_ref.refs_2_.refs_0_ = bf16[208,256]{1,0:T(8,128)(2,1)S(1)} collective-permute-done((bf16[208,256]{1,0:T(8,128)(2,1)}, bf16[208,256]{1,0:T(8,128)(2,1)S(1)}, u32[]{:S(2)}, u32[]{:S(2)}) %collective-permute-start.2) | collective-permute-done | bytes 106528 | tf_op jit(solution)/shard_map/ppermute | solution.py:286
  18.6 0.0 collective-permute-done.3.second_ref.refs_3_.refs_0_
  18.7 1.0 %collective-permute-done.4.refs_8_ = bf16[288,256]{1,0:T(8,128)(2,1)S(1)} collective-permute-done((bf16[288,256]{1,0:T(8,128)(2,1)S(1)}, bf16[288,256]{1,0:T(8,128)(2,1)S(1)}, u32[]{:S(2)}, u32[]{:S(2)}) %collective-permute-start.4) | collective-permute-done | bytes 147488 | tf_op jit(solution)/shard_map/ppermute | solution.py:286
  19.6 1.7 %collective-permute-start.7 = (bf16[288,256]{1,0:T(8,128)(2,1)S(1)}, bf16[288,256]{1,0:T(8,128)(2,1)S(1)}, u32[]{:S(2)}, u32[]{:S(2)}) collective-permute-start(bf16[288,256]{1,0:T(8,128)(2,1)S(1)} %pack.3.refs_5_.refs_1_), channel_id=1, source_target_pairs={{0,2},{2,0},{4,6},{6,4},{8,10},{10,8},{12,14},{14,12},{16,18},{18,... | collective-permute-start | bytes 442376 | tf_op jit(solution)/shard_map/ppermute | solution.py:286
  21.3 1.5 %collective-permute-start.8 = (bf16[288,256]{1,0:T(8,128)(2,1)S(1)}, bf16[288,256]{1,0:T(8,128)(2,1)S(1)}, u32[]{:S(2)}, u32[]{:S(2)}) collective-permute-start(bf16[288,256]{1,0:T(8,128)(2,1)S(1)} %pack.3.refs_5_.refs_1_), channel_id=1, source_target_pairs={{0,4},{2,6},{4,0},{6,2},{8,12},{10,14},{12,8},{14,10},{16,20},{18,... | collective-permute-start | bytes 442376 | tf_op jit(solution)/shard_map/ppermute | solution.py:286
  22.8 0.3 collective-permute-start.9
  23.1 0.0 collective-permute-done.5.refs_6_
  23.1 0.0 collective-permute-done.6.refs_7_
  23.1 0.0 copy-done.2
  23.1 2.2 %early.1 = (f32[1024,1280]{1,0:T(8,128)S(1)}, f32[1024,128]{1,0:T(8,128)S(1)}, bf16[1280,128]{1,0:T(8,128)(2,1)S(1)}) custom-call(bf16[64,256]{1,0:T(8,128)(2,1)S(1)} %copy-done.2, bf16[208,256]{1,0:T(8,128)(2,1)S(1)} %collective-permute-done.1.second_ref.refs_1_.refs_0_, bf16[208,256]{1,0:T(8,128)(2,1)S(1)} %collective-permute-done.2.first_ref.refs_2_.refs_0_, ...), custom_call_target="tpu_custom_call" | custom-call | flops 8000000000 | bytes 1310720 | tf_op jit(solution)/shard_map/early/pallas_call | solution.py:177
  25.3 1.1 %collective-permute-done.7.refs_5_ = bf16[288,256]{1,0:T(8,128)(2,1)S(1)} collective-permute-done((bf16[288,256]{1,0:T(8,128)(2,1)S(1)}, bf16[288,256]{1,0:T(8,128)(2,1)S(1)}, u32[]{:S(2)}, u32[]{:S(2)}) %collective-permute-start.7) | collective-permute-done | bytes 147488 | tf_op jit(solution)/shard_map/ppermute | solution.py:286
  26.4 1.5 %collective-permute-done.8.refs_6_ = bf16[288,256]{1,0:T(8,128)(2,1)S(1)} collective-permute-done((bf16[288,256]{1,0:T(8,128)(2,1)S(1)}, bf16[288,256]{1,0:T(8,128)(2,1)S(1)}, u32[]{:S(2)}, u32[]{:S(2)}) %collective-permute-start.8) | collective-permute-done | bytes 147488 | tf_op jit(solution)/shard_map/ppermute | solution.py:286
  27.9 1.0 %collective-permute-done.9.refs_7_ = bf16[288,256]{1,0:T(8,128)(2,1)S(1)} collective-permute-done((bf16[288,256]{1,0:T(8,128)(2,1)S(1)}, bf16[288,256]{1,0:T(8,128)(2,1)S(1)}, u32[]{:S(2)}, u32[]{:S(2)}) %collective-permute-start.9) | collective-permute-done | bytes 147488 | tf_op jit(solution)/shard_map/ppermute | solution.py:286
  28.9 1.4 %late.4 = bf16[128,128]{1,0:T(8,128)(2,1)S(1)} custom-call(bf16[208,256]{1,0:T(8,128)(2,1)S(1)} %collective-permute-done.3.second_ref.refs_3_.refs_0_, bf16[288,256]{1,0:T(8,128)(2,1)S(1)} %pack.3.refs_5_.refs_1_, f32[1024,1280]{1,0:T(8,128)S(1)} %get-tuple-element.34.refs_2_, f32[1024,128]{1,0:T(8,128)S(1)} %get-tuple-element.41.refs_3_, ...), custom_call_target="tpu_custom_call" | custom-call | flops 3000000000 | bytes 393216 | tf_op jit(solution)/shard_map/late/pallas_call | solution.py:228
  30.2 1.4 %late.5 = bf16[128,128]{1,0:T(8,128)(2,1)S(1)} custom-call(bf16[208,256]{1,0:T(8,128)(2,1)S(1)} %collective-permute-done.2.first_ref.refs_2_.refs_0_, bf16[288,256]{1,0:T(8,128)(2,1)S(1)} %pack.3.refs_5_.refs_1_, f32[1024,1280]{1,0:T(8,128)S(1)} %get-tuple-element.34.refs_2_, f32[1024,128]{1,0:T(8,128)S(1)} %get-tuple-element.41.refs_3_, ...), custom_call_target="tpu_custom_call" | custom-call | flops 3000000000 | bytes 393216 | tf_op jit(solution)/shard_map/late/pallas_call | solution.py:228
  31.6 4.7 %collective-permute-start.10 = (bf16[128,128]{1,0:T(8,128)(2,1)S(1)}, bf16[128,128]{1,0:T(8,128)(2,1)S(1)}, u32[]{:S(2)}, u32[]{:S(2)}) collective-permute-start(bf16[128,128]{1,0:T(8,128)(2,1)S(1)} %late.4), channel_id=1, source_target_pairs={{0,24},{2,26},{4,28},{6,30},{8,16},{10,18},{12,20},{14,22},{16,8},... | collective-permute-start | bytes 98312 | tf_op jit(solution)/shard_map/ppermute | solution.py:286
  36.3 1.4 %late.6 = bf16[128,128]{1,0:T(8,128)(2,1)S(1)} custom-call(bf16[208,256]{1,0:T(8,128)(2,1)S(1)} %collective-permute-done.1.second_ref.refs_1_.refs_0_, bf16[288,256]{1,0:T(8,128)(2,1)S(1)} %pack.2.refs_4_.refs_1_, f32[1024,1280]{1,0:T(8,128)S(1)} %get-tuple-element.34.refs_2_, f32[1024,128]{1,0:T(8,128)S(1)} %get-tuple-element.41.refs_3_, ...), custom_call_target="tpu_custom_call" | custom-call | flops 3000000000 | bytes 393216 | tf_op jit(solution)/shard_map/late/pallas_call | solution.py:228
  37.7 0.0 copy-start
  37.7 0.1 collective-permute-start.11
  37.8 0.6 %collective-permute-start.12 = (bf16[128,128]{1,0:T(8,128)(2,1)S(1)}, bf16[128,128]{1,0:T(8,128)(2,1)S(1)}, u32[]{:S(2)}, u32[]{:S(2)}) collective-permute-start(bf16[128,128]{1,0:T(8,128)(2,1)S(1)} %late.5), channel_id=1, source_target_pairs={{0,16},{2,18},{4,20},{6,22},{8,24},{10,26},{12,28},{14,30},{16,0},... | collective-permute-start | bytes 98312 | tf_op jit(solution)/shard_map/ppermute | solution.py:286
  38.4 0.0 collective-permute-done.10.refs_3_
  38.4 1.4 %late.7.refs_0_ = bf16[128,128]{1,0:T(8,128)(2,1)S(1)} custom-call(bf16[64,256]{1,0:T(8,128)(2,1)S(1)} %copy-done.2, bf16[288,256]{1,0:T(8,128)(2,1)S(1)} %pack.2.refs_4_.refs_1_, f32[1024,1280]{1,0:T(8,128)S(1)} %get-tuple-element.34.refs_2_, f32[1024,128]{1,0:T(8,128)S(1)} %get-tuple-element.41.refs_3_, bf16[1280,128]{1,0:T(8,128)(2,1)S(1)} %get-tuple-element.36.refs_4_, ...), custom_call_target="tpu_custom_call" | custom-call | flops 3000000000 | bytes 393216 | tf_op jit(solution)/shard_map/late/pallas_call | solution.py:228
  39.8 0.1 collective-permute-start.13
  39.8 1.9 %collective-permute-done.11.refs_1_ = bf16[128,128]{1,0:T(8,128)(2,1)S(1)} collective-permute-done((bf16[128,128]{1,0:T(8,128)(2,1)S(1)}, bf16[128,128]{1,0:T(8,128)(2,1)S(1)}, u32[]{:S(2)}, u32[]{:S(2)}) %collective-permute-start.11) | collective-permute-done | bytes 32800 | tf_op jit(solution)/shard_map/ppermute | solution.py:286
  41.7 0.0 collective-permute-start.14
  41.7 1.0 %collective-permute-done.12.refs_2_ = bf16[128,128]{1,0:T(8,128)(2,1)S(1)} collective-permute-done((bf16[128,128]{1,0:T(8,128)(2,1)S(1)}, bf16[128,128]{1,0:T(8,128)(2,1)S(1)}, u32[]{:S(2)}, u32[]{:S(2)}) %collective-permute-start.12) | collective-permute-done | bytes 32800 | tf_op jit(solution)/shard_map/ppermute | solution.py:286
  42.7 0.0 collective-permute-start.15
  42.7 0.5 %collective-permute-start.16 = (bf16[128,128]{1,0:T(8,128)(2,1)S(1)}, bf16[128,128]{1,0:T(8,128)(2,1)S(1)}, u32[]{:S(2)}, u32[]{:S(2)}) collective-permute-start(bf16[128,128]{1,0:T(8,128)(2,1)S(1)} %collective-permute-done.10.refs_3_), channel_id=1, source_target_pairs={{0,1},{1,0},{2,3},{3,2},{4,5},{5,4},{6,7},{7,6},{8,9},{9,8},{10,11... | collective-permute-start | bytes 98312 | tf_op jit(solution)/shard_map/ppermute | solution.py:289
  43.2 0.0 collective-permute-done.14.refs_5_
  43.2 0.0 collective-permute-done.13.refs_4_
  43.2 0.7 %collective-permute-done.15.refs_6_ = bf16[128,128]{1,0:T(8,128)(2,1)S(1)} collective-permute-done((bf16[128,128]{1,0:T(8,128)(2,1)S(1)}, bf16[128,128]{1,0:T(8,128)(2,1)S(1)}, u32[]{:S(2)}, u32[]{:S(2)}) %collective-permute-start.15) | collective-permute-done | bytes 32800 | tf_op jit(solution)/shard_map/ppermute | solution.py:289
  43.9 0.2 collective-permute-done.16.refs_7_
  44.1 0.0 copy-done
  44.1 1.1 %mix.1 = bf16[64,1024]{1,0:T(8,128)(2,1)} custom-call(bf16[128,128]{1,0:T(8,128)(2,1)S(1)} %late.7.refs_0_, bf16[128,128]{1,0:T(8,128)(2,1)S(1)} %collective-permute-done.11.refs_1_, bf16[128,128]{1,0:T(8,128)(2,1)S(1)} %collective-permute-done.12.refs_2_, bf16[128,128]{1,0:T(8,128)(2,1)S(1)} %collective-permute-done.10.refs_3_, ...), custom_call_target="tpu_custom_call" | custom-call | flops 134217728 | bytes 2097152 | tf_op jit(solution)/shard_map/mix/pallas_call | solution.py:266
  (2 shorter events, 0.0 us)
Async XLA Ops:
  0.0 9.8 %collective-permute-start = (bf16[512,1024]{1,0:T(8,128)(2,1)}, bf16[512,1024]{1,0:T(8,128)(2,1)S(1)}, u32[]{:S(2)}, u32[]{:S(2)}) collective-permute-start(bf16[512,1024]{1,0:T(8,128)(2,1)} %refs_8_.1), channel_id=1, source_target_pairs={{0,1},{1,0},{2,3},{3,2},{4,5},{5,4},{6,7},{7,6},{8,9},{9,8},{10,11... | collective-permute-start | bytes 3145736 | tf_op jit(solution)/shard_map/ppermute | solution.py:289
  4.5 6.5 %collective-permute-start.1 = (bf16[208,256]{1,0:T(8,128)(2,1)}, bf16[208,256]{1,0:T(8,128)(2,1)S(1)}, u32[]{:S(2)}, u32[]{:S(2)}) collective-permute-start(bf16[208,256]{1,0:T(8,128)(2,1)} %get-tuple-element.29), channel_id=1, source_target_pairs={{0,8},{2,10},{4,12},{6,14},{8,0},{10,2},{12,4},{14,6},{16,24},{18,... | collective-permute-start | bytes 319496 | tf_op jit(solution)/shard_map/ppermute | solution.py:286
  7.2 11.5 %collective-permute-start.2 = (bf16[208,256]{1,0:T(8,128)(2,1)}, bf16[208,256]{1,0:T(8,128)(2,1)S(1)}, u32[]{:S(2)}, u32[]{:S(2)}) collective-permute-start(bf16[208,256]{1,0:T(8,128)(2,1)} %get-tuple-element.30), channel_id=1, source_target_pairs={{0,16},{2,18},{4,20},{6,22},{8,24},{10,26},{12,28},{14,30},{16,0},... | collective-permute-start | bytes 319496 | tf_op jit(solution)/shard_map/ppermute | solution.py:286
  9.7 8.9 %collective-permute-start.3 = (bf16[208,256]{1,0:T(8,128)(2,1)}, bf16[208,256]{1,0:T(8,128)(2,1)S(1)}, u32[]{:S(2)}, u32[]{:S(2)}) collective-permute-start(bf16[208,256]{1,0:T(8,128)(2,1)} %get-tuple-element.31), channel_id=1, source_target_pairs={{0,24},{2,26},{4,28},{6,30},{8,16},{10,18},{12,20},{14,22},{16,8},... | collective-permute-start | bytes 319496 | tf_op jit(solution)/shard_map/ppermute | solution.py:286
  11.0 0.9 %copy-start.1 = (bf16[144,256]{1,0:T(8,128)(2,1)S(1)}, bf16[144,256]{1,0:T(8,128)(2,1)}, u32[]{:S(2)}) copy-start(bf16[144,256]{1,0:T(8,128)(2,1)} %get-tuple-element.28.first_ref) | copy-start | bytes 221188
  11.9 11.2 %copy-start.2 = (bf16[64,256]{1,0:T(8,128)(2,1)S(1)}, bf16[64,256]{1,0:T(8,128)(2,1)}, u32[]{:S(2)}) copy-start(bf16[64,256]{1,0:T(8,128)(2,1)} %get-tuple-element.26.refs_0_) | copy-start | bytes 98308
  11.9 7.7 %collective-permute-start.4 = (bf16[288,256]{1,0:T(8,128)(2,1)S(1)}, bf16[288,256]{1,0:T(8,128)(2,1)S(1)}, u32[]{:S(2)}, u32[]{:S(2)}) collective-permute-start(bf16[288,256]{1,0:T(8,128)(2,1)S(1)} %pack.2.refs_4_.refs_1_), channel_id=1, source_target_pairs={{0,6},{2,4},{4,2},{6,0},{8,14},{10,12},{12,10},{14,8},{16,22},{18,... | collective-permute-start | bytes 442376 | tf_op jit(solution)/shard_map/ppermute | solution.py:286
  14.6 8.5 %collective-permute-start.5 = (bf16[288,256]{1,0:T(8,128)(2,1)S(1)}, bf16[288,256]{1,0:T(8,128)(2,1)S(1)}, u32[]{:S(2)}, u32[]{:S(2)}) collective-permute-start(bf16[288,256]{1,0:T(8,128)(2,1)S(1)} %pack.2.refs_4_.refs_1_), channel_id=1, source_target_pairs={{0,2},{2,0},{4,6},{6,4},{8,10},{10,8},{12,14},{14,12},{16,18},{18,... | collective-permute-start | bytes 442376 | tf_op jit(solution)/shard_map/ppermute | solution.py:286
  15.1 8.0 %collective-permute-start.6 = (bf16[288,256]{1,0:T(8,128)(2,1)S(1)}, bf16[288,256]{1,0:T(8,128)(2,1)S(1)}, u32[]{:S(2)}, u32[]{:S(2)}) collective-permute-start(bf16[288,256]{1,0:T(8,128)(2,1)S(1)} %pack.2.refs_4_.refs_1_), channel_id=1, source_target_pairs={{0,4},{2,6},{4,0},{6,2},{8,12},{10,14},{12,8},{14,10},{16,20},{18,... | collective-permute-start | bytes 442376 | tf_op jit(solution)/shard_map/ppermute | solution.py:286
  19.6 6.8 %collective-permute-start.7 = (bf16[288,256]{1,0:T(8,128)(2,1)S(1)}, bf16[288,256]{1,0:T(8,128)(2,1)S(1)}, u32[]{:S(2)}, u32[]{:S(2)}) collective-permute-start(bf16[288,256]{1,0:T(8,128)(2,1)S(1)} %pack.3.refs_5_.refs_1_), channel_id=1, source_target_pairs={{0,2},{2,0},{4,6},{6,4},{8,10},{10,8},{12,14},{14,12},{16,18},{18,... | collective-permute-start | bytes 442376 | tf_op jit(solution)/shard_map/ppermute | solution.py:286
  21.3 6.6 %collective-permute-start.8 = (bf16[288,256]{1,0:T(8,128)(2,1)S(1)}, bf16[288,256]{1,0:T(8,128)(2,1)S(1)}, u32[]{:S(2)}, u32[]{:S(2)}) collective-permute-start(bf16[288,256]{1,0:T(8,128)(2,1)S(1)} %pack.3.refs_5_.refs_1_), channel_id=1, source_target_pairs={{0,4},{2,6},{4,0},{6,2},{8,12},{10,14},{12,8},{14,10},{16,20},{18,... | collective-permute-start | bytes 442376 | tf_op jit(solution)/shard_map/ppermute | solution.py:286
  22.8 6.0 %collective-permute-start.9 = (bf16[288,256]{1,0:T(8,128)(2,1)S(1)}, bf16[288,256]{1,0:T(8,128)(2,1)S(1)}, u32[]{:S(2)}, u32[]{:S(2)}) collective-permute-start(bf16[288,256]{1,0:T(8,128)(2,1)S(1)} %pack.3.refs_5_.refs_1_), channel_id=1, source_target_pairs={{0,6},{2,4},{4,2},{6,0},{8,14},{10,12},{12,10},{14,8},{16,22},{18,... | collective-permute-start | bytes 442376 | tf_op jit(solution)/shard_map/ppermute | solution.py:286
  31.6 6.8 %collective-permute-start.10 = (bf16[128,128]{1,0:T(8,128)(2,1)S(1)}, bf16[128,128]{1,0:T(8,128)(2,1)S(1)}, u32[]{:S(2)}, u32[]{:S(2)}) collective-permute-start(bf16[128,128]{1,0:T(8,128)(2,1)S(1)} %late.4), channel_id=1, source_target_pairs={{0,24},{2,26},{4,28},{6,30},{8,16},{10,18},{12,20},{14,22},{16,8},... | collective-permute-start | bytes 98312 | tf_op jit(solution)/shard_map/ppermute | solution.py:286
  37.7 6.3 %copy-start = (bf16[512,1024]{1,0:T(8,128)(2,1)S(1)}, bf16[512,1024]{1,0:T(8,128)(2,1)}, u32[]{:S(2)}) copy-start(bf16[512,1024]{1,0:T(8,128)(2,1)} %refs_8_.1) | copy-start | bytes 3145732
  37.7 4.0 %collective-permute-start.11 = (bf16[128,128]{1,0:T(8,128)(2,1)S(1)}, bf16[128,128]{1,0:T(8,128)(2,1)S(1)}, u32[]{:S(2)}, u32[]{:S(2)}) collective-permute-start(bf16[128,128]{1,0:T(8,128)(2,1)S(1)} %late.6), channel_id=1, source_target_pairs={{0,8},{2,10},{4,12},{6,14},{8,0},{10,2},{12,4},{14,6},{16,24},{18,... | collective-permute-start | bytes 98312 | tf_op jit(solution)/shard_map/ppermute | solution.py:286
  37.8 4.9 %collective-permute-start.12 = (bf16[128,128]{1,0:T(8,128)(2,1)S(1)}, bf16[128,128]{1,0:T(8,128)(2,1)S(1)}, u32[]{:S(2)}, u32[]{:S(2)}) collective-permute-start(bf16[128,128]{1,0:T(8,128)(2,1)S(1)} %late.5), channel_id=1, source_target_pairs={{0,16},{2,18},{4,20},{6,22},{8,24},{10,26},{12,28},{14,30},{16,0},... | collective-permute-start | bytes 98312 | tf_op jit(solution)/shard_map/ppermute | solution.py:286
  39.8 3.5 %collective-permute-start.13 = (bf16[128,128]{1,0:T(8,128)(2,1)S(1)}, bf16[128,128]{1,0:T(8,128)(2,1)S(1)}, u32[]{:S(2)}, u32[]{:S(2)}) collective-permute-start(bf16[128,128]{1,0:T(8,128)(2,1)S(1)} %late.7.refs_0_), channel_id=1, source_target_pairs={{0,1},{1,0},{2,3},{3,2},{4,5},{5,4},{6,7},{7,6},{8,9},{9,8},{10,11... | collective-permute-start | bytes 98312 | tf_op jit(solution)/shard_map/ppermute | solution.py:289
  41.7 1.5 %collective-permute-start.14 = (bf16[128,128]{1,0:T(8,128)(2,1)S(1)}, bf16[128,128]{1,0:T(8,128)(2,1)S(1)}, u32[]{:S(2)}, u32[]{:S(2)}) collective-permute-start(bf16[128,128]{1,0:T(8,128)(2,1)S(1)} %collective-permute-done.11.refs_1_), channel_id=1, source_target_pairs={{0,1},{1,0},{2,3},{3,2},{4,5},{5,4},{6,7},{7,6},{8,9},{9,8},{10,11... | collective-permute-start | bytes 98312 | tf_op jit(solution)/shard_map/ppermute | solution.py:289
  42.7 1.2 %collective-permute-start.15 = (bf16[128,128]{1,0:T(8,128)(2,1)S(1)}, bf16[128,128]{1,0:T(8,128)(2,1)S(1)}, u32[]{:S(2)}, u32[]{:S(2)}) collective-permute-start(bf16[128,128]{1,0:T(8,128)(2,1)S(1)} %collective-permute-done.12.refs_2_), channel_id=1, source_target_pairs={{0,1},{1,0},{2,3},{3,2},{4,5},{5,4},{6,7},{7,6},{8,9},{9,8},{10,11... | collective-permute-start | bytes 98312 | tf_op jit(solution)/shard_map/ppermute | solution.py:289
  42.7 1.4 %collective-permute-start.16 = (bf16[128,128]{1,0:T(8,128)(2,1)S(1)}, bf16[128,128]{1,0:T(8,128)(2,1)S(1)}, u32[]{:S(2)}, u32[]{:S(2)}) collective-permute-start(bf16[128,128]{1,0:T(8,128)(2,1)S(1)} %collective-permute-done.10.refs_3_), channel_id=1, source_target_pairs={{0,1},{1,0},{2,3},{3,2},{4,5},{5,4},{6,7},{7,6},{8,9},{9,8},{10,11... | collective-permute-start | bytes 98312 | tf_op jit(solution)/shard_map/ppermute | solution.py:289

commit v4 on v3

--- a/solution.py
+++ b/solution.py
@@ -12,79 +12,89 @@
 
 SPLIT = 4
 PLANE = 4
-META = 16
+META = 8
 BASE = 128
+PROJECT_LIMIT = (53 << 20) + (512 << 10)
 PACK_LIMIT = 4 << 20
 ATTEND_LIMIT = 16 << 20
+FAR_FLOPS = 10**10
 EARLY_FLOPS = 8 * 10**9
-LATE_FLOPS = (3 * 10**9,) * SPLIT
+LATE_FLOPS = 3 * 10**9
 LOG2E = 1.4426950408889634
 
 
-def project_kernel(tok_ref, pos_ref, cid_ref, wq_ref, wk_ref, wv_ref, *rest):
-    kv0_ref, q0_ref, m1_ref, m2_ref, m3_ref, rows, wbuf, qkv, sems, rows_sem = rest
-    tok, cols = tok_ref.shape[0], wq_ref.shape[1]
-    pair = cols // SPLIT
-    rows_copy = pltpu.make_async_copy(tok_ref, rows, rows_sem)
-    rows_copy.start()
+def project_kernel(steps, tok_hbm, pos_hbm, cid_hbm, wq_ref, wk_ref, wv_ref, *rest):
+    out_refs = list(rest[:-6])
+    rows, pos_ref, cid_ref, wbuf, sems, small_sems = rest[-6:]
+    tok, pair = rows.shape[0], wbuf.shape[2] // 3
+    chip = lax.axis_index("seq") // PLANE
+    small = [
+        pltpu.make_async_copy(source, target, small_sems.at[at])
+        for at, (source, target) in enumerate(
+            ((tok_hbm, rows), (pos_hbm, pos_ref), (cid_hbm, cid_ref))
+        )
+    ]
+    for copy in small:
+        copy.start()
     copies = []
-    for part, w_ref in enumerate((wq_ref, wk_ref, wv_ref)):
-        copy = pltpu.make_async_copy(w_ref, wbuf.at[part], sems.at[part])
-        copy.start()
-        copies.append(copy)
-    rows_copy.wait()
-    for part, copy in enumerate(copies):
+    for at, step in enumerate(steps):
+        lanes = pl.ds(pl.multiple_of(jnp.bitwise_xor(chip, step) * pair, pair), pair)
+        for part, w_ref in enumerate((wq_ref, wk_ref, wv_ref)):
+            target = wbuf.at[at, :, pl.ds(part * pair, pair)]
+            copy = pltpu.make_async_copy(w_ref.at[:, lanes], target, sems.at[at, part])
+            copy.start()
+            copies.append(copy)
+    for copy in small:
         copy.wait()
-        result = jnp.dot(rows[...], wbuf[part], preferred_element_type=jnp.float32)
-        qkv[:, part * cols : (part + 1) * cols] = result.astype(jnp.bfloat16)
     high_digit = jnp.broadcast_to(pos_ref[...] // BASE, (META, tok))
     low_digit = jnp.broadcast_to(pos_ref[...] % BASE, (META, tok))
     first = lax.broadcasted_iota(jnp.int32, (META, tok), 0) == 0
-    chip = lax.axis_index("seq") // PLANE
-    for step, refs in enumerate(((kv0_ref, q0_ref), (m1_ref,), (m2_ref,), (m3_ref,))):
+    for at, step in enumerate(steps):
+        for part in range(3):
+            copies[3 * at + part].wait()
+        result = jnp.dot(rows[...], wbuf[at], preferred_element_type=jnp.float32)
+        result = result.astype(jnp.bfloat16)
+        kv_ref = out_refs.pop(0)
+        kv_ref[:tok, :] = result[:, pair:]
         who = jnp.bitwise_xor(chip, step)
-        kv_ref = refs[0]
-        lo = pl.multiple_of(who * pair, pair)
-        query = qkv[:, pl.ds(lo, pair)]
-        kv_ref[:tok, :pair] = qkv[:, pl.ds(pl.multiple_of(cols + lo, pair), pair)]
-        kv_ref[:tok, pair:] = qkv[:, pl.ds(pl.multiple_of(2 * cols + lo, pair), pair)]
         ids = jnp.where(who >= SPLIT // 2, cid_ref[1:2, :], cid_ref[0:1, :])
         left = jnp.where(first, jnp.broadcast_to(ids, (META, tok)), low_digit)
         kv_ref[tok : tok + META, :pair] = left.astype(jnp.float32).astype(jnp.bfloat16)
         kv_ref[tok : tok + META, pair:] = high_digit.astype(jnp.float32).astype(jnp.bfloat16)
-        q_ref, base = (refs[1], 0) if step == 0 else (kv_ref, tok + META)
-        q_ref[base : base + tok // 2, :pair] = query[: tok // 2]
-        q_ref[base : base + tok // 2, pair:] = query[tok // 2 :]
-
-
-def project(tokens, positions, cluster_ids, w_query, w_key, w_value):
+        q_ref, base = (kv_ref, tok + META) if step else (out_refs.pop(0), 0)
+        q_ref[base : base + tok // 2, :pair] = result[: tok // 2, :pair]
+        q_ref[base : base + tok // 2, pair:] = result[tok // 2 :, :pair]
+
+
+def project(steps, tokens, positions, cluster_ids, weights):
     tok, depth = tokens.shape
-    cols = w_query.shape[1]
-    wide = 2 * cols // SPLIT
+    pair = weights[0].shape[1] // SPLIT
     vmem = pl.BlockSpec(memory_space=pltpu.VMEM)
     hbm = pl.BlockSpec(memory_space=pltpu.HBM)
-    full = tok + META + tok // 2
-
-    def shape(rows):
-        return jax.ShapeDtypeStruct((rows, wide), jnp.bfloat16)
-
+    sizes = []
+    for step in steps:
+        sizes += [tok + META + tok // 2] if step else [tok + META, tok // 2]
     return pl.pallas_call(
-        project_kernel,
-        out_shape=(shape(tok + META), shape(tok // 2), shape(full), shape(full), shape(full)),
-        in_specs=[hbm, vmem, vmem, hbm, hbm, hbm],
-        out_specs=(vmem,) * 5,
+        functools.partial(project_kernel, steps),
+        out_shape=tuple(jax.ShapeDtypeStruct((rows, 2 * pair), jnp.bfloat16) for rows in sizes),
+        in_specs=[hbm] * 6,
+        out_specs=(vmem,) * len(sizes),
         scratch_shapes=[
             pltpu.VMEM((tok, depth), jnp.bfloat16),
-            pltpu.VMEM((3, depth, cols), jnp.bfloat16),
-            pltpu.VMEM((tok, 3 * cols), jnp.bfloat16),
+            pltpu.VMEM((1, tok), jnp.int32),
+            pltpu.VMEM(cluster_ids.shape, jnp.int32),
+            pltpu.VMEM((len(steps), depth, 3 * pair), jnp.bfloat16),
+            pltpu.SemaphoreType.DMA((len(steps), 3)),
             pltpu.SemaphoreType.DMA((3,)),
-            pltpu.SemaphoreType.DMA(()),
         ],
+        compiler_params=pltpu.CompilerParams(vmem_limit_bytes=PROJECT_LIMIT),
         cost_estimate=pl.CostEstimate(
-            flops=6 * tok * depth * cols, bytes_accessed=6 * depth * cols, transcendentals=0
+            flops=6 * tok * depth * pair * len(steps),
+            bytes_accessed=6 * depth * pair * len(steps),
+            transcendentals=0,
         ),
         name="project",
-    )(tokens, positions.reshape(1, tok), cluster_ids, w_query, w_key, w_value)
+    )(tokens, positions.reshape(1, tok), cluster_ids, *weights)
 
 
 def pack_kernel(first_ref, second_ref, out_ref):
@@ -196,40 +206,45 @@
     )(*queries, *sources)
 
 
-def late_kernel(total, tok, item, count, *refs):
-    q_ref, ids_ref, expo_ref, stats_ref, old_values = refs[:5]
-    kv_refs = refs[5 : 5 + count]
-    out_ref, keys, values, codes, column = refs[5 + count :]
+def late_kernel(total, tok, items, count, *refs):
+    many = len(items)
+    q_refs, ids_refs = refs[:many], refs[many : 2 * many]
+    expo_ref, stats_ref, old_values = refs[2 * many : 2 * many + 3]
+    kv_refs = refs[2 * many + 3 : 2 * many + 3 + count]
+    out_refs = refs[2 * many + 3 + count : 3 * many + 3 + count]
+    keys, values, codes, column = refs[3 * many + 3 + count :]
     unpack(kv_refs, tok, total, keys, values, codes)
     pair = keys.shape[1]
-    scores = scores_of(q_ref, ids_ref, (item % 2) * (tok + META), tok, total, keys, codes, column)
-    rows = slice(item * 2 * tok, (item + 1) * 2 * tok)
-    old_top = stats_ref[rows, 0:1]
-    top = jnp.maximum(jnp.max(scores, axis=1, keepdims=True), old_top)
-    expo = jnp.exp2(scores - top)
-    factor = jnp.exp2(old_top - top)
-    inverse = 1.0 / (jnp.sum(expo, axis=1, keepdims=True) + stats_ref[rows, 1:2] * factor)
-    result = jnp.dot(
-        (expo_ref[rows, :] * (factor * inverse)).astype(jnp.bfloat16),
-        old_values[...],
-        preferred_element_type=jnp.float32,
-    )
-    result += jnp.dot(
-        (expo * inverse).astype(jnp.bfloat16), values[...], preferred_element_type=jnp.float32
-    )
     lane = lax.broadcasted_iota(jnp.int32, (tok, pair), 1) < HD
-    out_ref[...] = jnp.where(lane, result[:tok], result[tok:]).astype(jnp.bfloat16)
-
-
-def late(total, tok, item, query, ids, expo, stats, old_values, sources):
+    for at, item in enumerate(items):
+        base = (item % 2) * (tok + META)
+        scores = scores_of(q_refs[at], ids_refs[at], base, tok, total, keys, codes, column)
+        rows = slice(item * 2 * tok, (item + 1) * 2 * tok)
+        old_top = stats_ref[rows, 0:1]
+        top = jnp.maximum(jnp.max(scores, axis=1, keepdims=True), old_top)
+        expo = jnp.exp2(scores - top)
+        factor = jnp.exp2(old_top - top)
+        inverse = 1.0 / (jnp.sum(expo, axis=1, keepdims=True) + stats_ref[rows, 1:2] * factor)
+        result = jnp.dot(
+            (expo_ref[rows, :] * (factor * inverse)).astype(jnp.bfloat16),
+            old_values[...],
+            preferred_element_type=jnp.float32,
+        )
+        result += jnp.dot(
+            (expo * inverse).astype(jnp.bfloat16), values[...], preferred_element_type=jnp.float32
+        )
+        out_refs[at][...] = jnp.where(lane, result[:tok], result[tok:]).astype(jnp.bfloat16)
+
+
+def late(total, tok, items, queries, ids, expo, stats, old_values, sources):
     pair = old_values.shape[1]
     vmem = pl.BlockSpec(memory_space=pltpu.VMEM)
     count = sum(part.shape[0] for part in sources) // (tok + META) * tok
     return pl.pallas_call(
-        functools.partial(late_kernel, total, tok, item, len(sources)),
-        out_shape=jax.ShapeDtypeStruct((tok, pair), jnp.bfloat16),
-        in_specs=[vmem] * (5 + len(sources)),
-        out_specs=vmem,
+        functools.partial(late_kernel, total, tok, items, len(sources)),
+        out_shape=(jax.ShapeDtypeStruct((tok, pair), jnp.bfloat16),) * len(items),
+        in_specs=[vmem] * (2 * len(items) + 3 + len(sources)),
+        out_specs=(vmem,) * len(items),
         scratch_shapes=[
             pltpu.VMEM((count, pair), jnp.bfloat16),
             pltpu.VMEM((count, pair), jnp.bfloat16),
@@ -238,10 +253,12 @@
         ],
         compiler_params=pltpu.CompilerParams(vmem_limit_bytes=ATTEND_LIMIT),
         cost_estimate=pl.CostEstimate(
-            flops=LATE_FLOPS[item], bytes_accessed=4 * count * pair, transcendentals=2 * tok * count
+            flops=LATE_FLOPS,
+            bytes_accessed=4 * count * pair,
+            transcendentals=2 * len(items) * tok * count,
         ),
         name="late",
-    )(query, ids, expo, stats, old_values, *sources)
+    )(*queries, *ids, expo, stats, old_values, *sources)
 
 
 def mix_kernel(*refs):
@@ -289,27 +306,23 @@
         return lax.ppermute(array, "head", [(0, 1), (1, 0)])
 
     w_other = swap(w_out)
-    kv0, q0, m1, m2, m3 = project(tokens, positions, cluster_ids, w_query, w_key, w_value)
-    r1 = send(m1, PLANE)
-    r2 = send(m2, 2 * PLANE)
-    r3 = send(m3, 3 * PLANE)
+    weights = (w_query, w_key, w_value)
+    m1, kv0, q0, m3, m2 = project((1, 0, 3, 2), tokens, positions, cluster_ids, weights)
+    r1, r3, r2 = send(m1, PLANE), send(m3, 3 * PLANE), send(m2, 2 * PLANE)
     kv0, w_other = lax.optimization_barrier((kv0, w_other))
     near = pack(kv0, r1, block, 0)
     nears = [send(near, bits) for bits in (1, 2, 3)]
-    far = pack(r2, r3, block, 10**10)
+    far = pack(r2, r3, block, FAR_FLOPS)
     far, nears[2] = lax.optimization_barrier((far, nears[2]))
     fars = [send(far, bits) for bits in (1, 2, 3)]
     total = owners * tok
-    queries = (q0, r1, r2, r3)
-    expo, stats, values = early(total, tok, queries, [near, far, *nears])
-    own = [None] * SPLIT
-    for item in (3, 2, 1, 0):
-        ids = near if item < 2 else far
-        part = late(total, tok, item, queries[item], ids, expo, stats, values, fars)
-        part, stats = lax.optimization_barrier((part, stats))
-        own[item] = send(part, item * PLANE) if item else part
-        if item == 1:
-            own[3], stats = lax.optimization_barrier((own[3], stats))
+    expo, stats, values = early(total, tok, (q0, r1, r2, r3), [near, far, *nears])
+    a3, a2 = late(total, tok, (3, 2), (r3, r2), (far, far), expo, stats, values, fars)
+    a3, a2, stats = lax.optimization_barrier((a3, a2, stats))
+    b3, b2 = send(a3, 3 * PLANE), send(a2, 2 * PLANE)
+    a1, a0 = late(total, tok, (1, 0), (r1, q0), (near, near), expo, stats, values, fars)
+    a1, b2, b3 = lax.optimization_barrier((a1, b2, b3))
+    own = (a0, send(a1, PLANE), b2, b3)
     return mix(own, [swap(item) for item in own], w_out, w_other)
 
 

time: 45.4 us -> 45.6 us (level)
  waiting for transfers between devices: 12.6 us -> 15.1 us
  Pallas kernels: 12.9 us -> 11.2 us
  starting transfers between devices: 18.7 us -> 17.8 us
    ppermute x12, waiting for transfers between devices: 11.8 us -> 13.9 us  [send(): return lax.ppermute(array, 'seq', [(i, i ^ bits) for i in range(owners)])]
    pallas_call x5 -> x3, Pallas kernels: 9.55 us -> 7.8 us  [the longest x2 5.23 us: late(): pl.pallas_call(functools.partial(late_kernel, total, tok, items, len(sour...]
    ppermute x12, starting transfers between devices: 17.6 us -> 16.8 us  [send(): return lax.ppermute(array, 'seq', [(i, i ^ bits) for i in range(owners)])]
  transfers between devices with their start and end apart: 17 -> 17, of which waited for: 10 -> 8; matrix products, arithmetic and copies ran while one was open for 0% -> 0% of each run, Pallas kernels for 20% -> 16%
where the time goes in v4:
time: 45.6 us; the launch traced here: 45.4 us
  starting transfers between devices  17.8 us (39%)
  waiting for transfers between devices  15.1 us (33%)
  Pallas kernels  11.2 us (25%)
  local copies, waits for them, and re-layouts  1.34 us (3%)
    ppermute x12, starting transfers between devices, send(): return lax.ppermute(array, 'seq', [(i, i ^ bits) for i in range(owners)])  16.8 us
    ppermute x12, waiting for transfers between devices, send(): return lax.ppermute(array, 'seq', [(i, i ^ bits) for i in range(owners)])  13.9 us
    pallas_call x2, Pallas kernels, late(): pl.pallas_call(functools.partial(late_kernel, total, tok, items, len(sour...  5.23 us
    pallas_call x1, Pallas kernels, project(): pl.pallas_call(functools.partial(project_kernel, steps), out_shape=tuple(...  2.57 us
    pallas_call x1, Pallas kernels, early(): pl.pallas_call(functools.partial(early_kernel, total, tok, len(sources)),...  2.21 us
    unnamed x6, local copies, waits for them, and re-layouts  1.34 us
    ppermute x5, waiting for transfers between devices, swap(): return lax.ppermute(array, 'head', [(0, 1), (1, 0)])  1.2 us
    pallas_call x1, Pallas kernels, mix(): pl.pallas_call(mix_kernel, out_shape=jax.ShapeDtypeStruct((rows, width),...  1.14 us
  transfers between devices with their start and end apart: 17, of which 8 were waited for; matrix products, arithmetic and copies ran while one was open for 0% of the time, Pallas kernels for 16%

profile of v4, /device:TPU:0, one launch (start us, length us, event | category | flops | bytes accessed | tf_op | source)
XLA Modules:
  0.0 45.4 jit_solution(15684547737782162692)
XLA Ops:
  0.0 0.5 collective-permute-start.1
  0.5 0.0 copy-start.1
  0.5 0.7 %copy-done.1 = s32[2,128]{1,0:T(2,128)S(1)} copy-done((s32[2,128]{1,0:T(2,128)S(1)}, s32[2,128]{1,0:T(2,128)}, u32[]{:S(2)}) %copy-start.1) | copy-done | bytes 1048
  1.1 0.0 copy-start.2
  1.1 0.7 %copy-done.2 = s32[128]{0:T(128)S(1)} copy-done((s32[128]{0:T(128)S(1)}, s32[128]{0:T(128)}, u32[]{:S(2)}) %copy-start.2) | copy-done | bytes 536
  1.8 2.6 %project.1 = (bf16[200,256]{1,0:T(8,128)(2,1)S(1)}, bf16[136,256]{1,0:T(8,128)(2,1)S(1)}, bf16[64,256]{1,0:T(8,128)(2,1)S(1)}, bf16[200,256]{1,0:T(8,128)(2,1)S(1)}, bf16[200,256]{1,0:T(8,128)(2,1)S(1)}) custom-call(bf16[128,1024]{1,0:T(8,128)(2,1)} %tok_hbm.1, s32[1,128]{1,0:T(1,128)S(1)} %bitcast.1, s32[2,128]{1,0:T(2,128)S(1)} %copy-done.1, ...), custom_call_target="tpu_custom_call" | custom-call | flops 402653184 | bytes 3145728 | tf_op jit(solution)/shard_map/project/pallas_call | solution.py:77
  4.4 2.6 %collective-permute-start = (bf16[200,256]{1,0:T(8,128)(2,1)S(1)}, bf16[200,256]{1,0:T(8,128)(2,1)S(1)}, u32[]{:S(2)}, u32[]{:S(2)}) collective-permute-start(bf16[200,256]{1,0:T(8,128)(2,1)S(1)} %get-tuple-element.27), channel_id=1, source_target_pairs={{0,8},{2,10},{4,12},{6,14},{8,0},{10,2},{12,4},{14,6},{16,24},{18,... | collective-permute-start | bytes 307208 | tf_op jit(solution)/shard_map/ppermute | solution.py:303
  7.0 2.6 %collective-permute-start.2 = (bf16[200,256]{1,0:T(8,128)(2,1)S(1)}, bf16[200,256]{1,0:T(8,128)(2,1)S(1)}, u32[]{:S(2)}, u32[]{:S(2)}) collective-permute-start(bf16[200,256]{1,0:T(8,128)(2,1)S(1)} %get-tuple-element.31), channel_id=1, source_target_pairs={{0,16},{2,18},{4,20},{6,22},{8,24},{10,26},{12,28},{14,30},{16,0},... | collective-permute-start | bytes 307208 | tf_op jit(solution)/shard_map/ppermute | solution.py:303
  9.6 0.0 collective-permute-start.3
  9.6 0.0 collective-permute-done.1.refs_9_
  9.6 1.0 %collective-permute-done.second_ref.refs_1_.refs_0_ = bf16[200,256]{1,0:T(8,128)(2,1)S(1)} collective-permute-done((bf16[200,256]{1,0:T(8,128)(2,1)S(1)}, bf16[200,256]{1,0:T(8,128)(2,1)S(1)}, u32[]{:S(2)}, u32[]{:S(2)}) %collective-permute-start) | collective-permute-done | bytes 102432 | tf_op jit(solution)/shard_map/ppermute | solution.py:303
  10.6 2.7 %collective-permute-start.4 = (bf16[272,256]{1,0:T(8,128)(2,1)S(1)}, bf16[272,256]{1,0:T(8,128)(2,1)S(1)}, u32[]{:S(2)}, u32[]{:S(2)}) collective-permute-start(bf16[272,256]{1,0:T(8,128)(2,1)S(1)} %pack.2.refs_4_.refs_2_.refs_3_), channel_id=1, source_target_pairs={{0,6},{2,4},{4,2},{6,0},{8,14},{10,12},{12,10},{14,8},{16,22},{18,... | collective-permute-start | bytes 417800 | tf_op jit(solution)/shard_map/ppermute | solution.py:303
  13.2 0.5 %collective-permute-start.5 = (bf16[272,256]{1,0:T(8,128)(2,1)S(1)}, bf16[272,256]{1,0:T(8,128)(2,1)S(1)}, u32[]{:S(2)}, u32[]{:S(2)}) collective-permute-start(bf16[272,256]{1,0:T(8,128)(2,1)S(1)} %pack.2.refs_4_.refs_2_.refs_3_), channel_id=1, source_target_pairs={{0,2},{2,0},{4,6},{6,4},{8,10},{10,8},{12,14},{14,12},{16,18},{18,... | collective-permute-start | bytes 417800 | tf_op jit(solution)/shard_map/ppermute | solution.py:303
  13.8 0.3 collective-permute-start.6
  14.1 3.9 %collective-permute-done.2.first_ref.refs_2_.refs_1_ = bf16[200,256]{1,0:T(8,128)(2,1)S(1)} collective-permute-done((bf16[200,256]{1,0:T(8,128)(2,1)S(1)}, bf16[200,256]{1,0:T(8,128)(2,1)S(1)}, u32[]{:S(2)}, u32[]{:S(2)}) %collective-permute-start.2) | collective-permute-done | bytes 102432 | tf_op jit(solution)/shard_map/ppermute | solution.py:303
  18.0 0.0 collective-permute-done.3.second_ref.refs_3_.refs_0_
  18.0 0.1 collective-permute-done.4.refs_8_
  18.1 1.7 %collective-permute-start.7 = (bf16[272,256]{1,0:T(8,128)(2,1)S(1)}, bf16[272,256]{1,0:T(8,128)(2,1)S(1)}, u32[]{:S(2)}, u32[]{:S(2)}) collective-permute-start(bf16[272,256]{1,0:T(8,128)(2,1)S(1)} %pack.3.refs_5_.refs_2_.refs_3_), channel_id=1, source_target_pairs={{0,2},{2,0},{4,6},{6,4},{8,10},{10,8},{12,14},{14,12},{16,18},{18,... | collective-permute-start | bytes 417800 | tf_op jit(solution)/shard_map/ppermute | solution.py:303
  19.8 1.5 %collective-permute-start.8 = (bf16[272,256]{1,0:T(8,128)(2,1)S(1)}, bf16[272,256]{1,0:T(8,128)(2,1)S(1)}, u32[]{:S(2)}, u32[]{:S(2)}) collective-permute-start(bf16[272,256]{1,0:T(8,128)(2,1)S(1)} %pack.3.refs_5_.refs_2_.refs_3_), channel_id=1, source_target_pairs={{0,4},{2,6},{4,0},{6,2},{8,12},{10,14},{12,8},{14,10},{16,20},{18,... | collective-permute-start | bytes 417800 | tf_op jit(solution)/shard_map/ppermute | solution.py:303
  21.3 0.3 collective-permute-start.9
  21.6 0.0 collective-permute-done.5.refs_6_
  21.6 0.0 collective-permute-done.6.refs_7_
  21.6 2.2 %early.1 = (f32[1024,1280]{1,0:T(8,128)S(1)}, f32[1024,128]{1,0:T(8,128)S(1)}, bf16[1280,128]{1,0:T(8,128)(2,1)S(1)}) custom-call(bf16[64,256]{1,0:T(8,128)(2,1)S(1)} %get-tuple-element.28.refs_0_.refs_1_, bf16[200,256]{1,0:T(8,128)(2,1)S(1)} %collective-permute-done.second_ref.refs_1_.refs_0_, ...), custom_call_target="tpu_custom_call" | custom-call | flops 8000000000 | bytes 1310720 | tf_op jit(solution)/shard_map/early/pallas_call | solution.py:187
  23.8 0.5 %collective-permute-done.7.refs_7_ = bf16[272,256]{1,0:T(8,128)(2,1)S(1)} collective-permute-done((bf16[272,256]{1,0:T(8,128)(2,1)S(1)}, bf16[272,256]{1,0:T(8,128)(2,1)S(1)}, u32[]{:S(2)}, u32[]{:S(2)}) %collective-permute-start.7) | collective-permute-done | bytes 139296 | tf_op jit(solution)/shard_map/ppermute | solution.py:303
  24.3 3.3 %collective-permute-done.8.refs_8_ = bf16[272,256]{1,0:T(8,128)(2,1)S(1)} collective-permute-done((bf16[272,256]{1,0:T(8,128)(2,1)S(1)}, bf16[272,256]{1,0:T(8,128)(2,1)S(1)}, u32[]{:S(2)}, u32[]{:S(2)}) %collective-permute-start.8) | collective-permute-done | bytes 139296 | tf_op jit(solution)/shard_map/ppermute | solution.py:303
  27.6 0.0 collective-permute-done.9.refs_9_
  27.6 2.6 %late.2 = (bf16[128,128]{1,0:T(8,128)(2,1)S(1)}, bf16[128,128]{1,0:T(8,128)(2,1)S(1)}) custom-call(bf16[200,256]{1,0:T(8,128)(2,1)S(1)} %collective-permute-done.3.second_ref.refs_3_.refs_0_, bf16[200,256]{1,0:T(8,128)(2,1)S(1)} %collective-permute-done.2.first_ref.refs_2_.refs_1_, bf16[272,256]{1,0:T(8,128)(2,1)S(1)} %pack.3.refs_5_.refs_2_.refs_3_, ...), custom_call_target="tpu_custom_call" | custom-call | flops 3000000000 | bytes 393216 | tf_op jit(solution)/shard_map/late/pallas_call | solution.py:243
  30.2 0.0 copy-start
  30.3 3.2 %collective-permute-start.10 = (bf16[128,128]{1,0:T(8,128)(2,1)S(1)}, bf16[128,128]{1,0:T(8,128)(2,1)S(1)}, u32[]{:S(2)}, u32[]{:S(2)}) collective-permute-start(bf16[128,128]{1,0:T(8,128)(2,1)S(1)} %get-tuple-element.43), channel_id=1, source_target_pairs={{0,16},{2,18},{4,20},{6,22},{8,24},{10,26},{12,28},{14,30},{16,0},... | collective-permute-start | bytes 98312 | tf_op jit(solution)/shard_map/ppermute | solution.py:303
  33.4 1.3 %collective-permute-start.11 = (bf16[128,128]{1,0:T(8,128)(2,1)S(1)}, bf16[128,128]{1,0:T(8,128)(2,1)S(1)}, u32[]{:S(2)}, u32[]{:S(2)}) collective-permute-start(bf16[128,128]{1,0:T(8,128)(2,1)S(1)} %get-tuple-element.44), channel_id=1, source_target_pairs={{0,24},{2,26},{4,28},{6,30},{8,16},{10,18},{12,20},{14,22},{16,8},... | collective-permute-start | bytes 98312 | tf_op jit(solution)/shard_map/ppermute | solution.py:303
  34.8 2.6 %late.3 = (bf16[128,128]{1,0:T(8,128)(2,1)S(1)}, bf16[128,128]{1,0:T(8,128)(2,1)S(1)}) custom-call(bf16[200,256]{1,0:T(8,128)(2,1)S(1)} %collective-permute-done.second_ref.refs_1_.refs_0_, bf16[64,256]{1,0:T(8,128)(2,1)S(1)} %get-tuple-element.28.refs_0_.refs_1_, bf16[272,256]{1,0:T(8,128)(2,1)S(1)} %pack.2.refs_4_.refs_2_.refs_3_, ...), custom_call_target="tpu_custom_call" | custom-call | flops 3000000000 | bytes 393216 | tf_op jit(solution)/shard_map/late/pallas_call | solution.py:243
  37.4 0.0 collective-permute-done.10.refs_2_
  37.4 1.8 %collective-permute-done.11.refs_3_ = bf16[128,128]{1,0:T(8,128)(2,1)S(1)} collective-permute-done((bf16[128,128]{1,0:T(8,128)(2,1)S(1)}, bf16[128,128]{1,0:T(8,128)(2,1)S(1)}, u32[]{:S(2)}, u32[]{:S(2)}) %collective-permute-start.11) | collective-permute-done | bytes 32800 | tf_op jit(solution)/shard_map/ppermute | solution.py:303
  39.2 0.0 collective-permute-start.12
  39.2 0.0 collective-permute-start.13
  39.2 0.5 %collective-permute-start.15 = (bf16[128,128]{1,0:T(8,128)(2,1)S(1)}, bf16[128,128]{1,0:T(8,128)(2,1)S(1)}, u32[]{:S(2)}, u32[]{:S(2)}) collective-permute-start(bf16[128,128]{1,0:T(8,128)(2,1)S(1)} %collective-permute-done.10.refs_2_), channel_id=1, source_target_pairs={{0,1},{1,0},{2,3},{3,2},{4,5},{5,4},{6,7},{7,6},{8,9},{9,8},{10,11... | collective-permute-start | bytes 98312 | tf_op jit(solution)/shard_map/ppermute | solution.py:306
  39.7 0.0 collective-permute-start.16
  39.7 3.4 %collective-permute-done.12.refs_1_ = bf16[128,128]{1,0:T(8,128)(2,1)S(1)} collective-permute-done((bf16[128,128]{1,0:T(8,128)(2,1)S(1)}, bf16[128,128]{1,0:T(8,128)(2,1)S(1)}, u32[]{:S(2)}, u32[]{:S(2)}) %collective-permute-start.12) | collective-permute-done | bytes 32800 | tf_op jit(solution)/shard_map/ppermute | solution.py:303
  43.1 0.0 collective-permute-start.14
  43.1 0.0 collective-permute-done.13.refs_4_
  43.1 0.0 collective-permute-done.15.refs_6_
  43.1 0.0 collective-permute-done.16.refs_7_
  43.1 1.2 %collective-permute-done.14.refs_5_ = bf16[128,128]{1,0:T(8,128)(2,1)S(1)} collective-permute-done((bf16[128,128]{1,0:T(8,128)(2,1)S(1)}, bf16[128,128]{1,0:T(8,128)(2,1)S(1)}, u32[]{:S(2)}, u32[]{:S(2)}) %collective-permute-start.14) | collective-permute-done | bytes 32800 | tf_op jit(solution)/shard_map/ppermute | solution.py:306
  44.3 0.0 copy-done
  44.3 1.1 %mix.1 = bf16[64,1024]{1,0:T(8,128)(2,1)} custom-call(bf16[128,128]{1,0:T(8,128)(2,1)S(1)} %get-tuple-element.41.refs_0_, bf16[128,128]{1,0:T(8,128)(2,1)S(1)} %collective-permute-done.12.refs_1_, bf16[128,128]{1,0:T(8,128)(2,1)S(1)} %collective-permute-done.10.refs_2_, bf16[128,128]{1,0:T(8,128)(2,1)S(1)} %collective-permute-done.11.refs_3_, ...), custom_call_target="tpu_custom_call" | custom-call | flops 134217728 | bytes 2097152 | tf_op jit(solution)/shard_map/mix/pallas_call | solution.py:283
  (2 shorter events, 0.0 us)
Async XLA Ops:
  0.0 9.6 %collective-permute-start.1 = (bf16[512,1024]{1,0:T(8,128)(2,1)}, bf16[512,1024]{1,0:T(8,128)(2,1)S(1)}, u32[]{:S(2)}, u32[]{:S(2)}) collective-permute-start(bf16[512,1024]{1,0:T(8,128)(2,1)} %refs_8_.1), channel_id=1, source_target_pairs={{0,1},{1,0},{2,3},{3,2},{4,5},{5,4},{6,7},{7,6},{8,9},{9,8},{10,11... | collective-permute-start | bytes 3145736 | tf_op jit(solution)/shard_map/ppermute | solution.py:306
  0.5 0.7 %copy-start.1 = (s32[2,128]{1,0:T(2,128)S(1)}, s32[2,128]{1,0:T(2,128)}, u32[]{:S(2)}) copy-start(s32[2,128]{1,0:T(2,128)} %cid_hbm.1) | copy-start | bytes 3076
  1.1 0.7 %copy-start.2 = (s32[128]{0:T(128)S(1)}, s32[128]{0:T(128)}, u32[]{:S(2)}) copy-start(s32[128]{0:T(128)} %param.13) | copy-start | bytes 1540
  4.4 6.2 %collective-permute-start = (bf16[200,256]{1,0:T(8,128)(2,1)S(1)}, bf16[200,256]{1,0:T(8,128)(2,1)S(1)}, u32[]{:S(2)}, u32[]{:S(2)}) collective-permute-start(bf16[200,256]{1,0:T(8,128)(2,1)S(1)} %get-tuple-element.27), channel_id=1, source_target_pairs={{0,8},{2,10},{4,12},{6,14},{8,0},{10,2},{12,4},{14,6},{16,24},{18,... | collective-permute-start | bytes 307208 | tf_op jit(solution)/shard_map/ppermute | solution.py:303
  7.0 11.0 %collective-permute-start.2 = (bf16[200,256]{1,0:T(8,128)(2,1)S(1)}, bf16[200,256]{1,0:T(8,128)(2,1)S(1)}, u32[]{:S(2)}, u32[]{:S(2)}) collective-permute-start(bf16[200,256]{1,0:T(8,128)(2,1)S(1)} %get-tuple-element.31), channel_id=1, source_target_pairs={{0,16},{2,18},{4,20},{6,22},{8,24},{10,26},{12,28},{14,30},{16,0},... | collective-permute-start | bytes 307208 | tf_op jit(solution)/shard_map/ppermute | solution.py:303
  9.6 8.4 %collective-permute-start.3 = (bf16[200,256]{1,0:T(8,128)(2,1)S(1)}, bf16[200,256]{1,0:T(8,128)(2,1)S(1)}, u32[]{:S(2)}, u32[]{:S(2)}) collective-permute-start(bf16[200,256]{1,0:T(8,128)(2,1)S(1)} %get-tuple-element.32), channel_id=1, source_target_pairs={{0,24},{2,26},{4,28},{6,30},{8,16},{10,18},{12,20},{14,22},{16,8},... | collective-permute-start | bytes 307208 | tf_op jit(solution)/shard_map/ppermute | solution.py:303
  10.6 7.5 %collective-permute-start.4 = (bf16[272,256]{1,0:T(8,128)(2,1)S(1)}, bf16[272,256]{1,0:T(8,128)(2,1)S(1)}, u32[]{:S(2)}, u32[]{:S(2)}) collective-permute-start(bf16[272,256]{1,0:T(8,128)(2,1)S(1)} %pack.2.refs_4_.refs_2_.refs_3_), channel_id=1, source_target_pairs={{0,6},{2,4},{4,2},{6,0},{8,14},{10,12},{12,10},{14,8},{16,22},{18,... | collective-permute-start | bytes 417800 | tf_op jit(solution)/shard_map/ppermute | solution.py:303
  13.2 8.3 %collective-permute-start.5 = (bf16[272,256]{1,0:T(8,128)(2,1)S(1)}, bf16[272,256]{1,0:T(8,128)(2,1)S(1)}, u32[]{:S(2)}, u32[]{:S(2)}) collective-permute-start(bf16[272,256]{1,0:T(8,128)(2,1)S(1)} %pack.2.refs_4_.refs_2_.refs_3_), channel_id=1, source_target_pairs={{0,2},{2,0},{4,6},{6,4},{8,10},{10,8},{12,14},{14,12},{16,18},{18,... | collective-permute-start | bytes 417800 | tf_op jit(solution)/shard_map/ppermute | solution.py:303
  13.8 7.8 %collective-permute-start.6 = (bf16[272,256]{1,0:T(8,128)(2,1)S(1)}, bf16[272,256]{1,0:T(8,128)(2,1)S(1)}, u32[]{:S(2)}, u32[]{:S(2)}) collective-permute-start(bf16[272,256]{1,0:T(8,128)(2,1)S(1)} %pack.2.refs_4_.refs_2_.refs_3_), channel_id=1, source_target_pairs={{0,4},{2,6},{4,0},{6,2},{8,12},{10,14},{12,8},{14,10},{16,20},{18,... | collective-permute-start | bytes 417800 | tf_op jit(solution)/shard_map/ppermute | solution.py:303
  18.1 6.2 %collective-permute-start.7 = (bf16[272,256]{1,0:T(8,128)(2,1)S(1)}, bf16[272,256]{1,0:T(8,128)(2,1)S(1)}, u32[]{:S(2)}, u32[]{:S(2)}) collective-permute-start(bf16[272,256]{1,0:T(8,128)(2,1)S(1)} %pack.3.refs_5_.refs_2_.refs_3_), channel_id=1, source_target_pairs={{0,2},{2,0},{4,6},{6,4},{8,10},{10,8},{12,14},{14,12},{16,18},{18,... | collective-permute-start | bytes 417800 | tf_op jit(solution)/shard_map/ppermute | solution.py:303
  19.8 7.8 %collective-permute-start.8 = (bf16[272,256]{1,0:T(8,128)(2,1)S(1)}, bf16[272,256]{1,0:T(8,128)(2,1)S(1)}, u32[]{:S(2)}, u32[]{:S(2)}) collective-permute-start(bf16[272,256]{1,0:T(8,128)(2,1)S(1)} %pack.3.refs_5_.refs_2_.refs_3_), channel_id=1, source_target_pairs={{0,4},{2,6},{4,0},{6,2},{8,12},{10,14},{12,8},{14,10},{16,20},{18,... | collective-permute-start | bytes 417800 | tf_op jit(solution)/shard_map/ppermute | solution.py:303
  21.3 6.3 %collective-permute-start.9 = (bf16[272,256]{1,0:T(8,128)(2,1)S(1)}, bf16[272,256]{1,0:T(8,128)(2,1)S(1)}, u32[]{:S(2)}, u32[]{:S(2)}) collective-permute-start(bf16[272,256]{1,0:T(8,128)(2,1)S(1)} %pack.3.refs_5_.refs_2_.refs_3_), channel_id=1, source_target_pairs={{0,6},{2,4},{4,2},{6,0},{8,14},{10,12},{12,10},{14,8},{16,22},{18,... | collective-permute-start | bytes 417800 | tf_op jit(solution)/shard_map/ppermute | solution.py:303
  30.2 14.0 %copy-start = (bf16[512,1024]{1,0:T(8,128)(2,1)S(1)}, bf16[512,1024]{1,0:T(8,128)(2,1)}, u32[]{:S(2)}) copy-start(bf16[512,1024]{1,0:T(8,128)(2,1)} %refs_8_.1) | copy-start | bytes 3145732
  30.3 7.1 %collective-permute-start.10 = (bf16[128,128]{1,0:T(8,128)(2,1)S(1)}, bf16[128,128]{1,0:T(8,128)(2,1)S(1)}, u32[]{:S(2)}, u32[]{:S(2)}) collective-permute-start(bf16[128,128]{1,0:T(8,128)(2,1)S(1)} %get-tuple-element.43), channel_id=1, source_target_pairs={{0,16},{2,18},{4,20},{6,22},{8,24},{10,26},{12,28},{14,30},{16,0},... | collective-permute-start | bytes 98312 | tf_op jit(solution)/shard_map/ppermute | solution.py:303
  33.4 5.7 %collective-permute-start.11 = (bf16[128,128]{1,0:T(8,128)(2,1)S(1)}, bf16[128,128]{1,0:T(8,128)(2,1)S(1)}, u32[]{:S(2)}, u32[]{:S(2)}) collective-permute-start(bf16[128,128]{1,0:T(8,128)(2,1)S(1)} %get-tuple-element.44), channel_id=1, source_target_pairs={{0,24},{2,26},{4,28},{6,30},{8,16},{10,18},{12,20},{14,22},{16,8},... | collective-permute-start | bytes 98312 | tf_op jit(solution)/shard_map/ppermute | solution.py:303
  39.2 3.9 %collective-permute-start.12 = (bf16[128,128]{1,0:T(8,128)(2,1)S(1)}, bf16[128,128]{1,0:T(8,128)(2,1)S(1)}, u32[]{:S(2)}, u32[]{:S(2)}) collective-permute-start(bf16[128,128]{1,0:T(8,128)(2,1)S(1)} %get-tuple-element.45), channel_id=1, source_target_pairs={{0,8},{2,10},{4,12},{6,14},{8,0},{10,2},{12,4},{14,6},{16,24},{18,... | collective-permute-start | bytes 98312 | tf_op jit(solution)/shard_map/ppermute | solution.py:303
  39.2 3.9 %collective-permute-start.13 = (bf16[128,128]{1,0:T(8,128)(2,1)S(1)}, bf16[128,128]{1,0:T(8,128)(2,1)S(1)}, u32[]{:S(2)}, u32[]{:S(2)}) collective-permute-start(bf16[128,128]{1,0:T(8,128)(2,1)S(1)} %get-tuple-element.41.refs_0_), channel_id=1, source_target_pairs={{0,1},{1,0},{2,3},{3,2},{4,5},{5,4},{6,7},{7,6},{8,9},{9,8},{10,11... | collective-permute-start | bytes 98312 | tf_op jit(solution)/shard_map/ppermute | solution.py:306
  39.2 3.9 %collective-permute-start.15 = (bf16[128,128]{1,0:T(8,128)(2,1)S(1)}, bf16[128,128]{1,0:T(8,128)(2,1)S(1)}, u32[]{:S(2)}, u32[]{:S(2)}) collective-permute-start(bf16[128,128]{1,0:T(8,128)(2,1)S(1)} %collective-permute-done.10.refs_2_), channel_id=1, source_target_pairs={{0,1},{1,0},{2,3},{3,2},{4,5},{5,4},{6,7},{7,6},{8,9},{9,8},{10,11... | collective-permute-start | bytes 98312 | tf_op jit(solution)/shard_map/ppermute | solution.py:306
  39.7 3.4 %collective-permute-start.16 = (bf16[128,128]{1,0:T(8,128)(2,1)S(1)}, bf16[128,128]{1,0:T(8,128)(2,1)S(1)}, u32[]{:S(2)}, u32[]{:S(2)}) collective-permute-start(bf16[128,128]{1,0:T(8,128)(2,1)S(1)} %collective-permute-done.11.refs_3_), channel_id=1, source_target_pairs={{0,1},{1,0},{2,3},{3,2},{4,5},{5,4},{6,7},{7,6},{8,9},{9,8},{10,11... | collective-permute-start | bytes 98312 | tf_op jit(solution)/shard_map/ppermute | solution.py:306
  43.1 1.2 %collective-permute-start.14 = (bf16[128,128]{1,0:T(8,128)(2,1)S(1)}, bf16[128,128]{1,0:T(8,128)(2,1)S(1)}, u32[]{:S(2)}, u32[]{:S(2)}) collective-permute-start(bf16[128,128]{1,0:T(8,128)(2,1)S(1)} %collective-permute-done.12.refs_1_), channel_id=1, source_target_pairs={{0,1},{1,0},{2,3},{3,2},{4,5},{5,4},{6,7},{7,6},{8,9},{9,8},{10,11... | collective-permute-start | bytes 98312 | tf_op jit(solution)/shard_map/ppermute | solution.py:306

commit v5 on v4

--- a/solution.py
+++ b/solution.py
@@ -94,7 +94,7 @@
             transcendentals=0,
         ),
         name="project",
-    )(tokens, positions.reshape(1, tok), cluster_ids, *weights)
+    )(tokens, *(pltpu.with_memory_space_constraint(x, pltpu.HBM) for x in (positions.reshape(1, tok), cluster_ids)), *weights)
 
 
 def pack_kernel(first_ref, second_ref, out_ref):
@@ -317,12 +317,15 @@
     fars = [send(far, bits) for bits in (1, 2, 3)]
     total = owners * tok
     expo, stats, values = early(total, tok, (q0, r1, r2, r3), [near, far, *nears])
-    a3, a2 = late(total, tok, (3, 2), (r3, r2), (far, far), expo, stats, values, fars)
-    a3, a2, stats = lax.optimization_barrier((a3, a2, stats))
-    b3, b2 = send(a3, 3 * PLANE), send(a2, 2 * PLANE)
-    a1, a0 = late(total, tok, (1, 0), (r1, q0), (near, near), expo, stats, values, fars)
-    a1, b2, b3 = lax.optimization_barrier((a1, b2, b3))
-    own = (a0, send(a1, PLANE), b2, b3)
+    queries, own = (q0, r1, r2, r3), [None] * SPLIT
+    for item in (3, 2, 1, 0):
+        ids = near if item < 2 else far
+        (part,) = late(total, tok, (item,), (queries[item],), (ids,), expo, stats, values, fars)
+        part, stats = lax.optimization_barrier((part, stats))
+        own[item] = part
+    own[3], own[2] = lax.optimization_barrier((own[3], own[2]))
+    b3 = send(own[3], 3 * PLANE)
+    own = (own[0], send(own[1], PLANE), send(own[2], 2 * PLANE), b3)
     return mix(own, [swap(item) for item in own], w_out, w_other)
 
 

time: 45.6 us -> 41.9 us (0.919)
  waiting for transfers between devices: 15.1 us -> 11.5 us
  local copies, waits for them, and re-layouts: 1.34 us -> 0.01 us
  Pallas kernels: 11.2 us -> 12 us
  starting transfers between devices: 17.8 us -> 18.3 us
    ppermute x12, waiting for transfers between devices: 13.9 us -> 10.3 us  [send(): return lax.ppermute(array, 'seq', [(i, i ^ bits) for i in range(owners)])]
    unnamed x6 -> x2, local copies, waits for them, and re-layouts: 1.34 us -> 0.01 us
    pallas_call x1, Pallas kernels: 2.57 us -> 3.1 us  [project(): pl.pallas_call(functools.partial(project_kernel, steps), out_shape=tuple(...]
    ppermute x12, starting transfers between devices: 16.8 us -> 17.3 us  [send(): return lax.ppermute(array, 'seq', [(i, i ^ bits) for i in range(owners)])]
    pallas_call x2 -> x4, Pallas kernels: 5.23 us -> 5.48 us  [late(): pl.pallas_call(functools.partial(late_kernel, total, tok, items, len(sour...]
  transfers between devices with their start and end apart: 17 -> 17, of which waited for: 8 -> 9; matrix products, arithmetic and copies ran while one was open for 0% -> 0% of each run, Pallas kernels for 16% -> 19%
where the time goes in v5:
time: 41.9 us; the launch traced here: 41.8 us
  starting transfers between devices  18.3 us (44%)
  Pallas kernels  12 us (29%)
  waiting for transfers between devices  11.5 us (27%)
    ppermute x12, starting transfers between devices, send(): return lax.ppermute(array, 'seq', [(i, i ^ bits) for i in range(owners)])  17.3 us
    ppermute x12, waiting for transfers between devices, send(): return lax.ppermute(array, 'seq', [(i, i ^ bits) for i in range(owners)])  10.3 us
    pallas_call x4, Pallas kernels, late(): pl.pallas_call(functools.partial(late_kernel, total, tok, items, len(sour...  5.48 us
    pallas_call x1, Pallas kernels, project(): pl.pallas_call(functools.partial(project_kernel, steps), out_shape=tuple(...  3.1 us
    pallas_call x1, Pallas kernels, early(): pl.pallas_call(functools.partial(early_kernel, total, tok, len(sources)),...  2.21 us
    ppermute x5, waiting for transfers between devices, swap(): return lax.ppermute(array, 'head', [(0, 1), (1, 0)])  1.2 us
    pallas_call x1, Pallas kernels, mix(): pl.pallas_call(mix_kernel, out_shape=jax.ShapeDtypeStruct((rows, width),...  1.14 us
    ppermute x5, starting transfers between devices, swap(): return lax.ppermute(array, 'head', [(0, 1), (1, 0)])  1.02 us
  transfers between devices with their start and end apart: 17, of which 9 were waited for; matrix products, arithmetic and copies ran while one was open for 0% of the time, Pallas kernels for 19%

profile of v5, /device:TPU:0, one launch (start us, length us, event | category | flops | bytes accessed | tf_op | source)
XLA Modules:
  0.0 41.8 jit_solution(5899972920812369057)
XLA Ops:
  0.0 0.5 %collective-permute-start = (bf16[512,1024]{1,0:T(8,128)(2,1)}, bf16[512,1024]{1,0:T(8,128)(2,1)S(1)}, u32[]{:S(2)}, u32[]{:S(2)}) collective-permute-start(bf16[512,1024]{1,0:T(8,128)(2,1)} %refs_8_.1), channel_id=1, source_target_pairs={{0,1},{1,0},{2,3},{3,2},{4,5},{5,4},{6,7},{7,6},{8,9},{9,8},{10,11... | collective-permute-start | bytes 3145736 | tf_op jit(solution)/shard_map/ppermute | solution.py:306
  0.5 3.1 %project.1 = (bf16[200,256]{1,0:T(8,128)(2,1)S(1)}, bf16[136,256]{1,0:T(8,128)(2,1)S(1)}, bf16[64,256]{1,0:T(8,128)(2,1)S(1)}, bf16[200,256]{1,0:T(8,128)(2,1)S(1)}, bf16[200,256]{1,0:T(8,128)(2,1)S(1)}) custom-call(bf16[128,1024]{1,0:T(8,128)(2,1)} %tok_hbm.1, s32[1,128]{1,0:T(1,128)} %bitcast.1, s32[2,128]{1,0:T(2,128)} %cid_hbm.1, ...), custom_call_target="tpu_custom_call" | custom-call | flops 402653184 | bytes 3145728 | tf_op jit(solution)/shard_map/project/pallas_call | solution.py:77
  3.6 2.6 %collective-permute-start.1 = (bf16[200,256]{1,0:T(8,128)(2,1)S(1)}, bf16[200,256]{1,0:T(8,128)(2,1)S(1)}, u32[]{:S(2)}, u32[]{:S(2)}) collective-permute-start(bf16[200,256]{1,0:T(8,128)(2,1)S(1)} %get-tuple-element.29), channel_id=1, source_target_pairs={{0,8},{2,10},{4,12},{6,14},{8,0},{10,2},{12,4},{14,6},{16,24},{18,... | collective-permute-start | bytes 307208 | tf_op jit(solution)/shard_map/ppermute | solution.py:303
  6.2 2.6 %collective-permute-start.2 = (bf16[200,256]{1,0:T(8,128)(2,1)S(1)}, bf16[200,256]{1,0:T(8,128)(2,1)S(1)}, u32[]{:S(2)}, u32[]{:S(2)}) collective-permute-start(bf16[200,256]{1,0:T(8,128)(2,1)S(1)} %get-tuple-element.30), channel_id=1, source_target_pairs={{0,16},{2,18},{4,20},{6,22},{8,24},{10,26},{12,28},{14,30},{16,0},... | collective-permute-start | bytes 307208 | tf_op jit(solution)/shard_map/ppermute | solution.py:303
  8.8 0.0 collective-permute-start.3
  8.8 0.0 collective-permute-done.refs_9_
  8.8 1.0 %collective-permute-done.1.second_ref.refs_1_.refs_0_ = bf16[200,256]{1,0:T(8,128)(2,1)S(1)} collective-permute-done((bf16[200,256]{1,0:T(8,128)(2,1)S(1)}, bf16[200,256]{1,0:T(8,128)(2,1)S(1)}, u32[]{:S(2)}, u32[]{:S(2)}) %collective-permute-start.1) | collective-permute-done | bytes 102432 | tf_op jit(solution)/shard_map/ppermute | solution.py:303
  9.8 2.7 %collective-permute-start.4 = (bf16[272,256]{1,0:T(8,128)(2,1)S(1)}, bf16[272,256]{1,0:T(8,128)(2,1)S(1)}, u32[]{:S(2)}, u32[]{:S(2)}) collective-permute-start(bf16[272,256]{1,0:T(8,128)(2,1)S(1)} %pack.2.refs_4_.refs_1_), channel_id=1, source_target_pairs={{0,6},{2,4},{4,2},{6,0},{8,14},{10,12},{12,10},{14,8},{16,22},{18,... | collective-permute-start | bytes 417800 | tf_op jit(solution)/shard_map/ppermute | solution.py:303
  12.5 0.6 %collective-permute-start.5 = (bf16[272,256]{1,0:T(8,128)(2,1)S(1)}, bf16[272,256]{1,0:T(8,128)(2,1)S(1)}, u32[]{:S(2)}, u32[]{:S(2)}) collective-permute-start(bf16[272,256]{1,0:T(8,128)(2,1)S(1)} %pack.2.refs_4_.refs_1_), channel_id=1, source_target_pairs={{0,2},{2,0},{4,6},{6,4},{8,10},{10,8},{12,14},{14,12},{16,18},{18,... | collective-permute-start | bytes 417800 | tf_op jit(solution)/shard_map/ppermute | solution.py:303
  13.0 0.3 collective-permute-start.6
  13.3 3.9 %collective-permute-done.2.first_ref.refs_2_.refs_0_ = bf16[200,256]{1,0:T(8,128)(2,1)S(1)} collective-permute-done((bf16[200,256]{1,0:T(8,128)(2,1)S(1)}, bf16[200,256]{1,0:T(8,128)(2,1)S(1)}, u32[]{:S(2)}, u32[]{:S(2)}) %collective-permute-start.2) | collective-permute-done | bytes 102432 | tf_op jit(solution)/shard_map/ppermute | solution.py:303
  17.2 0.0 collective-permute-done.3.second_ref.refs_3_.refs_0_
  17.2 0.1 collective-permute-done.4.refs_8_
  17.3 1.7 %collective-permute-start.7 = (bf16[272,256]{1,0:T(8,128)(2,1)S(1)}, bf16[272,256]{1,0:T(8,128)(2,1)S(1)}, u32[]{:S(2)}, u32[]{:S(2)}) collective-permute-start(bf16[272,256]{1,0:T(8,128)(2,1)S(1)} %pack.3.refs_5_.refs_1_), channel_id=1, source_target_pairs={{0,2},{2,0},{4,6},{6,4},{8,10},{10,8},{12,14},{14,12},{16,18},{18,... | collective-permute-start | bytes 417800 | tf_op jit(solution)/shard_map/ppermute | solution.py:303
  19.0 1.5 %collective-permute-start.8 = (bf16[272,256]{1,0:T(8,128)(2,1)S(1)}, bf16[272,256]{1,0:T(8,128)(2,1)S(1)}, u32[]{:S(2)}, u32[]{:S(2)}) collective-permute-start(bf16[272,256]{1,0:T(8,128)(2,1)S(1)} %pack.3.refs_5_.refs_1_), channel_id=1, source_target_pairs={{0,4},{2,6},{4,0},{6,2},{8,12},{10,14},{12,8},{14,10},{16,20},{18,... | collective-permute-start | bytes 417800 | tf_op jit(solution)/shard_map/ppermute | solution.py:303
  20.5 0.3 collective-permute-start.9
  20.8 0.0 collective-permute-done.5.refs_6_
  20.8 0.0 collective-permute-done.6.refs_7_
  20.8 2.2 %early.1 = (f32[1024,1280]{1,0:T(8,128)S(1)}, f32[1024,128]{1,0:T(8,128)S(1)}, bf16[1280,128]{1,0:T(8,128)(2,1)S(1)}) custom-call(bf16[64,256]{1,0:T(8,128)(2,1)S(1)} %get-tuple-element.26.refs_0_, bf16[200,256]{1,0:T(8,128)(2,1)S(1)} %collective-permute-done.1.second_ref.refs_1_.refs_0_, ...), custom_call_target="tpu_custom_call" | custom-call | flops 8000000000 | bytes 1310720 | tf_op jit(solution)/shard_map/early/pallas_call | solution.py:187
  23.0 0.5 %collective-permute-done.7.refs_5_ = bf16[272,256]{1,0:T(8,128)(2,1)S(1)} collective-permute-done((bf16[272,256]{1,0:T(8,128)(2,1)S(1)}, bf16[272,256]{1,0:T(8,128)(2,1)S(1)}, u32[]{:S(2)}, u32[]{:S(2)}) %collective-permute-start.7) | collective-permute-done | bytes 139296 | tf_op jit(solution)/shard_map/ppermute | solution.py:303
  23.5 3.3 %collective-permute-done.8.refs_6_ = bf16[272,256]{1,0:T(8,128)(2,1)S(1)} collective-permute-done((bf16[272,256]{1,0:T(8,128)(2,1)S(1)}, bf16[272,256]{1,0:T(8,128)(2,1)S(1)}, u32[]{:S(2)}, u32[]{:S(2)}) %collective-permute-start.8) | collective-permute-done | bytes 139296 | tf_op jit(solution)/shard_map/ppermute | solution.py:303
  26.8 0.0 collective-permute-done.9.refs_7_
  26.8 1.4 %late.4 = bf16[128,128]{1,0:T(8,128)(2,1)S(1)} custom-call(bf16[200,256]{1,0:T(8,128)(2,1)S(1)} %collective-permute-done.3.second_ref.refs_3_.refs_0_, bf16[272,256]{1,0:T(8,128)(2,1)S(1)} %pack.3.refs_5_.refs_1_, f32[1024,1280]{1,0:T(8,128)S(1)} %get-tuple-element.34.refs_2_, f32[1024,128]{1,0:T(8,128)S(1)} %get-tuple-element.39.refs_3_, ...), custom_call_target="tpu_custom_call" | custom-call | flops 3000000000 | bytes 393216 | tf_op jit(solution)/shard_map/late/pallas_call | solution.py:243
  28.2 1.4 %late.5 = bf16[128,128]{1,0:T(8,128)(2,1)S(1)} custom-call(bf16[200,256]{1,0:T(8,128)(2,1)S(1)} %collective-permute-done.2.first_ref.refs_2_.refs_0_, bf16[272,256]{1,0:T(8,128)(2,1)S(1)} %pack.3.refs_5_.refs_1_, f32[1024,1280]{1,0:T(8,128)S(1)} %get-tuple-element.34.refs_2_, f32[1024,128]{1,0:T(8,128)S(1)} %get-tuple-element.39.refs_3_, ...), custom_call_target="tpu_custom_call" | custom-call | flops 3000000000 | bytes 393216 | tf_op jit(solution)/shard_map/late/pallas_call | solution.py:243
  29.6 3.2 %collective-permute-start.11 = (bf16[128,128]{1,0:T(8,128)(2,1)S(1)}, bf16[128,128]{1,0:T(8,128)(2,1)S(1)}, u32[]{:S(2)}, u32[]{:S(2)}) collective-permute-start(bf16[128,128]{1,0:T(8,128)(2,1)S(1)} %late.5), channel_id=1, source_target_pairs={{0,16},{2,18},{4,20},{6,22},{8,24},{10,26},{12,28},{14,30},{16,0},... | collective-permute-start | bytes 98312 | tf_op jit(solution)/shard_map/ppermute | solution.py:303
  32.8 1.3 %collective-permute-start.12 = (bf16[128,128]{1,0:T(8,128)(2,1)S(1)}, bf16[128,128]{1,0:T(8,128)(2,1)S(1)}, u32[]{:S(2)}, u32[]{:S(2)}) collective-permute-start(bf16[128,128]{1,0:T(8,128)(2,1)S(1)} %late.4), channel_id=1, source_target_pairs={{0,24},{2,26},{4,28},{6,30},{8,16},{10,18},{12,20},{14,22},{16,8},... | collective-permute-start | bytes 98312 | tf_op jit(solution)/shard_map/ppermute | solution.py:303
  34.1 1.4 %late.6 = bf16[128,128]{1,0:T(8,128)(2,1)S(1)} custom-call(bf16[200,256]{1,0:T(8,128)(2,1)S(1)} %collective-permute-done.1.second_ref.refs_1_.refs_0_, bf16[272,256]{1,0:T(8,128)(2,1)S(1)} %pack.2.refs_4_.refs_1_, f32[1024,1280]{1,0:T(8,128)S(1)} %get-tuple-element.34.refs_2_, f32[1024,128]{1,0:T(8,128)S(1)} %get-tuple-element.39.refs_3_, ...), custom_call_target="tpu_custom_call" | custom-call | flops 3000000000 | bytes 393216 | tf_op jit(solution)/shard_map/late/pallas_call | solution.py:243
  35.4 0.0 copy-start
  35.4 0.5 %collective-permute-start.10 = (bf16[128,128]{1,0:T(8,128)(2,1)S(1)}, bf16[128,128]{1,0:T(8,128)(2,1)S(1)}, u32[]{:S(2)}, u32[]{:S(2)}) collective-permute-start(bf16[128,128]{1,0:T(8,128)(2,1)S(1)} %late.6), channel_id=1, source_target_pairs={{0,8},{2,10},{4,12},{6,14},{8,0},{10,2},{12,4},{14,6},{16,24},{18,... | collective-permute-start | bytes 98312 | tf_op jit(solution)/shard_map/ppermute | solution.py:303
  35.9 1.4 %late.7.refs_0_ = bf16[128,128]{1,0:T(8,128)(2,1)S(1)} custom-call(bf16[64,256]{1,0:T(8,128)(2,1)S(1)} %get-tuple-element.26.refs_0_, bf16[272,256]{1,0:T(8,128)(2,1)S(1)} %pack.2.refs_4_.refs_1_, f32[1024,1280]{1,0:T(8,128)S(1)} %get-tuple-element.34.refs_2_, f32[1024,128]{1,0:T(8,128)S(1)} %get-tuple-element.39.refs_3_, ...), custom_call_target="tpu_custom_call" | custom-call | flops 3000000000 | bytes 393216 | tf_op jit(solution)/shard_map/late/pallas_call | solution.py:243
  37.3 0.1 collective-permute-start.13
  37.4 0.0 collective-permute-done.11.refs_2_
  37.4 0.5 %collective-permute-start.15 = (bf16[128,128]{1,0:T(8,128)(2,1)S(1)}, bf16[128,128]{1,0:T(8,128)(2,1)S(1)}, u32[]{:S(2)}, u32[]{:S(2)}) collective-permute-start(bf16[128,128]{1,0:T(8,128)(2,1)S(1)} %collective-permute-done.11.refs_2_), channel_id=1, source_target_pairs={{0,1},{1,0},{2,3},{3,2},{4,5},{5,4},{6,7},{7,6},{8,9},{9,8},{10,11... | collective-permute-start | bytes 98312 | tf_op jit(solution)/shard_map/ppermute | solution.py:306
  37.9 0.6 %collective-permute-done.12.refs_3_ = bf16[128,128]{1,0:T(8,128)(2,1)S(1)} collective-permute-done((bf16[128,128]{1,0:T(8,128)(2,1)S(1)}, bf16[128,128]{1,0:T(8,128)(2,1)S(1)}, u32[]{:S(2)}, u32[]{:S(2)}) %collective-permute-start.12) | collective-permute-done | bytes 32800 | tf_op jit(solution)/shard_map/ppermute | solution.py:303
  38.5 0.0 collective-permute-start.16
  38.5 0.9 %collective-permute-done.10.refs_1_ = bf16[128,128]{1,0:T(8,128)(2,1)S(1)} collective-permute-done((bf16[128,128]{1,0:T(8,128)(2,1)S(1)}, bf16[128,128]{1,0:T(8,128)(2,1)S(1)}, u32[]{:S(2)}, u32[]{:S(2)}) %collective-permute-start.10) | collective-permute-done | bytes 32800 | tf_op jit(solution)/shard_map/ppermute | solution.py:303
  39.4 0.0 collective-permute-start.14
  39.4 0.0 collective-permute-done.13.refs_4_
  39.4 0.0 collective-permute-done.15.refs_6_
  39.4 0.2 collective-permute-done.16.refs_7_
  39.7 0.9 %collective-permute-done.14.refs_5_ = bf16[128,128]{1,0:T(8,128)(2,1)S(1)} collective-permute-done((bf16[128,128]{1,0:T(8,128)(2,1)S(1)}, bf16[128,128]{1,0:T(8,128)(2,1)S(1)}, u32[]{:S(2)}, u32[]{:S(2)}) %collective-permute-start.14) | collective-permute-done | bytes 32800 | tf_op jit(solution)/shard_map/ppermute | solution.py:306
  40.6 0.0 copy-done
  40.6 1.1 %mix.1 = bf16[64,1024]{1,0:T(8,128)(2,1)} custom-call(bf16[128,128]{1,0:T(8,128)(2,1)S(1)} %late.7.refs_0_, bf16[128,128]{1,0:T(8,128)(2,1)S(1)} %collective-permute-done.10.refs_1_, bf16[128,128]{1,0:T(8,128)(2,1)S(1)} %collective-permute-done.11.refs_2_, bf16[128,128]{1,0:T(8,128)(2,1)S(1)} %collective-permute-done.12.refs_3_, ...), custom_call_target="tpu_custom_call" | custom-call | flops 134217728 | bytes 2097152 | tf_op jit(solution)/shard_map/mix/pallas_call | solution.py:283
  (2 shorter events, 0.0 us)
Async XLA Ops:
  0.0 8.8 %collective-permute-start = (bf16[512,1024]{1,0:T(8,128)(2,1)}, bf16[512,1024]{1,0:T(8,128)(2,1)S(1)}, u32[]{:S(2)}, u32[]{:S(2)}) collective-permute-start(bf16[512,1024]{1,0:T(8,128)(2,1)} %refs_8_.1), channel_id=1, source_target_pairs={{0,1},{1,0},{2,3},{3,2},{4,5},{5,4},{6,7},{7,6},{8,9},{9,8},{10,11... | collective-permute-start | bytes 3145736 | tf_op jit(solution)/shard_map/ppermute | solution.py:306
  3.6 6.2 %collective-permute-start.1 = (bf16[200,256]{1,0:T(8,128)(2,1)S(1)}, bf16[200,256]{1,0:T(8,128)(2,1)S(1)}, u32[]{:S(2)}, u32[]{:S(2)}) collective-permute-start(bf16[200,256]{1,0:T(8,128)(2,1)S(1)} %get-tuple-element.29), channel_id=1, source_target_pairs={{0,8},{2,10},{4,12},{6,14},{8,0},{10,2},{12,4},{14,6},{16,24},{18,... | collective-permute-start | bytes 307208 | tf_op jit(solution)/shard_map/ppermute | solution.py:303
  6.2 11.0 %collective-permute-start.2 = (bf16[200,256]{1,0:T(8,128)(2,1)S(1)}, bf16[200,256]{1,0:T(8,128)(2,1)S(1)}, u32[]{:S(2)}, u32[]{:S(2)}) collective-permute-start(bf16[200,256]{1,0:T(8,128)(2,1)S(1)} %get-tuple-element.30), channel_id=1, source_target_pairs={{0,16},{2,18},{4,20},{6,22},{8,24},{10,26},{12,28},{14,30},{16,0},... | collective-permute-start | bytes 307208 | tf_op jit(solution)/shard_map/ppermute | solution.py:303
  8.8 8.4 %collective-permute-start.3 = (bf16[200,256]{1,0:T(8,128)(2,1)S(1)}, bf16[200,256]{1,0:T(8,128)(2,1)S(1)}, u32[]{:S(2)}, u32[]{:S(2)}) collective-permute-start(bf16[200,256]{1,0:T(8,128)(2,1)S(1)} %get-tuple-element.31), channel_id=1, source_target_pairs={{0,24},{2,26},{4,28},{6,30},{8,16},{10,18},{12,20},{14,22},{16,8},... | collective-permute-start | bytes 307208 | tf_op jit(solution)/shard_map/ppermute | solution.py:303
  9.8 7.5 %collective-permute-start.4 = (bf16[272,256]{1,0:T(8,128)(2,1)S(1)}, bf16[272,256]{1,0:T(8,128)(2,1)S(1)}, u32[]{:S(2)}, u32[]{:S(2)}) collective-permute-start(bf16[272,256]{1,0:T(8,128)(2,1)S(1)} %pack.2.refs_4_.refs_1_), channel_id=1, source_target_pairs={{0,6},{2,4},{4,2},{6,0},{8,14},{10,12},{12,10},{14,8},{16,22},{18,... | collective-permute-start | bytes 417800 | tf_op jit(solution)/shard_map/ppermute | solution.py:303
  12.5 8.4 %collective-permute-start.5 = (bf16[272,256]{1,0:T(8,128)(2,1)S(1)}, bf16[272,256]{1,0:T(8,128)(2,1)S(1)}, u32[]{:S(2)}, u32[]{:S(2)}) collective-permute-start(bf16[272,256]{1,0:T(8,128)(2,1)S(1)} %pack.2.refs_4_.refs_1_), channel_id=1, source_target_pairs={{0,2},{2,0},{4,6},{6,4},{8,10},{10,8},{12,14},{14,12},{16,18},{18,... | collective-permute-start | bytes 417800 | tf_op jit(solution)/shard_map/ppermute | solution.py:303
  13.0 7.8 %collective-permute-start.6 = (bf16[272,256]{1,0:T(8,128)(2,1)S(1)}, bf16[272,256]{1,0:T(8,128)(2,1)S(1)}, u32[]{:S(2)}, u32[]{:S(2)}) collective-permute-start(bf16[272,256]{1,0:T(8,128)(2,1)S(1)} %pack.2.refs_4_.refs_1_), channel_id=1, source_target_pairs={{0,4},{2,6},{4,0},{6,2},{8,12},{10,14},{12,8},{14,10},{16,20},{18,... | collective-permute-start | bytes 417800 | tf_op jit(solution)/shard_map/ppermute | solution.py:303
  17.3 6.3 %collective-permute-start.7 = (bf16[272,256]{1,0:T(8,128)(2,1)S(1)}, bf16[272,256]{1,0:T(8,128)(2,1)S(1)}, u32[]{:S(2)}, u32[]{:S(2)}) collective-permute-start(bf16[272,256]{1,0:T(8,128)(2,1)S(1)} %pack.3.refs_5_.refs_1_), channel_id=1, source_target_pairs={{0,2},{2,0},{4,6},{6,4},{8,10},{10,8},{12,14},{14,12},{16,18},{18,... | collective-permute-start | bytes 417800 | tf_op jit(solution)/shard_map/ppermute | solution.py:303
  19.0 7.8 %collective-permute-start.8 = (bf16[272,256]{1,0:T(8,128)(2,1)S(1)}, bf16[272,256]{1,0:T(8,128)(2,1)S(1)}, u32[]{:S(2)}, u32[]{:S(2)}) collective-permute-start(bf16[272,256]{1,0:T(8,128)(2,1)S(1)} %pack.3.refs_5_.refs_1_), channel_id=1, source_target_pairs={{0,4},{2,6},{4,0},{6,2},{8,12},{10,14},{12,8},{14,10},{16,20},{18,... | collective-permute-start | bytes 417800 | tf_op jit(solution)/shard_map/ppermute | solution.py:303
  20.5 6.3 %collective-permute-start.9 = (bf16[272,256]{1,0:T(8,128)(2,1)S(1)}, bf16[272,256]{1,0:T(8,128)(2,1)S(1)}, u32[]{:S(2)}, u32[]{:S(2)}) collective-permute-start(bf16[272,256]{1,0:T(8,128)(2,1)S(1)} %pack.3.refs_5_.refs_1_), channel_id=1, source_target_pairs={{0,6},{2,4},{4,2},{6,0},{8,14},{10,12},{12,10},{14,8},{16,22},{18,... | collective-permute-start | bytes 417800 | tf_op jit(solution)/shard_map/ppermute | solution.py:303
  29.6 7.8 %collective-permute-start.11 = (bf16[128,128]{1,0:T(8,128)(2,1)S(1)}, bf16[128,128]{1,0:T(8,128)(2,1)S(1)}, u32[]{:S(2)}, u32[]{:S(2)}) collective-permute-start(bf16[128,128]{1,0:T(8,128)(2,1)S(1)} %late.5), channel_id=1, source_target_pairs={{0,16},{2,18},{4,20},{6,22},{8,24},{10,26},{12,28},{14,30},{16,0},... | collective-permute-start | bytes 98312 | tf_op jit(solution)/shard_map/ppermute | solution.py:303
  32.8 5.7 %collective-permute-start.12 = (bf16[128,128]{1,0:T(8,128)(2,1)S(1)}, bf16[128,128]{1,0:T(8,128)(2,1)S(1)}, u32[]{:S(2)}, u32[]{:S(2)}) collective-permute-start(bf16[128,128]{1,0:T(8,128)(2,1)S(1)} %late.4), channel_id=1, source_target_pairs={{0,24},{2,26},{4,28},{6,30},{8,16},{10,18},{12,20},{14,22},{16,8},... | collective-permute-start | bytes 98312 | tf_op jit(solution)/shard_map/ppermute | solution.py:303
  35.4 5.2 %copy-start = (bf16[512,1024]{1,0:T(8,128)(2,1)S(1)}, bf16[512,1024]{1,0:T(8,128)(2,1)}, u32[]{:S(2)}) copy-start(bf16[512,1024]{1,0:T(8,128)(2,1)} %refs_8_.1) | copy-start | bytes 3145732
  35.4 4.0 %collective-permute-start.10 = (bf16[128,128]{1,0:T(8,128)(2,1)S(1)}, bf16[128,128]{1,0:T(8,128)(2,1)S(1)}, u32[]{:S(2)}, u32[]{:S(2)}) collective-permute-start(bf16[128,128]{1,0:T(8,128)(2,1)S(1)} %late.6), channel_id=1, source_target_pairs={{0,8},{2,10},{4,12},{6,14},{8,0},{10,2},{12,4},{14,6},{16,24},{18,... | collective-permute-start | bytes 98312 | tf_op jit(solution)/shard_map/ppermute | solution.py:303
  37.3 2.1 %collective-permute-start.13 = (bf16[128,128]{1,0:T(8,128)(2,1)S(1)}, bf16[128,128]{1,0:T(8,128)(2,1)S(1)}, u32[]{:S(2)}, u32[]{:S(2)}) collective-permute-start(bf16[128,128]{1,0:T(8,128)(2,1)S(1)} %late.7.refs_0_), channel_id=1, source_target_pairs={{0,1},{1,0},{2,3},{3,2},{4,5},{5,4},{6,7},{7,6},{8,9},{9,8},{10,11... | collective-permute-start | bytes 98312 | tf_op jit(solution)/shard_map/ppermute | solution.py:306
  37.4 2.1 %collective-permute-start.15 = (bf16[128,128]{1,0:T(8,128)(2,1)S(1)}, bf16[128,128]{1,0:T(8,128)(2,1)S(1)}, u32[]{:S(2)}, u32[]{:S(2)}) collective-permute-start(bf16[128,128]{1,0:T(8,128)(2,1)S(1)} %collective-permute-done.11.refs_2_), channel_id=1, source_target_pairs={{0,1},{1,0},{2,3},{3,2},{4,5},{5,4},{6,7},{7,6},{8,9},{9,8},{10,11... | collective-permute-start | bytes 98312 | tf_op jit(solution)/shard_map/ppermute | solution.py:306
  38.5 1.2 %collective-permute-start.16 = (bf16[128,128]{1,0:T(8,128)(2,1)S(1)}, bf16[128,128]{1,0:T(8,128)(2,1)S(1)}, u32[]{:S(2)}, u32[]{:S(2)}) collective-permute-start(bf16[128,128]{1,0:T(8,128)(2,1)S(1)} %collective-permute-done.12.refs_3_), channel_id=1, source_target_pairs={{0,1},{1,0},{2,3},{3,2},{4,5},{5,4},{6,7},{7,6},{8,9},{9,8},{10,11... | collective-permute-start | bytes 98312 | tf_op jit(solution)/shard_map/ppermute | solution.py:306
  39.4 1.2 %collective-permute-start.14 = (bf16[128,128]{1,0:T(8,128)(2,1)S(1)}, bf16[128,128]{1,0:T(8,128)(2,1)S(1)}, u32[]{:S(2)}, u32[]{:S(2)}) collective-permute-start(bf16[128,128]{1,0:T(8,128)(2,1)S(1)} %collective-permute-done.10.refs_1_), channel_id=1, source_target_pairs={{0,1},{1,0},{2,3},{3,2},{4,5},{5,4},{6,7},{7,6},{8,9},{9,8},{10,11... | collective-permute-start | bytes 98312 | tf_op jit(solution)/shard_map/ppermute | solution.py:306

commit v6 on v5

--- a/solution.py
+++ b/solution.py
@@ -98,51 +98,57 @@
 
 
 def pack_kernel(first_ref, second_ref, out_ref):
-    half = out_ref.shape[0] // 2
-    out_ref[:half, :] = first_ref[:half, :]
-    out_ref[half:, :] = second_ref[:half, :]
-
-
-def pack(first, second, block, flops):
+    tok = (out_ref.shape[0] - META) // 2
+    out_ref[:tok, :] = first_ref[:tok, :]
+    out_ref[tok : 2 * tok, :] = second_ref[:tok, :]
+    first = first_ref[tok : tok + META, :].astype(jnp.float32)
+    second = second_ref[tok : tok + META, :].astype(jnp.float32)
+    row = lax.broadcasted_iota(jnp.int32, first.shape, 0)
+    low = jnp.broadcast_to(second[1:2], first.shape)
+    second = jnp.where(row == META // 2, jnp.broadcast_to(second[0:1], first.shape), low)
+    out_ref[2 * tok :, :] = jnp.where(row < META // 2, first, second).astype(jnp.bfloat16)
+
+
+def pack(first, second, tok, flops):
     vmem = pl.BlockSpec(memory_space=pltpu.VMEM)
     wide = first.shape[1]
     return pl.pallas_call(
         pack_kernel,
-        out_shape=jax.ShapeDtypeStruct((2 * block, wide), jnp.bfloat16),
+        out_shape=jax.ShapeDtypeStruct((2 * tok + META, wide), jnp.bfloat16),
         in_specs=[vmem, vmem],
         out_specs=vmem,
         compiler_params=pltpu.CompilerParams(vmem_limit_bytes=PACK_LIMIT),
         cost_estimate=pl.CostEstimate(
-            flops=flops, bytes_accessed=8 * block * wide, transcendentals=0
+            flops=flops, bytes_accessed=8 * tok * wide, transcendentals=0
         ),
         name="pack",
     )(first, second)
 
 
-def ids_of(ref, base, tok, total):
+def ids_of(ref, item, tok, total):
     pair = ref.shape[1] // 2
-    cid = ref[base + tok : base + tok + 1, :pair].astype(jnp.float32)
-    low = ref[base + tok + 1 : base + tok + 2, :pair].astype(jnp.float32)
-    high = ref[base + tok : base + tok + 1, pair:].astype(jnp.float32)
+    row = 2 * tok + item * (META // 2)
+    cid = ref[row : row + 1, :pair].astype(jnp.float32)
+    low = ref[row + 1 : row + 2, :pair].astype(jnp.float32)
+    high = ref[row : row + 1, pair:].astype(jnp.float32)
     pos = high * float(BASE) + low
     return cid * float(2 * total) + pos, pos
 
 
 def unpack(refs, tok, total, keys, values, codes):
     pair = keys.shape[1]
-    block = tok + META
-    at = 0
-    for ref in refs:
-        for base in range(0, ref.shape[0], block):
-            keys[at : at + tok, :] = ref[base : base + tok, :pair]
-            values[at : at + tok, :] = ref[base : base + tok, pair:]
-            codes[0:1, at : at + tok] = ids_of(ref, base, tok, total)[0]
-            at += tok
-
-
-def scores_of(q_ref, ids_ref, base, tok, total, keys, codes, column):
+    for at, ref in enumerate(refs):
+        rows = slice(2 * at * tok, 2 * (at + 1) * tok)
+        keys[rows, :] = ref[: 2 * tok, :pair]
+        values[rows, :] = ref[: 2 * tok, pair:]
+        for item in range(2):
+            start = (2 * at + item) * tok
+            codes[0:1, start : start + tok] = ids_of(ref, item, tok, total)[0]
+
+
+def scores_of(q_ref, ids_ref, which, tok, total, keys, codes, column):
     pair = keys.shape[1]
-    code, pos = ids_of(ids_ref, base, tok, total)
+    code, pos = ids_of(ids_ref, which, tok, total)
     column[0:1, :] = code
     column[1:2, :] = pos
     turned = jnp.transpose(column[...])
@@ -165,10 +171,9 @@
     kv_refs = refs[SPLIT : SPLIT + count]
     expo_ref, stats_ref, values, keys, codes, column = refs[SPLIT + count :]
     unpack(kv_refs, tok, total, keys, values, codes)
-    block = tok + META
     for item in range(SPLIT):
         scores = scores_of(
-            q_refs[item], kv_refs[item // 2], (item % 2) * block, tok, total, keys, codes, column
+            q_refs[item], kv_refs[item // 2], item % 2, tok, total, keys, codes, column
         )
         top = jnp.max(scores, axis=1, keepdims=True)
         expo = jnp.exp2(scores - top)
@@ -182,7 +187,7 @@
     wide = sources[0].shape[1]
     pair = wide // 2
     vmem = pl.BlockSpec(memory_space=pltpu.VMEM)
-    count = sum(item.shape[0] for item in sources) // (tok + META) * tok
+    count = 2 * tok * len(sources)
     rows = 2 * SPLIT * tok
     return pl.pallas_call(
         functools.partial(early_kernel, total, tok, len(sources)),
@@ -217,8 +222,7 @@
     pair = keys.shape[1]
     lane = lax.broadcasted_iota(jnp.int32, (tok, pair), 1) < HD
     for at, item in enumerate(items):
-        base = (item % 2) * (tok + META)
-        scores = scores_of(q_refs[at], ids_refs[at], base, tok, total, keys, codes, column)
+        scores = scores_of(q_refs[at], ids_refs[at], item % 2, tok, total, keys, codes, column)
         rows = slice(item * 2 * tok, (item + 1) * 2 * tok)
         old_top = stats_ref[rows, 0:1]
         top = jnp.maximum(jnp.max(scores, axis=1, keepdims=True), old_top)
@@ -239,7 +243,7 @@
 def late(total, tok, items, queries, ids, expo, stats, old_values, sources):
     pair = old_values.shape[1]
     vmem = pl.BlockSpec(memory_space=pltpu.VMEM)
-    count = sum(part.shape[0] for part in sources) // (tok + META) * tok
+    count = 2 * tok * len(sources)
     return pl.pallas_call(
         functools.partial(late_kernel, total, tok, items, len(sources)),
         out_shape=(jax.ShapeDtypeStruct((tok, pair), jnp.bfloat16),) * len(items),
@@ -261,43 +265,43 @@
     )(*queries, *ids, expo, stats, old_values, *sources)
 
 
-def mix_kernel(*refs):
-    own_refs, other_refs = refs[:SPLIT], refs[SPLIT : 2 * SPLIT]
-    w_own, w_other, out_ref, left, right = refs[2 * SPLIT :]
-    rows, pair = out_ref.shape[0], own_refs[0].shape[1]
+def mix_kernel(with_sum, *refs):
+    piece_refs, (w_ref, *sum_refs, out_ref, rows_buf) = refs[:SPLIT], refs[SPLIT:]
+    rows, pair = out_ref.shape[0], piece_refs[0].shape[1]
     chip = lax.axis_index("seq") // PLANE
     mine = pl.ds(pl.multiple_of(lax.axis_index("head") * rows, rows), rows)
     for step in range(SPLIT):
         lanes = pl.ds(pl.multiple_of(jnp.bitwise_xor(chip, step) * pair, pair), pair)
-        left[:, lanes] = own_refs[step][mine, :]
-        right[:, lanes] = other_refs[step][mine, :]
-    total = jnp.dot(left[...], w_own[...], preferred_element_type=jnp.float32)
-    total += jnp.dot(right[...], w_other[...], preferred_element_type=jnp.float32)
-    out_ref[...] = total.astype(jnp.bfloat16)
-
-
-def mix(own, other, w_own, w_other):
-    rows = own[0].shape[0] // 2
-    deep, width = w_own.shape
+        rows_buf[:, lanes] = piece_refs[step][mine, :]
+    total = jnp.dot(rows_buf[...], w_ref[...], preferred_element_type=jnp.float32)
+    if with_sum:
+        total += sum_refs[0][...]
+    out_ref[...] = total.astype(out_ref.dtype)
+
+
+def mix(pieces, weight, before=None):
+    rows = pieces[0].shape[0] // 2
+    deep, width = weight.shape
     vmem = pl.BlockSpec(memory_space=pltpu.VMEM)
+    sums = [] if before is None else [before]
+    dtype = jnp.float32 if before is None else jnp.bfloat16
     return pl.pallas_call(
-        mix_kernel,
-        out_shape=jax.ShapeDtypeStruct((rows, width), jnp.bfloat16),
-        in_specs=[vmem] * (2 * SPLIT + 2),
+        functools.partial(mix_kernel, before is not None),
+        out_shape=jax.ShapeDtypeStruct((rows, width), dtype),
+        in_specs=[vmem] * (SPLIT + 1 + len(sums)),
         out_specs=vmem,
-        scratch_shapes=[pltpu.VMEM((rows, deep), jnp.bfloat16)] * 2,
+        scratch_shapes=[pltpu.VMEM((rows, deep), jnp.bfloat16)],
         compiler_params=pltpu.CompilerParams(vmem_limit_bytes=PACK_LIMIT),
         cost_estimate=pl.CostEstimate(
-            flops=4 * rows * deep * width, bytes_accessed=4 * deep * width, transcendentals=0
+            flops=2 * rows * deep * width, bytes_accessed=2 * deep * width, transcendentals=0
         ),
         name="mix",
-    )(*own, *other, w_own, w_other)
+    )(*pieces, weight, *sums)
 
 
 def per_device_split(tokens, w_query, w_key, w_value, w_out, cluster_ids, positions):
     tok = tokens.shape[0]
     owners = lax.axis_size("seq")
-    block = tok + META
 
     def send(array, bits):
         return lax.ppermute(array, "seq", [(i, i ^ bits) for i in range(owners)])
@@ -310,10 +314,10 @@
     m1, kv0, q0, m3, m2 = project((1, 0, 3, 2), tokens, positions, cluster_ids, weights)
     r1, r3, r2 = send(m1, PLANE), send(m3, 3 * PLANE), send(m2, 2 * PLANE)
     kv0, w_other = lax.optimization_barrier((kv0, w_other))
-    near = pack(kv0, r1, block, 0)
+    near = pack(kv0, r1, tok, 0)
     nears = [send(near, bits) for bits in (1, 2, 3)]
-    far = pack(r2, r3, block, FAR_FLOPS)
-    far, nears[2] = lax.optimization_barrier((far, nears[2]))
+    far = pack(r2, r3, tok, FAR_FLOPS)
+    far, nears[1] = lax.optimization_barrier((far, nears[1]))
     fars = [send(far, bits) for bits in (1, 2, 3)]
     total = owners * tok
     expo, stats, values = early(total, tok, (q0, r1, r2, r3), [near, far, *nears])
@@ -326,7 +330,8 @@
     own[3], own[2] = lax.optimization_barrier((own[3], own[2]))
     b3 = send(own[3], 3 * PLANE)
     own = (own[0], send(own[1], PLANE), send(own[2], 2 * PLANE), b3)
-    return mix(own, [swap(item) for item in own], w_out, w_other)
+    half = mix(own, w_out)
+    return mix([swap(item) for item in own], w_other, half)
 
 
 def attend_rows(query, keys, values, query_pos, key_pos):

time: 41.9 us -> 41.6 us (level)
    pallas_call x3 -> x4, Pallas kernels: 1.16 us -> 1.29 us  [the longest x2 1.25 us: mix(): pl.pallas_call(functools.partial(mix_kernel, before is not None), out_sha...]
  transfers between devices with their start and end apart: 17 -> 17, of which waited for: 9 -> 7; matrix products, arithmetic and copies ran while one was open for 0% -> 0% of each run, Pallas kernels for 19% -> 20%
where the time goes in v6:
time: 41.6 us; the launch traced here: 41.5 us
  starting transfers between devices  18 us (43%)
  Pallas kernels  12.1 us (29%)
  waiting for transfers between devices  11.3 us (27%)
    ppermute x12, starting transfers between devices, send(): return lax.ppermute(array, 'seq', [(i, i ^ bits) for i in range(owners)])  17 us
    ppermute x12, waiting for transfers between devices, send(): return lax.ppermute(array, 'seq', [(i, i ^ bits) for i in range(owners)])  10.4 us
    pallas_call x4, Pallas kernels, late(): pl.pallas_call(functools.partial(late_kernel, total, tok, items, len(sour...  5.5 us
    pallas_call x1, Pallas kernels, project(): pl.pallas_call(functools.partial(project_kernel, steps), out_shape=tuple(...  3.1 us
    pallas_call x1, Pallas kernels, early(): pl.pallas_call(functools.partial(early_kernel, total, tok, len(sources)),...  2.2 us
    pallas_call x2, Pallas kernels, mix(): pl.pallas_call(functools.partial(mix_kernel, before is not None), out_sha...  1.25 us
    ppermute x5, starting transfers between devices, swap(): return lax.ppermute(array, 'head', [(0, 1), (1, 0)])  1.02 us
    ppermute x5, waiting for transfers between devices, swap(): return lax.ppermute(array, 'head', [(0, 1), (1, 0)])  0.88 us
  transfers between devices with their start and end apart: 17, of which 7 were waited for; matrix products, arithmetic and copies ran while one was open for 0% of the time, Pallas kernels for 20%

profile of v6, /device:TPU:0, one launch (start us, length us, event | category | flops | bytes accessed | tf_op | source)
XLA Modules:
  0.0 41.5 jit_solution(573697107697193205)
XLA Ops:
  0.0 0.5 %collective-permute-start = (bf16[512,1024]{1,0:T(8,128)(2,1)}, bf16[512,1024]{1,0:T(8,128)(2,1)S(1)}, u32[]{:S(2)}, u32[]{:S(2)}) collective-permute-start(bf16[512,1024]{1,0:T(8,128)(2,1)} %refs_4_.1), channel_id=1, source_target_pairs={{0,1},{1,0},{2,3},{3,2},{4,5},{5,4},{6,7},{7,6},{8,9},{9,8},{10,11... | collective-permute-start | bytes 3145736 | tf_op jit(solution)/shard_map/ppermute | solution.py:310
  0.5 3.1 %project.1 = (bf16[200,256]{1,0:T(8,128)(2,1)S(1)}, bf16[136,256]{1,0:T(8,128)(2,1)S(1)}, bf16[64,256]{1,0:T(8,128)(2,1)S(1)}, bf16[200,256]{1,0:T(8,128)(2,1)S(1)}, bf16[200,256]{1,0:T(8,128)(2,1)S(1)}) custom-call(bf16[128,1024]{1,0:T(8,128)(2,1)} %tok_hbm.1, s32[1,128]{1,0:T(1,128)} %bitcast.1, s32[2,128]{1,0:T(2,128)} %cid_hbm.1, ...), custom_call_target="tpu_custom_call" | custom-call | flops 402653184 | bytes 3145728 | tf_op jit(solution)/shard_map/project/pallas_call | solution.py:77
  3.6 2.6 %collective-permute-start.1 = (bf16[200,256]{1,0:T(8,128)(2,1)S(1)}, bf16[200,256]{1,0:T(8,128)(2,1)S(1)}, u32[]{:S(2)}, u32[]{:S(2)}) collective-permute-start(bf16[200,256]{1,0:T(8,128)(2,1)S(1)} %get-tuple-element.29), channel_id=1, source_target_pairs={{0,8},{2,10},{4,12},{6,14},{8,0},{10,2},{12,4},{14,6},{16,24},{18,... | collective-permute-start | bytes 307208 | tf_op jit(solution)/shard_map/ppermute | solution.py:307
  6.2 2.6 %collective-permute-start.2 = (bf16[200,256]{1,0:T(8,128)(2,1)S(1)}, bf16[200,256]{1,0:T(8,128)(2,1)S(1)}, u32[]{:S(2)}, u32[]{:S(2)}) collective-permute-start(bf16[200,256]{1,0:T(8,128)(2,1)S(1)} %get-tuple-element.30), channel_id=1, source_target_pairs={{0,16},{2,18},{4,20},{6,22},{8,24},{10,26},{12,28},{14,30},{16,0},... | collective-permute-start | bytes 307208 | tf_op jit(solution)/shard_map/ppermute | solution.py:307
  8.8 0.0 collective-permute-start.3
  8.8 0.0 collective-permute-done.refs_4_
  8.8 1.0 %collective-permute-done.1.second_ref.refs_1_.refs_0_ = bf16[200,256]{1,0:T(8,128)(2,1)S(1)} collective-permute-done((bf16[200,256]{1,0:T(8,128)(2,1)S(1)}, bf16[200,256]{1,0:T(8,128)(2,1)S(1)}, u32[]{:S(2)}, u32[]{:S(2)}) %collective-permute-start.1) | collective-permute-done | bytes 102432 | tf_op jit(solution)/shard_map/ppermute | solution.py:307
  9.8 1.8 %collective-permute-start.4 = (bf16[264,256]{1,0:T(8,128)(2,1)S(1)}, bf16[264,256]{1,0:T(8,128)(2,1)S(1)}, u32[]{:S(2)}, u32[]{:S(2)}) collective-permute-start(bf16[264,256]{1,0:T(8,128)(2,1)S(1)} %pack.2.refs_4_.refs_1_), channel_id=1, source_target_pairs={{0,4},{2,6},{4,0},{6,2},{8,12},{10,14},{12,8},{14,10},{16,20},{18,... | collective-permute-start | bytes 405512 | tf_op jit(solution)/shard_map/ppermute | solution.py:307
  11.5 1.5 %collective-permute-start.5 = (bf16[264,256]{1,0:T(8,128)(2,1)S(1)}, bf16[264,256]{1,0:T(8,128)(2,1)S(1)}, u32[]{:S(2)}, u32[]{:S(2)}) collective-permute-start(bf16[264,256]{1,0:T(8,128)(2,1)S(1)} %pack.2.refs_4_.refs_1_), channel_id=1, source_target_pairs={{0,2},{2,0},{4,6},{6,4},{8,10},{10,8},{12,14},{14,12},{16,18},{18,... | collective-permute-start | bytes 405512 | tf_op jit(solution)/shard_map/ppermute | solution.py:307
  13.0 0.3 collective-permute-start.6
  13.3 3.9 %collective-permute-done.2.first_ref.refs_2_.refs_0_ = bf16[200,256]{1,0:T(8,128)(2,1)S(1)} collective-permute-done((bf16[200,256]{1,0:T(8,128)(2,1)S(1)}, bf16[200,256]{1,0:T(8,128)(2,1)S(1)}, u32[]{:S(2)}, u32[]{:S(2)}) %collective-permute-start.2) | collective-permute-done | bytes 102432 | tf_op jit(solution)/shard_map/ppermute | solution.py:307
  17.2 0.0 collective-permute-done.3.second_ref.refs_3_.refs_0_
  17.2 0.0 collective-permute-done.4.refs_7_
  17.2 1.6 %collective-permute-start.7 = (bf16[264,256]{1,0:T(8,128)(2,1)S(1)}, bf16[264,256]{1,0:T(8,128)(2,1)S(1)}, u32[]{:S(2)}, u32[]{:S(2)}) collective-permute-start(bf16[264,256]{1,0:T(8,128)(2,1)S(1)} %pack.3.refs_5_.refs_1_), channel_id=1, source_target_pairs={{0,2},{2,0},{4,6},{6,4},{8,10},{10,8},{12,14},{14,12},{16,18},{18,... | collective-permute-start | bytes 405512 | tf_op jit(solution)/shard_map/ppermute | solution.py:307
  18.8 1.5 %collective-permute-start.8 = (bf16[264,256]{1,0:T(8,128)(2,1)S(1)}, bf16[264,256]{1,0:T(8,128)(2,1)S(1)}, u32[]{:S(2)}, u32[]{:S(2)}) collective-permute-start(bf16[264,256]{1,0:T(8,128)(2,1)S(1)} %pack.3.refs_5_.refs_1_), channel_id=1, source_target_pairs={{0,4},{2,6},{4,0},{6,2},{8,12},{10,14},{12,8},{14,10},{16,20},{18,... | collective-permute-start | bytes 405512 | tf_op jit(solution)/shard_map/ppermute | solution.py:307
  20.3 0.5 %collective-permute-start.9 = (bf16[264,256]{1,0:T(8,128)(2,1)S(1)}, bf16[264,256]{1,0:T(8,128)(2,1)S(1)}, u32[]{:S(2)}, u32[]{:S(2)}) collective-permute-start(bf16[264,256]{1,0:T(8,128)(2,1)S(1)} %pack.3.refs_5_.refs_1_), channel_id=1, source_target_pairs={{0,6},{2,4},{4,2},{6,0},{8,14},{10,12},{12,10},{14,8},{16,22},{18,... | collective-permute-start | bytes 405512 | tf_op jit(solution)/shard_map/ppermute | solution.py:307
  20.8 0.0 collective-permute-done.5.refs_6_
  20.8 0.0 collective-permute-done.6.refs_8_
  20.8 2.2 %early.1 = (f32[1024,1280]{1,0:T(8,128)S(1)}, f32[1024,128]{1,0:T(8,128)S(1)}, bf16[1280,128]{1,0:T(8,128)(2,1)S(1)}) custom-call(bf16[64,256]{1,0:T(8,128)(2,1)S(1)} %get-tuple-element.26.refs_0_, bf16[200,256]{1,0:T(8,128)(2,1)S(1)} %collective-permute-done.1.second_ref.refs_1_.refs_0_, ...), custom_call_target="tpu_custom_call" | custom-call | flops 8000000000 | bytes 1310720 | tf_op jit(solution)/shard_map/early/pallas_call | solution.py:192
  23.0 0.4 %collective-permute-done.7.refs_5_ = bf16[264,256]{1,0:T(8,128)(2,1)S(1)} collective-permute-done((bf16[264,256]{1,0:T(8,128)(2,1)S(1)}, bf16[264,256]{1,0:T(8,128)(2,1)S(1)}, u32[]{:S(2)}, u32[]{:S(2)}) %collective-permute-start.7) | collective-permute-done | bytes 135200 | tf_op jit(solution)/shard_map/ppermute | solution.py:307
  23.5 3.2 %collective-permute-done.8.refs_6_ = bf16[264,256]{1,0:T(8,128)(2,1)S(1)} collective-permute-done((bf16[264,256]{1,0:T(8,128)(2,1)S(1)}, bf16[264,256]{1,0:T(8,128)(2,1)S(1)}, u32[]{:S(2)}, u32[]{:S(2)}) %collective-permute-start.8) | collective-permute-done | bytes 135200 | tf_op jit(solution)/shard_map/ppermute | solution.py:307
  26.6 0.0 collective-permute-done.9.refs_7_
  26.6 1.4 %late.4 = bf16[128,128]{1,0:T(8,128)(2,1)S(1)} custom-call(bf16[200,256]{1,0:T(8,128)(2,1)S(1)} %collective-permute-done.3.second_ref.refs_3_.refs_0_, bf16[264,256]{1,0:T(8,128)(2,1)S(1)} %pack.3.refs_5_.refs_1_, f32[1024,1280]{1,0:T(8,128)S(1)} %get-tuple-element.34.refs_2_, f32[1024,128]{1,0:T(8,128)S(1)} %get-tuple-element.39.refs_3_, ...), custom_call_target="tpu_custom_call" | custom-call | flops 3000000000 | bytes 393216 | tf_op jit(solution)/shard_map/late/pallas_call | solution.py:247
  28.0 1.4 %late.5 = bf16[128,128]{1,0:T(8,128)(2,1)S(1)} custom-call(bf16[200,256]{1,0:T(8,128)(2,1)S(1)} %collective-permute-done.2.first_ref.refs_2_.refs_0_, bf16[264,256]{1,0:T(8,128)(2,1)S(1)} %pack.3.refs_5_.refs_1_, f32[1024,1280]{1,0:T(8,128)S(1)} %get-tuple-element.34.refs_2_, f32[1024,128]{1,0:T(8,128)S(1)} %get-tuple-element.39.refs_3_, ...), custom_call_target="tpu_custom_call" | custom-call | flops 3000000000 | bytes 393216 | tf_op jit(solution)/shard_map/late/pallas_call | solution.py:247
  29.4 3.3 %collective-permute-start.13 = (bf16[128,128]{1,0:T(8,128)(2,1)S(1)}, bf16[128,128]{1,0:T(8,128)(2,1)S(1)}, u32[]{:S(2)}, u32[]{:S(2)}) collective-permute-start(bf16[128,128]{1,0:T(8,128)(2,1)S(1)} %late.5), channel_id=1, source_target_pairs={{0,16},{2,18},{4,20},{6,22},{8,24},{10,26},{12,28},{14,30},{16,0},... | collective-permute-start | bytes 98312 | tf_op jit(solution)/shard_map/ppermute | solution.py:307
  32.6 1.3 %collective-permute-start.15 = (bf16[128,128]{1,0:T(8,128)(2,1)S(1)}, bf16[128,128]{1,0:T(8,128)(2,1)S(1)}, u32[]{:S(2)}, u32[]{:S(2)}) collective-permute-start(bf16[128,128]{1,0:T(8,128)(2,1)S(1)} %late.4), channel_id=1, source_target_pairs={{0,24},{2,26},{4,28},{6,30},{8,16},{10,18},{12,20},{14,22},{16,8},... | collective-permute-start | bytes 98312 | tf_op jit(solution)/shard_map/ppermute | solution.py:307
  34.0 1.4 %late.6 = bf16[128,128]{1,0:T(8,128)(2,1)S(1)} custom-call(bf16[200,256]{1,0:T(8,128)(2,1)S(1)} %collective-permute-done.1.second_ref.refs_1_.refs_0_, bf16[264,256]{1,0:T(8,128)(2,1)S(1)} %pack.2.refs_4_.refs_1_, f32[1024,1280]{1,0:T(8,128)S(1)} %get-tuple-element.34.refs_2_, f32[1024,128]{1,0:T(8,128)S(1)} %get-tuple-element.39.refs_3_, ...), custom_call_target="tpu_custom_call" | custom-call | flops 3000000000 | bytes 393216 | tf_op jit(solution)/shard_map/late/pallas_call | solution.py:247
  35.3 0.0 copy-start
  35.3 0.1 collective-permute-start.11
  35.4 1.4 %late.7.refs_0_ = bf16[128,128]{1,0:T(8,128)(2,1)S(1)} custom-call(bf16[64,256]{1,0:T(8,128)(2,1)S(1)} %get-tuple-element.26.refs_0_, bf16[264,256]{1,0:T(8,128)(2,1)S(1)} %pack.2.refs_4_.refs_1_, f32[1024,1280]{1,0:T(8,128)S(1)} %get-tuple-element.34.refs_2_, f32[1024,128]{1,0:T(8,128)S(1)} %get-tuple-element.39.refs_3_, ...), custom_call_target="tpu_custom_call" | custom-call | flops 3000000000 | bytes 393216 | tf_op jit(solution)/shard_map/late/pallas_call | solution.py:247
  36.8 0.1 collective-permute-start.10
  36.9 0.0 collective-permute-done.13.refs_2_
  36.9 0.5 %collective-permute-start.14 = (bf16[128,128]{1,0:T(8,128)(2,1)S(1)}, bf16[128,128]{1,0:T(8,128)(2,1)S(1)}, u32[]{:S(2)}, u32[]{:S(2)}) collective-permute-start(bf16[128,128]{1,0:T(8,128)(2,1)S(1)} %collective-permute-done.13.refs_2_), channel_id=1, source_target_pairs={{0,1},{1,0},{2,3},{3,2},{4,5},{5,4},{6,7},{7,6},{8,9},{9,8},{10,11... | collective-permute-start | bytes 98312 | tf_op jit(solution)/shard_map/ppermute | solution.py:310
  37.4 1.0 %collective-permute-done.15.refs_3_ = bf16[128,128]{1,0:T(8,128)(2,1)S(1)} collective-permute-done((bf16[128,128]{1,0:T(8,128)(2,1)S(1)}, bf16[128,128]{1,0:T(8,128)(2,1)S(1)}, u32[]{:S(2)}, u32[]{:S(2)}) %collective-permute-start.15) | collective-permute-done | bytes 32800 | tf_op jit(solution)/shard_map/ppermute | solution.py:307
  38.4 0.0 collective-permute-start.16
  38.4 1.0 %collective-permute-done.11.refs_1_ = bf16[128,128]{1,0:T(8,128)(2,1)S(1)} collective-permute-done((bf16[128,128]{1,0:T(8,128)(2,1)S(1)}, bf16[128,128]{1,0:T(8,128)(2,1)S(1)}, u32[]{:S(2)}, u32[]{:S(2)}) %collective-permute-start.11) | collective-permute-done | bytes 32800 | tf_op jit(solution)/shard_map/ppermute | solution.py:307
  39.3 0.0 collective-permute-start.12
  39.3 0.0 copy-done
  39.3 0.3 mix.2.refs_5_
  39.6 0.0 collective-permute-done.10.refs_0_
  39.6 0.0 collective-permute-done.14.refs_2_
  39.7 0.0 collective-permute-done.16.refs_3_
  39.7 0.9 %collective-permute-done.12.refs_1_ = bf16[128,128]{1,0:T(8,128)(2,1)S(1)} collective-permute-done((bf16[128,128]{1,0:T(8,128)(2,1)S(1)}, bf16[128,128]{1,0:T(8,128)(2,1)S(1)}, u32[]{:S(2)}, u32[]{:S(2)}) %collective-permute-start.12) | collective-permute-done | bytes 32800 | tf_op jit(solution)/shard_map/ppermute | solution.py:310
  40.5 1.0 %mix.3 = bf16[64,1024]{1,0:T(8,128)(2,1)} custom-call(bf16[128,128]{1,0:T(8,128)(2,1)S(1)} %collective-permute-done.10.refs_0_, bf16[128,128]{1,0:T(8,128)(2,1)S(1)} %collective-permute-done.12.refs_1_, bf16[128,128]{1,0:T(8,128)(2,1)S(1)} %collective-permute-done.14.refs_2_, bf16[128,128]{1,0:T(8,128)(2,1)S(1)} %collective-permute-done.16.refs_3_, ...), custom_call_target="tpu_custom_call" | custom-call | flops 67108864 | bytes 1048576 | tf_op jit(solution)/shard_map/mix/pallas_call | solution.py:288
  (2 shorter events, 0.0 us)
Async XLA Ops:
  0.0 8.8 %collective-permute-start = (bf16[512,1024]{1,0:T(8,128)(2,1)}, bf16[512,1024]{1,0:T(8,128)(2,1)S(1)}, u32[]{:S(2)}, u32[]{:S(2)}) collective-permute-start(bf16[512,1024]{1,0:T(8,128)(2,1)} %refs_4_.1), channel_id=1, source_target_pairs={{0,1},{1,0},{2,3},{3,2},{4,5},{5,4},{6,7},{7,6},{8,9},{9,8},{10,11... | collective-permute-start | bytes 3145736 | tf_op jit(solution)/shard_map/ppermute | solution.py:310
  3.6 6.2 %collective-permute-start.1 = (bf16[200,256]{1,0:T(8,128)(2,1)S(1)}, bf16[200,256]{1,0:T(8,128)(2,1)S(1)}, u32[]{:S(2)}, u32[]{:S(2)}) collective-permute-start(bf16[200,256]{1,0:T(8,128)(2,1)S(1)} %get-tuple-element.29), channel_id=1, source_target_pairs={{0,8},{2,10},{4,12},{6,14},{8,0},{10,2},{12,4},{14,6},{16,24},{18,... | collective-permute-start | bytes 307208 | tf_op jit(solution)/shard_map/ppermute | solution.py:307
  6.2 11.0 %collective-permute-start.2 = (bf16[200,256]{1,0:T(8,128)(2,1)S(1)}, bf16[200,256]{1,0:T(8,128)(2,1)S(1)}, u32[]{:S(2)}, u32[]{:S(2)}) collective-permute-start(bf16[200,256]{1,0:T(8,128)(2,1)S(1)} %get-tuple-element.30), channel_id=1, source_target_pairs={{0,16},{2,18},{4,20},{6,22},{8,24},{10,26},{12,28},{14,30},{16,0},... | collective-permute-start | bytes 307208 | tf_op jit(solution)/shard_map/ppermute | solution.py:307
  8.8 8.4 %collective-permute-start.3 = (bf16[200,256]{1,0:T(8,128)(2,1)S(1)}, bf16[200,256]{1,0:T(8,128)(2,1)S(1)}, u32[]{:S(2)}, u32[]{:S(2)}) collective-permute-start(bf16[200,256]{1,0:T(8,128)(2,1)S(1)} %get-tuple-element.31), channel_id=1, source_target_pairs={{0,24},{2,26},{4,28},{6,30},{8,16},{10,18},{12,20},{14,22},{16,8},... | collective-permute-start | bytes 307208 | tf_op jit(solution)/shard_map/ppermute | solution.py:307
  9.8 7.5 %collective-permute-start.4 = (bf16[264,256]{1,0:T(8,128)(2,1)S(1)}, bf16[264,256]{1,0:T(8,128)(2,1)S(1)}, u32[]{:S(2)}, u32[]{:S(2)}) collective-permute-start(bf16[264,256]{1,0:T(8,128)(2,1)S(1)} %pack.2.refs_4_.refs_1_), channel_id=1, source_target_pairs={{0,4},{2,6},{4,0},{6,2},{8,12},{10,14},{12,8},{14,10},{16,20},{18,... | collective-permute-start | bytes 405512 | tf_op jit(solution)/shard_map/ppermute | solution.py:307
  11.5 9.3 %collective-permute-start.5 = (bf16[264,256]{1,0:T(8,128)(2,1)S(1)}, bf16[264,256]{1,0:T(8,128)(2,1)S(1)}, u32[]{:S(2)}, u32[]{:S(2)}) collective-permute-start(bf16[264,256]{1,0:T(8,128)(2,1)S(1)} %pack.2.refs_4_.refs_1_), channel_id=1, source_target_pairs={{0,2},{2,0},{4,6},{6,4},{8,10},{10,8},{12,14},{14,12},{16,18},{18,... | collective-permute-start | bytes 405512 | tf_op jit(solution)/shard_map/ppermute | solution.py:307
  13.0 7.8 %collective-permute-start.6 = (bf16[264,256]{1,0:T(8,128)(2,1)S(1)}, bf16[264,256]{1,0:T(8,128)(2,1)S(1)}, u32[]{:S(2)}, u32[]{:S(2)}) collective-permute-start(bf16[264,256]{1,0:T(8,128)(2,1)S(1)} %pack.2.refs_4_.refs_1_), channel_id=1, source_target_pairs={{0,6},{2,4},{4,2},{6,0},{8,14},{10,12},{12,10},{14,8},{16,22},{18,... | collective-permute-start | bytes 405512 | tf_op jit(solution)/shard_map/ppermute | solution.py:307
  17.2 6.2 %collective-permute-start.7 = (bf16[264,256]{1,0:T(8,128)(2,1)S(1)}, bf16[264,256]{1,0:T(8,128)(2,1)S(1)}, u32[]{:S(2)}, u32[]{:S(2)}) collective-permute-start(bf16[264,256]{1,0:T(8,128)(2,1)S(1)} %pack.3.refs_5_.refs_1_), channel_id=1, source_target_pairs={{0,2},{2,0},{4,6},{6,4},{8,10},{10,8},{12,14},{14,12},{16,18},{18,... | collective-permute-start | bytes 405512 | tf_op jit(solution)/shard_map/ppermute | solution.py:307
  18.8 7.8 %collective-permute-start.8 = (bf16[264,256]{1,0:T(8,128)(2,1)S(1)}, bf16[264,256]{1,0:T(8,128)(2,1)S(1)}, u32[]{:S(2)}, u32[]{:S(2)}) collective-permute-start(bf16[264,256]{1,0:T(8,128)(2,1)S(1)} %pack.3.refs_5_.refs_1_), channel_id=1, source_target_pairs={{0,4},{2,6},{4,0},{6,2},{8,12},{10,14},{12,8},{14,10},{16,20},{18,... | collective-permute-start | bytes 405512 | tf_op jit(solution)/shard_map/ppermute | solution.py:307
  20.3 6.3 %collective-permute-start.9 = (bf16[264,256]{1,0:T(8,128)(2,1)S(1)}, bf16[264,256]{1,0:T(8,128)(2,1)S(1)}, u32[]{:S(2)}, u32[]{:S(2)}) collective-permute-start(bf16[264,256]{1,0:T(8,128)(2,1)S(1)} %pack.3.refs_5_.refs_1_), channel_id=1, source_target_pairs={{0,6},{2,4},{4,2},{6,0},{8,14},{10,12},{12,10},{14,8},{16,22},{18,... | collective-permute-start | bytes 405512 | tf_op jit(solution)/shard_map/ppermute | solution.py:307
  29.4 7.5 %collective-permute-start.13 = (bf16[128,128]{1,0:T(8,128)(2,1)S(1)}, bf16[128,128]{1,0:T(8,128)(2,1)S(1)}, u32[]{:S(2)}, u32[]{:S(2)}) collective-permute-start(bf16[128,128]{1,0:T(8,128)(2,1)S(1)} %late.5), channel_id=1, source_target_pairs={{0,16},{2,18},{4,20},{6,22},{8,24},{10,26},{12,28},{14,30},{16,0},... | collective-permute-start | bytes 98312 | tf_op jit(solution)/shard_map/ppermute | solution.py:307
  32.6 5.7 %collective-permute-start.15 = (bf16[128,128]{1,0:T(8,128)(2,1)S(1)}, bf16[128,128]{1,0:T(8,128)(2,1)S(1)}, u32[]{:S(2)}, u32[]{:S(2)}) collective-permute-start(bf16[128,128]{1,0:T(8,128)(2,1)S(1)} %late.4), channel_id=1, source_target_pairs={{0,24},{2,26},{4,28},{6,30},{8,16},{10,18},{12,20},{14,22},{16,8},... | collective-permute-start | bytes 98312 | tf_op jit(solution)/shard_map/ppermute | solution.py:307
  35.3 4.0 %copy-start = (bf16[512,1024]{1,0:T(8,128)(2,1)S(1)}, bf16[512,1024]{1,0:T(8,128)(2,1)}, u32[]{:S(2)}) copy-start(bf16[512,1024]{1,0:T(8,128)(2,1)} %refs_4_.1) | copy-start | bytes 3145732
  35.3 4.0 %collective-permute-start.11 = (bf16[128,128]{1,0:T(8,128)(2,1)S(1)}, bf16[128,128]{1,0:T(8,128)(2,1)S(1)}, u32[]{:S(2)}, u32[]{:S(2)}) collective-permute-start(bf16[128,128]{1,0:T(8,128)(2,1)S(1)} %late.6), channel_id=1, source_target_pairs={{0,8},{2,10},{4,12},{6,14},{8,0},{10,2},{12,4},{14,6},{16,24},{18,... | collective-permute-start | bytes 98312 | tf_op jit(solution)/shard_map/ppermute | solution.py:307
  36.8 2.8 %collective-permute-start.10 = (bf16[128,128]{1,0:T(8,128)(2,1)S(1)}, bf16[128,128]{1,0:T(8,128)(2,1)S(1)}, u32[]{:S(2)}, u32[]{:S(2)}) collective-permute-start(bf16[128,128]{1,0:T(8,128)(2,1)S(1)} %late.7.refs_0_), channel_id=1, source_target_pairs={{0,1},{1,0},{2,3},{3,2},{4,5},{5,4},{6,7},{7,6},{8,9},{9,8},{10,11... | collective-permute-start | bytes 98312 | tf_op jit(solution)/shard_map/ppermute | solution.py:310
  36.9 2.7 %collective-permute-start.14 = (bf16[128,128]{1,0:T(8,128)(2,1)S(1)}, bf16[128,128]{1,0:T(8,128)(2,1)S(1)}, u32[]{:S(2)}, u32[]{:S(2)}) collective-permute-start(bf16[128,128]{1,0:T(8,128)(2,1)S(1)} %collective-permute-done.13.refs_2_), channel_id=1, source_target_pairs={{0,1},{1,0},{2,3},{3,2},{4,5},{5,4},{6,7},{7,6},{8,9},{9,8},{10,11... | collective-permute-start | bytes 98312 | tf_op jit(solution)/shard_map/ppermute | solution.py:310
  38.4 1.3 %collective-permute-start.16 = (bf16[128,128]{1,0:T(8,128)(2,1)S(1)}, bf16[128,128]{1,0:T(8,128)(2,1)S(1)}, u32[]{:S(2)}, u32[]{:S(2)}) collective-permute-start(bf16[128,128]{1,0:T(8,128)(2,1)S(1)} %collective-permute-done.15.refs_3_), channel_id=1, source_target_pairs={{0,1},{1,0},{2,3},{3,2},{4,5},{5,4},{6,7},{7,6},{8,9},{9,8},{10,11... | collective-permute-start | bytes 98312 | tf_op jit(solution)/shard_map/ppermute | solution.py:310
  39.3 1.2 %collective-permute-start.12 = (bf16[128,128]{1,0:T(8,128)(2,1)S(1)}, bf16[128,128]{1,0:T(8,128)(2,1)S(1)}, u32[]{:S(2)}, u32[]{:S(2)}) collective-permute-start(bf16[128,128]{1,0:T(8,128)(2,1)S(1)} %collective-permute-done.11.refs_1_), channel_id=1, source_target_pairs={{0,1},{1,0},{2,3},{3,2},{4,5},{5,4},{6,7},{7,6},{8,9},{9,8},{10,11... | collective-permute-start | bytes 98312 | tf_op jit(solution)/shard_map/ppermute | solution.py:310

commit v7 on v6

--- a/solution.py
+++ b/solution.py
@@ -318,7 +318,7 @@
     nears = [send(near, bits) for bits in (1, 2, 3)]
     far = pack(r2, r3, tok, FAR_FLOPS)
     far, nears[1] = lax.optimization_barrier((far, nears[1]))
-    fars = [send(far, bits) for bits in (1, 2, 3)]
+    fars = [send(far, bits) for bits in (3, 1, 2)]
     total = owners * tok
     expo, stats, values = early(total, tok, (q0, r1, r2, r3), [near, far, *nears])
     queries, own = (q0, r1, r2, r3), [None] * SPLIT

time: 41.6 us -> 41 us (0.986)
  waiting for transfers between devices: 11.3 us -> 10.2 us
    ppermute x12, waiting for transfers between devices: 10.4 us -> 9.33 us  [send(): return lax.ppermute(array, 'seq', [(i, i ^ bits) for i in range(owners)])]
    ppermute x12, starting transfers between devices: 17 us -> 17.4 us  [send(): return lax.ppermute(array, 'seq', [(i, i ^ bits) for i in range(owners)])]
  transfers between devices with their start and end apart: 17 -> 17, of which waited for: 7 -> 8; matrix products, arithmetic and copies ran while one was open for 0% -> 0% of each run, Pallas kernels for 20% -> 21%
where the time goes in v7:
time: 41 us; the launch traced here: 40.9 us
  starting transfers between devices  18.4 us (45%)
  Pallas kernels  12.1 us (30%)
  waiting for transfers between devices  10.2 us (25%)
    ppermute x12, starting transfers between devices, send(): return lax.ppermute(array, 'seq', [(i, i ^ bits) for i in range(owners)])  17.4 us
    ppermute x12, waiting for transfers between devices, send(): return lax.ppermute(array, 'seq', [(i, i ^ bits) for i in range(owners)])  9.33 us
    pallas_call x4, Pallas kernels, late(): pl.pallas_call(functools.partial(late_kernel, total, tok, items, len(sour...  5.49 us
    pallas_call x1, Pallas kernels, project(): pl.pallas_call(functools.partial(project_kernel, steps), out_shape=tuple(...  3.1 us
    pallas_call x1, Pallas kernels, early(): pl.pallas_call(functools.partial(early_kernel, total, tok, len(sources)),...  2.2 us
    pallas_call x2, Pallas kernels, mix(): pl.pallas_call(functools.partial(mix_kernel, before is not None), out_sha...  1.25 us
    ppermute x5, starting transfers between devices, swap(): return lax.ppermute(array, 'head', [(0, 1), (1, 0)])  1.02 us
    ppermute x5, waiting for transfers between devices, swap(): return lax.ppermute(array, 'head', [(0, 1), (1, 0)])  0.89 us
  transfers between devices with their start and end apart: 17, of which 8 were waited for; matrix products, arithmetic and copies ran while one was open for 0% of the time, Pallas kernels for 21%

profile of v7, /device:TPU:0, one launch (start us, length us, event | category | flops | bytes accessed | tf_op | source)
XLA Modules:
  0.0 40.9 jit_solution(5692956357914655483)
XLA Ops:
  0.0 0.5 %collective-permute-start = (bf16[512,1024]{1,0:T(8,128)(2,1)}, bf16[512,1024]{1,0:T(8,128)(2,1)S(1)}, u32[]{:S(2)}, u32[]{:S(2)}) collective-permute-start(bf16[512,1024]{1,0:T(8,128)(2,1)} %refs_4_.1), channel_id=1, source_target_pairs={{0,1},{1,0},{2,3},{3,2},{4,5},{5,4},{6,7},{7,6},{8,9},{9,8},{10,11... | collective-permute-start | bytes 3145736 | tf_op jit(solution)/shard_map/ppermute | solution.py:310
  0.5 3.1 %project.1 = (bf16[200,256]{1,0:T(8,128)(2,1)S(1)}, bf16[136,256]{1,0:T(8,128)(2,1)S(1)}, bf16[64,256]{1,0:T(8,128)(2,1)S(1)}, bf16[200,256]{1,0:T(8,128)(2,1)S(1)}, bf16[200,256]{1,0:T(8,128)(2,1)S(1)}) custom-call(bf16[128,1024]{1,0:T(8,128)(2,1)} %tok_hbm.1, s32[1,128]{1,0:T(1,128)} %bitcast.1, s32[2,128]{1,0:T(2,128)} %cid_hbm.1, ...), custom_call_target="tpu_custom_call" | custom-call | flops 402653184 | bytes 3145728 | tf_op jit(solution)/shard_map/project/pallas_call | solution.py:77
  3.6 2.6 %collective-permute-start.1 = (bf16[200,256]{1,0:T(8,128)(2,1)S(1)}, bf16[200,256]{1,0:T(8,128)(2,1)S(1)}, u32[]{:S(2)}, u32[]{:S(2)}) collective-permute-start(bf16[200,256]{1,0:T(8,128)(2,1)S(1)} %get-tuple-element.29), channel_id=1, source_target_pairs={{0,8},{2,10},{4,12},{6,14},{8,0},{10,2},{12,4},{14,6},{16,24},{18,... | collective-permute-start | bytes 307208 | tf_op jit(solution)/shard_map/ppermute | solution.py:307
  6.2 2.6 %collective-permute-start.2 = (bf16[200,256]{1,0:T(8,128)(2,1)S(1)}, bf16[200,256]{1,0:T(8,128)(2,1)S(1)}, u32[]{:S(2)}, u32[]{:S(2)}) collective-permute-start(bf16[200,256]{1,0:T(8,128)(2,1)S(1)} %get-tuple-element.30), channel_id=1, source_target_pairs={{0,16},{2,18},{4,20},{6,22},{8,24},{10,26},{12,28},{14,30},{16,0},... | collective-permute-start | bytes 307208 | tf_op jit(solution)/shard_map/ppermute | solution.py:307
  8.8 0.0 collective-permute-start.3
  8.8 0.0 collective-permute-done.refs_4_
  8.8 1.0 %collective-permute-done.1.second_ref.refs_1_.refs_0_ = bf16[200,256]{1,0:T(8,128)(2,1)S(1)} collective-permute-done((bf16[200,256]{1,0:T(8,128)(2,1)S(1)}, bf16[200,256]{1,0:T(8,128)(2,1)S(1)}, u32[]{:S(2)}, u32[]{:S(2)}) %collective-permute-start.1) | collective-permute-done | bytes 102432 | tf_op jit(solution)/shard_map/ppermute | solution.py:307
  9.8 1.8 %collective-permute-start.4 = (bf16[264,256]{1,0:T(8,128)(2,1)S(1)}, bf16[264,256]{1,0:T(8,128)(2,1)S(1)}, u32[]{:S(2)}, u32[]{:S(2)}) collective-permute-start(bf16[264,256]{1,0:T(8,128)(2,1)S(1)} %pack.2.refs_4_.refs_1_), channel_id=1, source_target_pairs={{0,4},{2,6},{4,0},{6,2},{8,12},{10,14},{12,8},{14,10},{16,20},{18,... | collective-permute-start | bytes 405512 | tf_op jit(solution)/shard_map/ppermute | solution.py:307
  11.5 1.5 %collective-permute-start.5 = (bf16[264,256]{1,0:T(8,128)(2,1)S(1)}, bf16[264,256]{1,0:T(8,128)(2,1)S(1)}, u32[]{:S(2)}, u32[]{:S(2)}) collective-permute-start(bf16[264,256]{1,0:T(8,128)(2,1)S(1)} %pack.2.refs_4_.refs_1_), channel_id=1, source_target_pairs={{0,2},{2,0},{4,6},{6,4},{8,10},{10,8},{12,14},{14,12},{16,18},{18,... | collective-permute-start | bytes 405512 | tf_op jit(solution)/shard_map/ppermute | solution.py:307
  13.0 0.3 collective-permute-start.6
  13.3 3.9 %collective-permute-done.2.first_ref.refs_2_.refs_0_ = bf16[200,256]{1,0:T(8,128)(2,1)S(1)} collective-permute-done((bf16[200,256]{1,0:T(8,128)(2,1)S(1)}, bf16[200,256]{1,0:T(8,128)(2,1)S(1)}, u32[]{:S(2)}, u32[]{:S(2)}) %collective-permute-start.2) | collective-permute-done | bytes 102432 | tf_op jit(solution)/shard_map/ppermute | solution.py:307
  17.2 0.0 collective-permute-done.3.second_ref.refs_3_.refs_0_
  17.2 0.0 collective-permute-done.4.refs_7_
  17.2 2.5 %collective-permute-start.7 = (bf16[264,256]{1,0:T(8,128)(2,1)S(1)}, bf16[264,256]{1,0:T(8,128)(2,1)S(1)}, u32[]{:S(2)}, u32[]{:S(2)}) collective-permute-start(bf16[264,256]{1,0:T(8,128)(2,1)S(1)} %pack.3.refs_5_.refs_1_), channel_id=1, source_target_pairs={{0,6},{2,4},{4,2},{6,0},{8,14},{10,12},{12,10},{14,8},{16,22},{18,... | collective-permute-start | bytes 405512 | tf_op jit(solution)/shard_map/ppermute | solution.py:307
  19.8 0.5 %collective-permute-start.8 = (bf16[264,256]{1,0:T(8,128)(2,1)S(1)}, bf16[264,256]{1,0:T(8,128)(2,1)S(1)}, u32[]{:S(2)}, u32[]{:S(2)}) collective-permute-start(bf16[264,256]{1,0:T(8,128)(2,1)S(1)} %pack.3.refs_5_.refs_1_), channel_id=1, source_target_pairs={{0,2},{2,0},{4,6},{6,4},{8,10},{10,8},{12,14},{14,12},{16,18},{18,... | collective-permute-start | bytes 405512 | tf_op jit(solution)/shard_map/ppermute | solution.py:307
  20.3 0.5 %collective-permute-start.9 = (bf16[264,256]{1,0:T(8,128)(2,1)S(1)}, bf16[264,256]{1,0:T(8,128)(2,1)S(1)}, u32[]{:S(2)}, u32[]{:S(2)}) collective-permute-start(bf16[264,256]{1,0:T(8,128)(2,1)S(1)} %pack.3.refs_5_.refs_1_), channel_id=1, source_target_pairs={{0,4},{2,6},{4,0},{6,2},{8,12},{10,14},{12,8},{14,10},{16,20},{18,... | collective-permute-start | bytes 405512 | tf_op jit(solution)/shard_map/ppermute | solution.py:307
  20.8 0.0 collective-permute-done.5.refs_6_
  20.8 0.0 collective-permute-done.6.refs_8_
  20.8 2.2 %early.1 = (f32[1024,1280]{1,0:T(8,128)S(1)}, f32[1024,128]{1,0:T(8,128)S(1)}, bf16[1280,128]{1,0:T(8,128)(2,1)S(1)}) custom-call(bf16[64,256]{1,0:T(8,128)(2,1)S(1)} %get-tuple-element.26.refs_0_, bf16[200,256]{1,0:T(8,128)(2,1)S(1)} %collective-permute-done.1.second_ref.refs_1_.refs_0_, ...), custom_call_target="tpu_custom_call" | custom-call | flops 8000000000 | bytes 1310720 | tf_op jit(solution)/shard_map/early/pallas_call | solution.py:192
  23.0 1.1 %collective-permute-done.7.refs_5_ = bf16[264,256]{1,0:T(8,128)(2,1)S(1)} collective-permute-done((bf16[264,256]{1,0:T(8,128)(2,1)S(1)}, bf16[264,256]{1,0:T(8,128)(2,1)S(1)}, u32[]{:S(2)}, u32[]{:S(2)}) %collective-permute-start.7) | collective-permute-done | bytes 135200 | tf_op jit(solution)/shard_map/ppermute | solution.py:307
  24.1 1.4 %collective-permute-done.8.refs_6_ = bf16[264,256]{1,0:T(8,128)(2,1)S(1)} collective-permute-done((bf16[264,256]{1,0:T(8,128)(2,1)S(1)}, bf16[264,256]{1,0:T(8,128)(2,1)S(1)}, u32[]{:S(2)}, u32[]{:S(2)}) %collective-permute-start.8) | collective-permute-done | bytes 135200 | tf_op jit(solution)/shard_map/ppermute | solution.py:307
  25.5 0.0 collective-permute-done.9.refs_7_
  25.6 1.4 %late.4 = bf16[128,128]{1,0:T(8,128)(2,1)S(1)} custom-call(bf16[200,256]{1,0:T(8,128)(2,1)S(1)} %collective-permute-done.3.second_ref.refs_3_.refs_0_, bf16[264,256]{1,0:T(8,128)(2,1)S(1)} %pack.3.refs_5_.refs_1_, f32[1024,1280]{1,0:T(8,128)S(1)} %get-tuple-element.34.refs_2_, f32[1024,128]{1,0:T(8,128)S(1)} %get-tuple-element.39.refs_3_, ...), custom_call_target="tpu_custom_call" | custom-call | flops 3000000000 | bytes 393216 | tf_op jit(solution)/shard_map/late/pallas_call | solution.py:247
  26.9 1.4 %late.5 = bf16[128,128]{1,0:T(8,128)(2,1)S(1)} custom-call(bf16[200,256]{1,0:T(8,128)(2,1)S(1)} %collective-permute-done.2.first_ref.refs_2_.refs_0_, bf16[264,256]{1,0:T(8,128)(2,1)S(1)} %pack.3.refs_5_.refs_1_, f32[1024,1280]{1,0:T(8,128)S(1)} %get-tuple-element.34.refs_2_, f32[1024,128]{1,0:T(8,128)S(1)} %get-tuple-element.39.refs_3_, ...), custom_call_target="tpu_custom_call" | custom-call | flops 3000000000 | bytes 393216 | tf_op jit(solution)/shard_map/late/pallas_call | solution.py:247
  28.3 3.7 %collective-permute-start.13 = (bf16[128,128]{1,0:T(8,128)(2,1)S(1)}, bf16[128,128]{1,0:T(8,128)(2,1)S(1)}, u32[]{:S(2)}, u32[]{:S(2)}) collective-permute-start(bf16[128,128]{1,0:T(8,128)(2,1)S(1)} %late.5), channel_id=1, source_target_pairs={{0,16},{2,18},{4,20},{6,22},{8,24},{10,26},{12,28},{14,30},{16,0},... | collective-permute-start | bytes 98312 | tf_op jit(solution)/shard_map/ppermute | solution.py:307
  32.0 1.3 %collective-permute-start.15 = (bf16[128,128]{1,0:T(8,128)(2,1)S(1)}, bf16[128,128]{1,0:T(8,128)(2,1)S(1)}, u32[]{:S(2)}, u32[]{:S(2)}) collective-permute-start(bf16[128,128]{1,0:T(8,128)(2,1)S(1)} %late.4), channel_id=1, source_target_pairs={{0,24},{2,26},{4,28},{6,30},{8,16},{10,18},{12,20},{14,22},{16,8},... | collective-permute-start | bytes 98312 | tf_op jit(solution)/shard_map/ppermute | solution.py:307
  33.3 1.4 %late.6 = bf16[128,128]{1,0:T(8,128)(2,1)S(1)} custom-call(bf16[200,256]{1,0:T(8,128)(2,1)S(1)} %collective-permute-done.1.second_ref.refs_1_.refs_0_, bf16[264,256]{1,0:T(8,128)(2,1)S(1)} %pack.2.refs_4_.refs_1_, f32[1024,1280]{1,0:T(8,128)S(1)} %get-tuple-element.34.refs_2_, f32[1024,128]{1,0:T(8,128)S(1)} %get-tuple-element.39.refs_3_, ...), custom_call_target="tpu_custom_call" | custom-call | flops 3000000000 | bytes 393216 | tf_op jit(solution)/shard_map/late/pallas_call | solution.py:247
  34.7 0.0 copy-start
  34.7 0.1 collective-permute-start.11
  34.8 1.4 %late.7.refs_0_ = bf16[128,128]{1,0:T(8,128)(2,1)S(1)} custom-call(bf16[64,256]{1,0:T(8,128)(2,1)S(1)} %get-tuple-element.26.refs_0_, bf16[264,256]{1,0:T(8,128)(2,1)S(1)} %pack.2.refs_4_.refs_1_, f32[1024,1280]{1,0:T(8,128)S(1)} %get-tuple-element.34.refs_2_, f32[1024,128]{1,0:T(8,128)S(1)} %get-tuple-element.39.refs_3_, ...), custom_call_target="tpu_custom_call" | custom-call | flops 3000000000 | bytes 393216 | tf_op jit(solution)/shard_map/late/pallas_call | solution.py:247
  36.2 0.1 collective-permute-start.10
  36.2 0.0 collective-permute-done.13.refs_2_
  36.3 0.5 %collective-permute-start.14 = (bf16[128,128]{1,0:T(8,128)(2,1)S(1)}, bf16[128,128]{1,0:T(8,128)(2,1)S(1)}, u32[]{:S(2)}, u32[]{:S(2)}) collective-permute-start(bf16[128,128]{1,0:T(8,128)(2,1)S(1)} %collective-permute-done.13.refs_2_), channel_id=1, source_target_pairs={{0,1},{1,0},{2,3},{3,2},{4,5},{5,4},{6,7},{7,6},{8,9},{9,8},{10,11... | collective-permute-start | bytes 98312 | tf_op jit(solution)/shard_map/ppermute | solution.py:310
  36.8 1.1 %collective-permute-done.15.refs_3_ = bf16[128,128]{1,0:T(8,128)(2,1)S(1)} collective-permute-done((bf16[128,128]{1,0:T(8,128)(2,1)S(1)}, bf16[128,128]{1,0:T(8,128)(2,1)S(1)}, u32[]{:S(2)}, u32[]{:S(2)}) %collective-permute-start.15) | collective-permute-done | bytes 32800 | tf_op jit(solution)/shard_map/ppermute | solution.py:307
  37.9 0.0 collective-permute-start.16
  37.9 0.8 %collective-permute-done.11.refs_1_ = bf16[128,128]{1,0:T(8,128)(2,1)S(1)} collective-permute-done((bf16[128,128]{1,0:T(8,128)(2,1)S(1)}, bf16[128,128]{1,0:T(8,128)(2,1)S(1)}, u32[]{:S(2)}, u32[]{:S(2)}) %collective-permute-start.11) | collective-permute-done | bytes 32800 | tf_op jit(solution)/shard_map/ppermute | solution.py:307
  38.7 0.0 collective-permute-start.12
  38.7 0.0 copy-done
  38.7 0.3 mix.2.refs_5_
  39.0 0.0 collective-permute-done.10.refs_0_
  39.0 0.0 collective-permute-done.14.refs_2_
  39.0 0.1 collective-permute-done.16.refs_3_
  39.1 0.8 %collective-permute-done.12.refs_1_ = bf16[128,128]{1,0:T(8,128)(2,1)S(1)} collective-permute-done((bf16[128,128]{1,0:T(8,128)(2,1)S(1)}, bf16[128,128]{1,0:T(8,128)(2,1)S(1)}, u32[]{:S(2)}, u32[]{:S(2)}) %collective-permute-start.12) | collective-permute-done | bytes 32800 | tf_op jit(solution)/shard_map/ppermute | solution.py:310
  39.9 1.0 %mix.3 = bf16[64,1024]{1,0:T(8,128)(2,1)} custom-call(bf16[128,128]{1,0:T(8,128)(2,1)S(1)} %collective-permute-done.10.refs_0_, bf16[128,128]{1,0:T(8,128)(2,1)S(1)} %collective-permute-done.12.refs_1_, bf16[128,128]{1,0:T(8,128)(2,1)S(1)} %collective-permute-done.14.refs_2_, bf16[128,128]{1,0:T(8,128)(2,1)S(1)} %collective-permute-done.16.refs_3_, ...), custom_call_target="tpu_custom_call" | custom-call | flops 67108864 | bytes 1048576 | tf_op jit(solution)/shard_map/mix/pallas_call | solution.py:288
  (2 shorter events, 0.0 us)
Async XLA Ops:
  0.0 8.8 %collective-permute-start = (bf16[512,1024]{1,0:T(8,128)(2,1)}, bf16[512,1024]{1,0:T(8,128)(2,1)S(1)}, u32[]{:S(2)}, u32[]{:S(2)}) collective-permute-start(bf16[512,1024]{1,0:T(8,128)(2,1)} %refs_4_.1), channel_id=1, source_target_pairs={{0,1},{1,0},{2,3},{3,2},{4,5},{5,4},{6,7},{7,6},{8,9},{9,8},{10,11... | collective-permute-start | bytes 3145736 | tf_op jit(solution)/shard_map/ppermute | solution.py:310
  3.6 6.2 %collective-permute-start.1 = (bf16[200,256]{1,0:T(8,128)(2,1)S(1)}, bf16[200,256]{1,0:T(8,128)(2,1)S(1)}, u32[]{:S(2)}, u32[]{:S(2)}) collective-permute-start(bf16[200,256]{1,0:T(8,128)(2,1)S(1)} %get-tuple-element.29), channel_id=1, source_target_pairs={{0,8},{2,10},{4,12},{6,14},{8,0},{10,2},{12,4},{14,6},{16,24},{18,... | collective-permute-start | bytes 307208 | tf_op jit(solution)/shard_map/ppermute | solution.py:307
  6.2 11.0 %collective-permute-start.2 = (bf16[200,256]{1,0:T(8,128)(2,1)S(1)}, bf16[200,256]{1,0:T(8,128)(2,1)S(1)}, u32[]{:S(2)}, u32[]{:S(2)}) collective-permute-start(bf16[200,256]{1,0:T(8,128)(2,1)S(1)} %get-tuple-element.30), channel_id=1, source_target_pairs={{0,16},{2,18},{4,20},{6,22},{8,24},{10,26},{12,28},{14,30},{16,0},... | collective-permute-start | bytes 307208 | tf_op jit(solution)/shard_map/ppermute | solution.py:307
  8.8 8.4 %collective-permute-start.3 = (bf16[200,256]{1,0:T(8,128)(2,1)S(1)}, bf16[200,256]{1,0:T(8,128)(2,1)S(1)}, u32[]{:S(2)}, u32[]{:S(2)}) collective-permute-start(bf16[200,256]{1,0:T(8,128)(2,1)S(1)} %get-tuple-element.31), channel_id=1, source_target_pairs={{0,24},{2,26},{4,28},{6,30},{8,16},{10,18},{12,20},{14,22},{16,8},... | collective-permute-start | bytes 307208 | tf_op jit(solution)/shard_map/ppermute | solution.py:307
  9.8 7.5 %collective-permute-start.4 = (bf16[264,256]{1,0:T(8,128)(2,1)S(1)}, bf16[264,256]{1,0:T(8,128)(2,1)S(1)}, u32[]{:S(2)}, u32[]{:S(2)}) collective-permute-start(bf16[264,256]{1,0:T(8,128)(2,1)S(1)} %pack.2.refs_4_.refs_1_), channel_id=1, source_target_pairs={{0,4},{2,6},{4,0},{6,2},{8,12},{10,14},{12,8},{14,10},{16,20},{18,... | collective-permute-start | bytes 405512 | tf_op jit(solution)/shard_map/ppermute | solution.py:307
  11.5 9.3 %collective-permute-start.5 = (bf16[264,256]{1,0:T(8,128)(2,1)S(1)}, bf16[264,256]{1,0:T(8,128)(2,1)S(1)}, u32[]{:S(2)}, u32[]{:S(2)}) collective-permute-start(bf16[264,256]{1,0:T(8,128)(2,1)S(1)} %pack.2.refs_4_.refs_1_), channel_id=1, source_target_pairs={{0,2},{2,0},{4,6},{6,4},{8,10},{10,8},{12,14},{14,12},{16,18},{18,... | collective-permute-start | bytes 405512 | tf_op jit(solution)/shard_map/ppermute | solution.py:307
  13.0 7.8 %collective-permute-start.6 = (bf16[264,256]{1,0:T(8,128)(2,1)S(1)}, bf16[264,256]{1,0:T(8,128)(2,1)S(1)}, u32[]{:S(2)}, u32[]{:S(2)}) collective-permute-start(bf16[264,256]{1,0:T(8,128)(2,1)S(1)} %pack.2.refs_4_.refs_1_), channel_id=1, source_target_pairs={{0,6},{2,4},{4,2},{6,0},{8,14},{10,12},{12,10},{14,8},{16,22},{18,... | collective-permute-start | bytes 405512 | tf_op jit(solution)/shard_map/ppermute | solution.py:307
  17.2 6.9 %collective-permute-start.7 = (bf16[264,256]{1,0:T(8,128)(2,1)S(1)}, bf16[264,256]{1,0:T(8,128)(2,1)S(1)}, u32[]{:S(2)}, u32[]{:S(2)}) collective-permute-start(bf16[264,256]{1,0:T(8,128)(2,1)S(1)} %pack.3.refs_5_.refs_1_), channel_id=1, source_target_pairs={{0,6},{2,4},{4,2},{6,0},{8,14},{10,12},{12,10},{14,8},{16,22},{18,... | collective-permute-start | bytes 405512 | tf_op jit(solution)/shard_map/ppermute | solution.py:307
  19.8 5.8 %collective-permute-start.8 = (bf16[264,256]{1,0:T(8,128)(2,1)S(1)}, bf16[264,256]{1,0:T(8,128)(2,1)S(1)}, u32[]{:S(2)}, u32[]{:S(2)}) collective-permute-start(bf16[264,256]{1,0:T(8,128)(2,1)S(1)} %pack.3.refs_5_.refs_1_), channel_id=1, source_target_pairs={{0,2},{2,0},{4,6},{6,4},{8,10},{10,8},{12,14},{14,12},{16,18},{18,... | collective-permute-start | bytes 405512 | tf_op jit(solution)/shard_map/ppermute | solution.py:307
  20.3 5.3 %collective-permute-start.9 = (bf16[264,256]{1,0:T(8,128)(2,1)S(1)}, bf16[264,256]{1,0:T(8,128)(2,1)S(1)}, u32[]{:S(2)}, u32[]{:S(2)}) collective-permute-start(bf16[264,256]{1,0:T(8,128)(2,1)S(1)} %pack.3.refs_5_.refs_1_), channel_id=1, source_target_pairs={{0,4},{2,6},{4,0},{6,2},{8,12},{10,14},{12,8},{14,10},{16,20},{18,... | collective-permute-start | bytes 405512 | tf_op jit(solution)/shard_map/ppermute | solution.py:307
  28.3 7.9 %collective-permute-start.13 = (bf16[128,128]{1,0:T(8,128)(2,1)S(1)}, bf16[128,128]{1,0:T(8,128)(2,1)S(1)}, u32[]{:S(2)}, u32[]{:S(2)}) collective-permute-start(bf16[128,128]{1,0:T(8,128)(2,1)S(1)} %late.5), channel_id=1, source_target_pairs={{0,16},{2,18},{4,20},{6,22},{8,24},{10,26},{12,28},{14,30},{16,0},... | collective-permute-start | bytes 98312 | tf_op jit(solution)/shard_map/ppermute | solution.py:307
  32.0 5.8 %collective-permute-start.15 = (bf16[128,128]{1,0:T(8,128)(2,1)S(1)}, bf16[128,128]{1,0:T(8,128)(2,1)S(1)}, u32[]{:S(2)}, u32[]{:S(2)}) collective-permute-start(bf16[128,128]{1,0:T(8,128)(2,1)S(1)} %late.4), channel_id=1, source_target_pairs={{0,24},{2,26},{4,28},{6,30},{8,16},{10,18},{12,20},{14,22},{16,8},... | collective-permute-start | bytes 98312 | tf_op jit(solution)/shard_map/ppermute | solution.py:307
  34.7 4.0 %copy-start = (bf16[512,1024]{1,0:T(8,128)(2,1)S(1)}, bf16[512,1024]{1,0:T(8,128)(2,1)}, u32[]{:S(2)}) copy-start(bf16[512,1024]{1,0:T(8,128)(2,1)} %refs_4_.1) | copy-start | bytes 3145732
  34.7 4.0 %collective-permute-start.11 = (bf16[128,128]{1,0:T(8,128)(2,1)S(1)}, bf16[128,128]{1,0:T(8,128)(2,1)S(1)}, u32[]{:S(2)}, u32[]{:S(2)}) collective-permute-start(bf16[128,128]{1,0:T(8,128)(2,1)S(1)} %late.6), channel_id=1, source_target_pairs={{0,8},{2,10},{4,12},{6,14},{8,0},{10,2},{12,4},{14,6},{16,24},{18,... | collective-permute-start | bytes 98312 | tf_op jit(solution)/shard_map/ppermute | solution.py:307
  36.2 2.8 %collective-permute-start.10 = (bf16[128,128]{1,0:T(8,128)(2,1)S(1)}, bf16[128,128]{1,0:T(8,128)(2,1)S(1)}, u32[]{:S(2)}, u32[]{:S(2)}) collective-permute-start(bf16[128,128]{1,0:T(8,128)(2,1)S(1)} %late.7.refs_0_), channel_id=1, source_target_pairs={{0,1},{1,0},{2,3},{3,2},{4,5},{5,4},{6,7},{7,6},{8,9},{9,8},{10,11... | collective-permute-start | bytes 98312 | tf_op jit(solution)/shard_map/ppermute | solution.py:310
  36.3 2.7 %collective-permute-start.14 = (bf16[128,128]{1,0:T(8,128)(2,1)S(1)}, bf16[128,128]{1,0:T(8,128)(2,1)S(1)}, u32[]{:S(2)}, u32[]{:S(2)}) collective-permute-start(bf16[128,128]{1,0:T(8,128)(2,1)S(1)} %collective-permute-done.13.refs_2_), channel_id=1, source_target_pairs={{0,1},{1,0},{2,3},{3,2},{4,5},{5,4},{6,7},{7,6},{8,9},{9,8},{10,11... | collective-permute-start | bytes 98312 | tf_op jit(solution)/shard_map/ppermute | solution.py:310
  37.9 1.2 %collective-permute-start.16 = (bf16[128,128]{1,0:T(8,128)(2,1)S(1)}, bf16[128,128]{1,0:T(8,128)(2,1)S(1)}, u32[]{:S(2)}, u32[]{:S(2)}) collective-permute-start(bf16[128,128]{1,0:T(8,128)(2,1)S(1)} %collective-permute-done.15.refs_3_), channel_id=1, source_target_pairs={{0,1},{1,0},{2,3},{3,2},{4,5},{5,4},{6,7},{7,6},{8,9},{9,8},{10,11... | collective-permute-start | bytes 98312 | tf_op jit(solution)/shard_map/ppermute | solution.py:310
  38.7 1.2 %collective-permute-start.12 = (bf16[128,128]{1,0:T(8,128)(2,1)S(1)}, bf16[128,128]{1,0:T(8,128)(2,1)S(1)}, u32[]{:S(2)}, u32[]{:S(2)}) collective-permute-start(bf16[128,128]{1,0:T(8,128)(2,1)S(1)} %collective-permute-done.11.refs_1_), channel_id=1, source_target_pairs={{0,1},{1,0},{2,3},{3,2},{4,5},{5,4},{6,7},{7,6},{8,9},{9,8},{10,11... | collective-permute-start | bytes 98312 | tf_op jit(solution)/shard_map/ppermute | solution.py:310

commit v8 on v7

--- a/solution.py
+++ b/solution.py
@@ -309,9 +309,10 @@
     def swap(array):
         return lax.ppermute(array, "head", [(0, 1), (1, 0)])
 
-    w_other = swap(w_out)
     weights = (w_query, w_key, w_value)
     m1, kv0, q0, m3, m2 = project((1, 0, 3, 2), tokens, positions, cluster_ids, weights)
+    m1, w_late = lax.optimization_barrier((m1, w_out))
+    w_other = swap(w_late)
     r1, r3, r2 = send(m1, PLANE), send(m3, 3 * PLANE), send(m2, 2 * PLANE)
     kv0, w_other = lax.optimization_barrier((kv0, w_other))
     near = pack(kv0, r1, tok, 0)

time: 41 us -> 40.9 us (level)
  transfers between devices with their start and end apart: 17 -> 17, of which waited for: 8 -> 8; matrix products, arithmetic and copies ran while one was open for 0% -> 0% of each run, Pallas kernels for 21% -> 13%
where the time goes in v8:
time: 40.9 us; the launch traced here: 40.8 us
  starting transfers between devices  18.5 us (45%)
  Pallas kernels  12.1 us (30%)
  waiting for transfers between devices  10.1 us (25%)
    ppermute x12, starting transfers between devices, send(): return lax.ppermute(array, 'seq', [(i, i ^ bits) for i in range(owners)])  17.4 us
    ppermute x12, waiting for transfers between devices, send(): return lax.ppermute(array, 'seq', [(i, i ^ bits) for i in range(owners)])  9.19 us
    pallas_call x4, Pallas kernels, late(): pl.pallas_call(functools.partial(late_kernel, total, tok, items, len(sour...  5.48 us
    pallas_call x1, Pallas kernels, project(): pl.pallas_call(functools.partial(project_kernel, steps), out_shape=tuple(...  3.1 us
    pallas_call x1, Pallas kernels, early(): pl.pallas_call(functools.partial(early_kernel, total, tok, len(sources)),...  2.2 us
    pallas_call x2, Pallas kernels, mix(): pl.pallas_call(functools.partial(mix_kernel, before is not None), out_sha...  1.25 us
    ppermute x5, starting transfers between devices, swap(): return lax.ppermute(array, 'head', [(0, 1), (1, 0)])  1.09 us
    ppermute x5, waiting for transfers between devices, swap(): return lax.ppermute(array, 'head', [(0, 1), (1, 0)])  0.89 us
  transfers between devices with their start and end apart: 17, of which 8 were waited for; matrix products, arithmetic and copies ran while one was open for 0% of the time, Pallas kernels for 13%

profile of v8, /device:TPU:0, one launch (start us, length us, event | category | flops | bytes accessed | tf_op | source)
XLA Modules:
  0.0 40.8 jit_solution(2346044865435600780)
XLA Ops:
  0.0 3.1 %project.1 = (bf16[200,256]{1,0:T(8,128)(2,1)S(1)}, bf16[136,256]{1,0:T(8,128)(2,1)S(1)}, bf16[64,256]{1,0:T(8,128)(2,1)S(1)}, bf16[200,256]{1,0:T(8,128)(2,1)S(1)}, bf16[200,256]{1,0:T(8,128)(2,1)S(1)}) custom-call(bf16[128,1024]{1,0:T(8,128)(2,1)} %tok_hbm.1, s32[1,128]{1,0:T(1,128)} %bitcast.1, s32[2,128]{1,0:T(2,128)} %cid_hbm.1, ...), custom_call_target="tpu_custom_call" | custom-call | flops 402653184 | bytes 3145728 | tf_op jit(solution)/shard_map/project/pallas_call | solution.py:77
  3.1 0.5 %collective-permute-start = (bf16[512,1024]{1,0:T(8,128)(2,1)}, bf16[512,1024]{1,0:T(8,128)(2,1)S(1)}, u32[]{:S(2)}, u32[]{:S(2)}) collective-permute-start(bf16[512,1024]{1,0:T(8,128)(2,1)} %refs_4_.1), channel_id=1, source_target_pairs={{0,1},{1,0},{2,3},{3,2},{4,5},{5,4},{6,7},{7,6},{8,9},{9,8},{10,11... | collective-permute-start | bytes 3145736 | tf_op jit(solution)/shard_map/ppermute | solution.py:310
  3.6 2.6 %collective-permute-start.1 = (bf16[200,256]{1,0:T(8,128)(2,1)S(1)}, bf16[200,256]{1,0:T(8,128)(2,1)S(1)}, u32[]{:S(2)}, u32[]{:S(2)}) collective-permute-start(bf16[200,256]{1,0:T(8,128)(2,1)S(1)} %get-tuple-element.33), channel_id=1, source_target_pairs={{0,8},{2,10},{4,12},{6,14},{8,0},{10,2},{12,4},{14,6},{16,24},{18,... | collective-permute-start | bytes 307208 | tf_op jit(solution)/shard_map/ppermute | solution.py:307
  6.3 2.6 %collective-permute-start.2 = (bf16[200,256]{1,0:T(8,128)(2,1)S(1)}, bf16[200,256]{1,0:T(8,128)(2,1)S(1)}, u32[]{:S(2)}, u32[]{:S(2)}) collective-permute-start(bf16[200,256]{1,0:T(8,128)(2,1)S(1)} %get-tuple-element.34), channel_id=1, source_target_pairs={{0,16},{2,18},{4,20},{6,22},{8,24},{10,26},{12,28},{14,30},{16,0},... | collective-permute-start | bytes 307208 | tf_op jit(solution)/shard_map/ppermute | solution.py:307
  8.9 0.0 collective-permute-start.3
  8.9 0.0 collective-permute-done.refs_4_
  8.9 0.9 %collective-permute-done.1.second_ref.refs_1_.refs_0_ = bf16[200,256]{1,0:T(8,128)(2,1)S(1)} collective-permute-done((bf16[200,256]{1,0:T(8,128)(2,1)S(1)}, bf16[200,256]{1,0:T(8,128)(2,1)S(1)}, u32[]{:S(2)}, u32[]{:S(2)}) %collective-permute-start.1) | collective-permute-done | bytes 102432 | tf_op jit(solution)/shard_map/ppermute | solution.py:307
  9.8 1.8 %collective-permute-start.4 = (bf16[264,256]{1,0:T(8,128)(2,1)S(1)}, bf16[264,256]{1,0:T(8,128)(2,1)S(1)}, u32[]{:S(2)}, u32[]{:S(2)}) collective-permute-start(bf16[264,256]{1,0:T(8,128)(2,1)S(1)} %pack.2.refs_4_.refs_1_), channel_id=1, source_target_pairs={{0,4},{2,6},{4,0},{6,2},{8,12},{10,14},{12,8},{14,10},{16,20},{18,... | collective-permute-start | bytes 405512 | tf_op jit(solution)/shard_map/ppermute | solution.py:307
  11.5 1.5 %collective-permute-start.5 = (bf16[264,256]{1,0:T(8,128)(2,1)S(1)}, bf16[264,256]{1,0:T(8,128)(2,1)S(1)}, u32[]{:S(2)}, u32[]{:S(2)}) collective-permute-start(bf16[264,256]{1,0:T(8,128)(2,1)S(1)} %pack.2.refs_4_.refs_1_), channel_id=1, source_target_pairs={{0,2},{2,0},{4,6},{6,4},{8,10},{10,8},{12,14},{14,12},{16,18},{18,... | collective-permute-start | bytes 405512 | tf_op jit(solution)/shard_map/ppermute | solution.py:307
  13.0 0.3 collective-permute-start.6
  13.3 4.0 %collective-permute-done.2.first_ref.refs_2_.refs_0_ = bf16[200,256]{1,0:T(8,128)(2,1)S(1)} collective-permute-done((bf16[200,256]{1,0:T(8,128)(2,1)S(1)}, bf16[200,256]{1,0:T(8,128)(2,1)S(1)}, u32[]{:S(2)}, u32[]{:S(2)}) %collective-permute-start.2) | collective-permute-done | bytes 102432 | tf_op jit(solution)/shard_map/ppermute | solution.py:307
  17.3 0.0 collective-permute-done.3.second_ref.refs_3_.refs_0_
  17.3 0.0 collective-permute-done.4.refs_7_
  17.3 2.5 %collective-permute-start.7 = (bf16[264,256]{1,0:T(8,128)(2,1)S(1)}, bf16[264,256]{1,0:T(8,128)(2,1)S(1)}, u32[]{:S(2)}, u32[]{:S(2)}) collective-permute-start(bf16[264,256]{1,0:T(8,128)(2,1)S(1)} %pack.3.refs_5_.refs_1_), channel_id=1, source_target_pairs={{0,6},{2,4},{4,2},{6,0},{8,14},{10,12},{12,10},{14,8},{16,22},{18,... | collective-permute-start | bytes 405512 | tf_op jit(solution)/shard_map/ppermute | solution.py:307
  19.8 0.5 %collective-permute-start.8 = (bf16[264,256]{1,0:T(8,128)(2,1)S(1)}, bf16[264,256]{1,0:T(8,128)(2,1)S(1)}, u32[]{:S(2)}, u32[]{:S(2)}) collective-permute-start(bf16[264,256]{1,0:T(8,128)(2,1)S(1)} %pack.3.refs_5_.refs_1_), channel_id=1, source_target_pairs={{0,2},{2,0},{4,6},{6,4},{8,10},{10,8},{12,14},{14,12},{16,18},{18,... | collective-permute-start | bytes 405512 | tf_op jit(solution)/shard_map/ppermute | solution.py:307
  20.4 0.5 %collective-permute-start.9 = (bf16[264,256]{1,0:T(8,128)(2,1)S(1)}, bf16[264,256]{1,0:T(8,128)(2,1)S(1)}, u32[]{:S(2)}, u32[]{:S(2)}) collective-permute-start(bf16[264,256]{1,0:T(8,128)(2,1)S(1)} %pack.3.refs_5_.refs_1_), channel_id=1, source_target_pairs={{0,4},{2,6},{4,0},{6,2},{8,12},{10,14},{12,8},{14,10},{16,20},{18,... | collective-permute-start | bytes 405512 | tf_op jit(solution)/shard_map/ppermute | solution.py:307
  20.9 0.0 collective-permute-done.5.refs_6_
  20.9 0.0 collective-permute-done.6.refs_8_
  20.9 2.2 %early.1 = (f32[1024,1280]{1,0:T(8,128)S(1)}, f32[1024,128]{1,0:T(8,128)S(1)}, bf16[1280,128]{1,0:T(8,128)(2,1)S(1)}) custom-call(bf16[64,256]{1,0:T(8,128)(2,1)S(1)} %get-tuple-element.28.refs_0_, bf16[200,256]{1,0:T(8,128)(2,1)S(1)} %collective-permute-done.1.second_ref.refs_1_.refs_0_, ...), custom_call_target="tpu_custom_call" | custom-call | flops 8000000000 | bytes 1310720 | tf_op jit(solution)/shard_map/early/pallas_call | solution.py:192
  23.1 1.0 %collective-permute-done.7.refs_5_ = bf16[264,256]{1,0:T(8,128)(2,1)S(1)} collective-permute-done((bf16[264,256]{1,0:T(8,128)(2,1)S(1)}, bf16[264,256]{1,0:T(8,128)(2,1)S(1)}, u32[]{:S(2)}, u32[]{:S(2)}) %collective-permute-start.7) | collective-permute-done | bytes 135200 | tf_op jit(solution)/shard_map/ppermute | solution.py:307
  24.1 1.4 %collective-permute-done.8.refs_6_ = bf16[264,256]{1,0:T(8,128)(2,1)S(1)} collective-permute-done((bf16[264,256]{1,0:T(8,128)(2,1)S(1)}, bf16[264,256]{1,0:T(8,128)(2,1)S(1)}, u32[]{:S(2)}, u32[]{:S(2)}) %collective-permute-start.8) | collective-permute-done | bytes 135200 | tf_op jit(solution)/shard_map/ppermute | solution.py:307
  25.5 0.0 collective-permute-done.9.refs_7_
  25.5 1.4 %late.4 = bf16[128,128]{1,0:T(8,128)(2,1)S(1)} custom-call(bf16[200,256]{1,0:T(8,128)(2,1)S(1)} %collective-permute-done.3.second_ref.refs_3_.refs_0_, bf16[264,256]{1,0:T(8,128)(2,1)S(1)} %pack.3.refs_5_.refs_1_, f32[1024,1280]{1,0:T(8,128)S(1)} %get-tuple-element.38.refs_2_, f32[1024,128]{1,0:T(8,128)S(1)} %get-tuple-element.43.refs_3_, ...), custom_call_target="tpu_custom_call" | custom-call | flops 3000000000 | bytes 393216 | tf_op jit(solution)/shard_map/late/pallas_call | solution.py:247
  26.9 1.4 %late.5 = bf16[128,128]{1,0:T(8,128)(2,1)S(1)} custom-call(bf16[200,256]{1,0:T(8,128)(2,1)S(1)} %collective-permute-done.2.first_ref.refs_2_.refs_0_, bf16[264,256]{1,0:T(8,128)(2,1)S(1)} %pack.3.refs_5_.refs_1_, f32[1024,1280]{1,0:T(8,128)S(1)} %get-tuple-element.38.refs_2_, f32[1024,128]{1,0:T(8,128)S(1)} %get-tuple-element.43.refs_3_, ...), custom_call_target="tpu_custom_call" | custom-call | flops 3000000000 | bytes 393216 | tf_op jit(solution)/shard_map/late/pallas_call | solution.py:247
  28.3 3.7 %collective-permute-start.13 = (bf16[128,128]{1,0:T(8,128)(2,1)S(1)}, bf16[128,128]{1,0:T(8,128)(2,1)S(1)}, u32[]{:S(2)}, u32[]{:S(2)}) collective-permute-start(bf16[128,128]{1,0:T(8,128)(2,1)S(1)} %late.5), channel_id=1, source_target_pairs={{0,16},{2,18},{4,20},{6,22},{8,24},{10,26},{12,28},{14,30},{16,0},... | collective-permute-start | bytes 98312 | tf_op jit(solution)/shard_map/ppermute | solution.py:307
  32.0 1.3 %collective-permute-start.15 = (bf16[128,128]{1,0:T(8,128)(2,1)S(1)}, bf16[128,128]{1,0:T(8,128)(2,1)S(1)}, u32[]{:S(2)}, u32[]{:S(2)}) collective-permute-start(bf16[128,128]{1,0:T(8,128)(2,1)S(1)} %late.4), channel_id=1, source_target_pairs={{0,24},{2,26},{4,28},{6,30},{8,16},{10,18},{12,20},{14,22},{16,8},... | collective-permute-start | bytes 98312 | tf_op jit(solution)/shard_map/ppermute | solution.py:307
  33.2 1.4 %late.6 = bf16[128,128]{1,0:T(8,128)(2,1)S(1)} custom-call(bf16[200,256]{1,0:T(8,128)(2,1)S(1)} %collective-permute-done.1.second_ref.refs_1_.refs_0_, bf16[264,256]{1,0:T(8,128)(2,1)S(1)} %pack.2.refs_4_.refs_1_, f32[1024,1280]{1,0:T(8,128)S(1)} %get-tuple-element.38.refs_2_, f32[1024,128]{1,0:T(8,128)S(1)} %get-tuple-element.43.refs_3_, ...), custom_call_target="tpu_custom_call" | custom-call | flops 3000000000 | bytes 393216 | tf_op jit(solution)/shard_map/late/pallas_call | solution.py:247
  34.6 0.0 copy-start
  34.6 0.1 collective-permute-start.11
  34.7 1.4 %late.7.refs_0_ = bf16[128,128]{1,0:T(8,128)(2,1)S(1)} custom-call(bf16[64,256]{1,0:T(8,128)(2,1)S(1)} %get-tuple-element.28.refs_0_, bf16[264,256]{1,0:T(8,128)(2,1)S(1)} %pack.2.refs_4_.refs_1_, f32[1024,1280]{1,0:T(8,128)S(1)} %get-tuple-element.38.refs_2_, f32[1024,128]{1,0:T(8,128)S(1)} %get-tuple-element.43.refs_3_, ...), custom_call_target="tpu_custom_call" | custom-call | flops 3000000000 | bytes 393216 | tf_op jit(solution)/shard_map/late/pallas_call | solution.py:247
  36.1 0.1 collective-permute-start.10
  36.2 0.0 collective-permute-done.13.refs_2_
  36.2 0.5 %collective-permute-start.14 = (bf16[128,128]{1,0:T(8,128)(2,1)S(1)}, bf16[128,128]{1,0:T(8,128)(2,1)S(1)}, u32[]{:S(2)}, u32[]{:S(2)}) collective-permute-start(bf16[128,128]{1,0:T(8,128)(2,1)S(1)} %collective-permute-done.13.refs_2_), channel_id=1, source_target_pairs={{0,1},{1,0},{2,3},{3,2},{4,5},{5,4},{6,7},{7,6},{8,9},{9,8},{10,11... | collective-permute-start | bytes 98312 | tf_op jit(solution)/shard_map/ppermute | solution.py:310
  36.7 1.2 %collective-permute-done.15.refs_3_ = bf16[128,128]{1,0:T(8,128)(2,1)S(1)} collective-permute-done((bf16[128,128]{1,0:T(8,128)(2,1)S(1)}, bf16[128,128]{1,0:T(8,128)(2,1)S(1)}, u32[]{:S(2)}, u32[]{:S(2)}) %collective-permute-start.15) | collective-permute-done | bytes 32800 | tf_op jit(solution)/shard_map/ppermute | solution.py:307
  37.9 0.0 collective-permute-start.16
  37.9 0.7 %collective-permute-done.11.refs_1_ = bf16[128,128]{1,0:T(8,128)(2,1)S(1)} collective-permute-done((bf16[128,128]{1,0:T(8,128)(2,1)S(1)}, bf16[128,128]{1,0:T(8,128)(2,1)S(1)}, u32[]{:S(2)}, u32[]{:S(2)}) %collective-permute-start.11) | collective-permute-done | bytes 32800 | tf_op jit(solution)/shard_map/ppermute | solution.py:307
  38.6 0.0 collective-permute-start.12
  38.6 0.0 copy-done
  38.6 0.3 mix.2.refs_5_
  38.9 0.0 collective-permute-done.10.refs_0_
  38.9 0.0 collective-permute-done.14.refs_2_
  38.9 0.2 collective-permute-done.16.refs_3_
  39.1 0.7 %collective-permute-done.12.refs_1_ = bf16[128,128]{1,0:T(8,128)(2,1)S(1)} collective-permute-done((bf16[128,128]{1,0:T(8,128)(2,1)S(1)}, bf16[128,128]{1,0:T(8,128)(2,1)S(1)}, u32[]{:S(2)}, u32[]{:S(2)}) %collective-permute-start.12) | collective-permute-done | bytes 32800 | tf_op jit(solution)/shard_map/ppermute | solution.py:310
  39.8 1.0 %mix.3 = bf16[64,1024]{1,0:T(8,128)(2,1)} custom-call(bf16[128,128]{1,0:T(8,128)(2,1)S(1)} %collective-permute-done.10.refs_0_, bf16[128,128]{1,0:T(8,128)(2,1)S(1)} %collective-permute-done.12.refs_1_, bf16[128,128]{1,0:T(8,128)(2,1)S(1)} %collective-permute-done.14.refs_2_, bf16[128,128]{1,0:T(8,128)(2,1)S(1)} %collective-permute-done.16.refs_3_, ...), custom_call_target="tpu_custom_call" | custom-call | flops 67108864 | bytes 1048576 | tf_op jit(solution)/shard_map/mix/pallas_call | solution.py:288
  (2 shorter events, 0.0 us)
Async XLA Ops:
  3.1 5.8 %collective-permute-start = (bf16[512,1024]{1,0:T(8,128)(2,1)}, bf16[512,1024]{1,0:T(8,128)(2,1)S(1)}, u32[]{:S(2)}, u32[]{:S(2)}) collective-permute-start(bf16[512,1024]{1,0:T(8,128)(2,1)} %refs_4_.1), channel_id=1, source_target_pairs={{0,1},{1,0},{2,3},{3,2},{4,5},{5,4},{6,7},{7,6},{8,9},{9,8},{10,11... | collective-permute-start | bytes 3145736 | tf_op jit(solution)/shard_map/ppermute | solution.py:310
  3.6 6.1 %collective-permute-start.1 = (bf16[200,256]{1,0:T(8,128)(2,1)S(1)}, bf16[200,256]{1,0:T(8,128)(2,1)S(1)}, u32[]{:S(2)}, u32[]{:S(2)}) collective-permute-start(bf16[200,256]{1,0:T(8,128)(2,1)S(1)} %get-tuple-element.33), channel_id=1, source_target_pairs={{0,8},{2,10},{4,12},{6,14},{8,0},{10,2},{12,4},{14,6},{16,24},{18,... | collective-permute-start | bytes 307208 | tf_op jit(solution)/shard_map/ppermute | solution.py:307
  6.3 11.0 %collective-permute-start.2 = (bf16[200,256]{1,0:T(8,128)(2,1)S(1)}, bf16[200,256]{1,0:T(8,128)(2,1)S(1)}, u32[]{:S(2)}, u32[]{:S(2)}) collective-permute-start(bf16[200,256]{1,0:T(8,128)(2,1)S(1)} %get-tuple-element.34), channel_id=1, source_target_pairs={{0,16},{2,18},{4,20},{6,22},{8,24},{10,26},{12,28},{14,30},{16,0},... | collective-permute-start | bytes 307208 | tf_op jit(solution)/shard_map/ppermute | solution.py:307
  8.9 8.4 %collective-permute-start.3 = (bf16[200,256]{1,0:T(8,128)(2,1)S(1)}, bf16[200,256]{1,0:T(8,128)(2,1)S(1)}, u32[]{:S(2)}, u32[]{:S(2)}) collective-permute-start(bf16[200,256]{1,0:T(8,128)(2,1)S(1)} %get-tuple-element.35), channel_id=1, source_target_pairs={{0,24},{2,26},{4,28},{6,30},{8,16},{10,18},{12,20},{14,22},{16,8},... | collective-permute-start | bytes 307208 | tf_op jit(solution)/shard_map/ppermute | solution.py:307
  9.8 7.5 %collective-permute-start.4 = (bf16[264,256]{1,0:T(8,128)(2,1)S(1)}, bf16[264,256]{1,0:T(8,128)(2,1)S(1)}, u32[]{:S(2)}, u32[]{:S(2)}) collective-permute-start(bf16[264,256]{1,0:T(8,128)(2,1)S(1)} %pack.2.refs_4_.refs_1_), channel_id=1, source_target_pairs={{0,4},{2,6},{4,0},{6,2},{8,12},{10,14},{12,8},{14,10},{16,20},{18,... | collective-permute-start | bytes 405512 | tf_op jit(solution)/shard_map/ppermute | solution.py:307
  11.5 9.3 %collective-permute-start.5 = (bf16[264,256]{1,0:T(8,128)(2,1)S(1)}, bf16[264,256]{1,0:T(8,128)(2,1)S(1)}, u32[]{:S(2)}, u32[]{:S(2)}) collective-permute-start(bf16[264,256]{1,0:T(8,128)(2,1)S(1)} %pack.2.refs_4_.refs_1_), channel_id=1, source_target_pairs={{0,2},{2,0},{4,6},{6,4},{8,10},{10,8},{12,14},{14,12},{16,18},{18,... | collective-permute-start | bytes 405512 | tf_op jit(solution)/shard_map/ppermute | solution.py:307
  13.0 7.9 %collective-permute-start.6 = (bf16[264,256]{1,0:T(8,128)(2,1)S(1)}, bf16[264,256]{1,0:T(8,128)(2,1)S(1)}, u32[]{:S(2)}, u32[]{:S(2)}) collective-permute-start(bf16[264,256]{1,0:T(8,128)(2,1)S(1)} %pack.2.refs_4_.refs_1_), channel_id=1, source_target_pairs={{0,6},{2,4},{4,2},{6,0},{8,14},{10,12},{12,10},{14,8},{16,22},{18,... | collective-permute-start | bytes 405512 | tf_op jit(solution)/shard_map/ppermute | solution.py:307
  17.3 6.8 %collective-permute-start.7 = (bf16[264,256]{1,0:T(8,128)(2,1)S(1)}, bf16[264,256]{1,0:T(8,128)(2,1)S(1)}, u32[]{:S(2)}, u32[]{:S(2)}) collective-permute-start(bf16[264,256]{1,0:T(8,128)(2,1)S(1)} %pack.3.refs_5_.refs_1_), channel_id=1, source_target_pairs={{0,6},{2,4},{4,2},{6,0},{8,14},{10,12},{12,10},{14,8},{16,22},{18,... | collective-permute-start | bytes 405512 | tf_op jit(solution)/shard_map/ppermute | solution.py:307
  19.8 5.7 %collective-permute-start.8 = (bf16[264,256]{1,0:T(8,128)(2,1)S(1)}, bf16[264,256]{1,0:T(8,128)(2,1)S(1)}, u32[]{:S(2)}, u32[]{:S(2)}) collective-permute-start(bf16[264,256]{1,0:T(8,128)(2,1)S(1)} %pack.3.refs_5_.refs_1_), channel_id=1, source_target_pairs={{0,2},{2,0},{4,6},{6,4},{8,10},{10,8},{12,14},{14,12},{16,18},{18,... | collective-permute-start | bytes 405512 | tf_op jit(solution)/shard_map/ppermute | solution.py:307
  20.4 5.1 %collective-permute-start.9 = (bf16[264,256]{1,0:T(8,128)(2,1)S(1)}, bf16[264,256]{1,0:T(8,128)(2,1)S(1)}, u32[]{:S(2)}, u32[]{:S(2)}) collective-permute-start(bf16[264,256]{1,0:T(8,128)(2,1)S(1)} %pack.3.refs_5_.refs_1_), channel_id=1, source_target_pairs={{0,4},{2,6},{4,0},{6,2},{8,12},{10,14},{12,8},{14,10},{16,20},{18,... | collective-permute-start | bytes 405512 | tf_op jit(solution)/shard_map/ppermute | solution.py:307
  28.3 7.9 %collective-permute-start.13 = (bf16[128,128]{1,0:T(8,128)(2,1)S(1)}, bf16[128,128]{1,0:T(8,128)(2,1)S(1)}, u32[]{:S(2)}, u32[]{:S(2)}) collective-permute-start(bf16[128,128]{1,0:T(8,128)(2,1)S(1)} %late.5), channel_id=1, source_target_pairs={{0,16},{2,18},{4,20},{6,22},{8,24},{10,26},{12,28},{14,30},{16,0},... | collective-permute-start | bytes 98312 | tf_op jit(solution)/shard_map/ppermute | solution.py:307
  32.0 5.9 %collective-permute-start.15 = (bf16[128,128]{1,0:T(8,128)(2,1)S(1)}, bf16[128,128]{1,0:T(8,128)(2,1)S(1)}, u32[]{:S(2)}, u32[]{:S(2)}) collective-permute-start(bf16[128,128]{1,0:T(8,128)(2,1)S(1)} %late.4), channel_id=1, source_target_pairs={{0,24},{2,26},{4,28},{6,30},{8,16},{10,18},{12,20},{14,22},{16,8},... | collective-permute-start | bytes 98312 | tf_op jit(solution)/shard_map/ppermute | solution.py:307
  34.6 4.0 %copy-start = (bf16[512,1024]{1,0:T(8,128)(2,1)S(1)}, bf16[512,1024]{1,0:T(8,128)(2,1)}, u32[]{:S(2)}) copy-start(bf16[512,1024]{1,0:T(8,128)(2,1)} %refs_4_.1) | copy-start | bytes 3145732
  34.6 4.0 %collective-permute-start.11 = (bf16[128,128]{1,0:T(8,128)(2,1)S(1)}, bf16[128,128]{1,0:T(8,128)(2,1)S(1)}, u32[]{:S(2)}, u32[]{:S(2)}) collective-permute-start(bf16[128,128]{1,0:T(8,128)(2,1)S(1)} %late.6), channel_id=1, source_target_pairs={{0,8},{2,10},{4,12},{6,14},{8,0},{10,2},{12,4},{14,6},{16,24},{18,... | collective-permute-start | bytes 98312 | tf_op jit(solution)/shard_map/ppermute | solution.py:307
  36.1 2.8 %collective-permute-start.10 = (bf16[128,128]{1,0:T(8,128)(2,1)S(1)}, bf16[128,128]{1,0:T(8,128)(2,1)S(1)}, u32[]{:S(2)}, u32[]{:S(2)}) collective-permute-start(bf16[128,128]{1,0:T(8,128)(2,1)S(1)} %late.7.refs_0_), channel_id=1, source_target_pairs={{0,1},{1,0},{2,3},{3,2},{4,5},{5,4},{6,7},{7,6},{8,9},{9,8},{10,11... | collective-permute-start | bytes 98312 | tf_op jit(solution)/shard_map/ppermute | solution.py:310
  36.2 2.7 %collective-permute-start.14 = (bf16[128,128]{1,0:T(8,128)(2,1)S(1)}, bf16[128,128]{1,0:T(8,128)(2,1)S(1)}, u32[]{:S(2)}, u32[]{:S(2)}) collective-permute-start(bf16[128,128]{1,0:T(8,128)(2,1)S(1)} %collective-permute-done.13.refs_2_), channel_id=1, source_target_pairs={{0,1},{1,0},{2,3},{3,2},{4,5},{5,4},{6,7},{7,6},{8,9},{9,8},{10,11... | collective-permute-start | bytes 98312 | tf_op jit(solution)/shard_map/ppermute | solution.py:310
  37.9 1.2 %collective-permute-start.16 = (bf16[128,128]{1,0:T(8,128)(2,1)S(1)}, bf16[128,128]{1,0:T(8,128)(2,1)S(1)}, u32[]{:S(2)}, u32[]{:S(2)}) collective-permute-start(bf16[128,128]{1,0:T(8,128)(2,1)S(1)} %collective-permute-done.15.refs_3_), channel_id=1, source_target_pairs={{0,1},{1,0},{2,3},{3,2},{4,5},{5,4},{6,7},{7,6},{8,9},{9,8},{10,11... | collective-permute-start | bytes 98312 | tf_op jit(solution)/shard_map/ppermute | solution.py:310
  38.6 1.2 %collective-permute-start.12 = (bf16[128,128]{1,0:T(8,128)(2,1)S(1)}, bf16[128,128]{1,0:T(8,128)(2,1)S(1)}, u32[]{:S(2)}, u32[]{:S(2)}) collective-permute-start(bf16[128,128]{1,0:T(8,128)(2,1)S(1)} %collective-permute-done.11.refs_1_), channel_id=1, source_target_pairs={{0,1},{1,0},{2,3},{3,2},{4,5},{5,4},{6,7},{7,6},{8,9},{9,8},{10,11... | collective-permute-start | bytes 98312 | tf_op jit(solution)/shard_map/ppermute | solution.py:310
